TPU v7x, 256 devices: a whole 4x4x8 slice. The times are simulated.
256 devices in a mesh: stream: 8 (over z), mod: 32 (over y, x, core).
Axes of the slice: x: 4, y: 4, z: 8, core: 2. Of those that a mesh axis runs over, the one named last changes fastest.
Arguments:
- pixels: bfloat16 [8, 768, 512, 384], P('stream', None, 'mod'), may hold values from -6 to 6
- stem_weight: bfloat16 [256, 128], replicated, may hold values from -0.375 to 0.375
- veto_weight: float32 [32, 128], replicated, may hold values from -0.25 to 0.25
- hit_frames: int32 [8, 192], P('stream'), may hold values from 0 to 767, as said below
- assign: int32 [8, 192, 1], P('stream'), may hold values from 0 to 7; in each aligned block of 6 rows (0 to 5, 6 to 11, ..., all dimensions but the last counted through in order) at most 2 rows name the same one
- token_in: bfloat16 [8, 384, 24], P('stream'), may hold values from -1.25 to 1.25
- token_out: bfloat16 [8, 24, 384], P('stream'), may hold values from -0.3125 to 0.3125
- chan_in: bfloat16 [8, 128, 512], P('stream'), may hold values from -0.5 to 0.5
- chan_out: bfloat16 [8, 512, 128], P('stream'), may hold values from -0.25 to 0.25
- readout: bfloat16 [4096, 128], replicated, may hold values from -0.09375 to 0.09375
- latent_gain: float32 [128], replicated, may hold values from 0.1 to 1.9
- class_weight: float32 [128, 8], replicated, may hold values from -0.5 to 0.5
Outputs:
- veto: float32 [8, 768], P('stream', 'mod')
- latents: float32 [8, 192, 128], P('stream', 'mod')
- scores: float32 [8, 192, 8], P('stream', 'mod')
Inputs may be any that keep to these rules, and one draw needn't show every extreme that they name: `hit_frames`: each row lists, rising and distinct, exactly 6 frames from every aligned block of 24 frames. `assign`: within the 6 hits of one aligned block (one owner's hits) no stream is named more than 2 times.
All inputs are finite; a program needn't handle non-finite values.
Results may differ from a plain program's by a relative error of at most 0.0095.
Values may be sent and summed in bfloat16 or wider, within the bound.
A program may use at most 128 MiB of HBM per device.

v0:
```python
import jax
import jax.numpy as jnp
from jax import lax
from jax.sharding import PartitionSpec as P

PATCH = 16
CAP = 2


def rms_norm(values):
    return values * lax.rsqrt(jnp.mean(values * values, axis=-1, keepdims=True) + 1e-06)


def stem_layer(frame_pixels, stem_weight):
    count, height, width = frame_pixels.shape
    pixel_tiles = frame_pixels.reshape(count, height // PATCH, PATCH, width // PATCH, PATCH)
    kernel = stem_weight.reshape(PATCH, PATCH, -1)
    response = jnp.einsum(
        "fapbq,pqc->fabc", pixel_tiles, kernel, preferred_element_type=jnp.float32
    )
    return jax.nn.gelu(response).astype(jnp.bfloat16).reshape(count, -1, kernel.shape[-1])


def encode(
    tokens, mix_in, mix_out, chan_in, chan_out, readout, latent_gain, class_weight, module_count
):
    batch = tokens.shape[0]
    channels = tokens.shape[-1]
    row_len = mix_in.shape[1]
    grid_tokens = tokens.reshape(batch, -1, row_len, channels)
    normed = rms_norm(grid_tokens.astype(jnp.float32)).astype(jnp.bfloat16)
    mixed_tok = jax.nn.gelu(
        jnp.einsum("mw,brwc->brmc", mix_in, normed, preferred_element_type=jnp.float32)
    ).astype(jnp.bfloat16)
    after_mix = (
        grid_tokens.astype(jnp.float32)
        + jnp.einsum("wm,brmc->brwc", mix_out, mixed_tok, preferred_element_type=jnp.float32)
    ).astype(jnp.bfloat16)
    after_mix = after_mix.reshape(batch, -1, channels)
    normed_two = rms_norm(after_mix.astype(jnp.float32)).astype(jnp.bfloat16)
    hidden = jax.nn.gelu(
        jnp.einsum("btc,ch->bth", normed_two, chan_in, preferred_element_type=jnp.float32)
    ).astype(jnp.bfloat16)
    after_mlp = after_mix.astype(jnp.float32) + jnp.einsum(
        "bth,hc->btc", hidden, chan_out, preferred_element_type=jnp.float32
    )
    pooled = (
        jnp.mean(after_mlp.reshape(batch, module_count, -1, channels), axis=2)
        .reshape(batch, -1)
        .astype(jnp.bfloat16)
    )
    projected = jnp.dot(pooled, readout, preferred_element_type=jnp.float32)
    latent = rms_norm(projected) * latent_gain
    class_scores = jnp.dot(latent, class_weight, precision=lax.Precision.HIGHEST)
    return (latent, class_scores)


def local(
    pixels,
    stem_weight,
    veto_weight,
    hit_frames,
    assign,
    token_in,
    token_out,
    chan_in,
    chan_out,
    readout,
    latent_gain,
    class_weight,
):
    module_count = lax.axis_size("mod")
    stream_count = lax.axis_size("stream")
    mod_index = lax.axis_index("mod")
    frames_total = pixels.shape[1]
    frames_owned = frames_total // module_count
    hits_owned = hit_frames.shape[1] // module_count
    features = stem_layer(pixels[0], stem_weight)
    channels = features.shape[2]
    own_hits = lax.dynamic_slice_in_dim(hit_frames[0], mod_index * hits_owned, hits_owned)
    targets = lax.dynamic_slice_in_dim(assign[0, :, 0], mod_index * hits_owned, hits_owned)
    owned_frames = lax.all_to_all(features, "mod", split_axis=0, concat_axis=1, tiled=True)
    module_means = jnp.mean(
        owned_frames.reshape(frames_owned, module_count, -1, channels), axis=2, dtype=jnp.float32
    )
    veto_score = jnp.sum(module_means * veto_weight, axis=(1, 2))
    chosen = jnp.take(owned_frames, own_hits - mod_index * frames_owned, axis=0)
    position = jnp.arange(hits_owned, dtype=jnp.int32)
    earlier = (targets[:, None] == targets[None, :]) & (position[None, :] < position[:, None])
    slot_rank = jnp.sum(earlier.astype(jnp.int32), axis=1)
    stream_ids = jnp.arange(stream_count, dtype=jnp.int32)
    slot_ids = jnp.arange(CAP, dtype=jnp.int32)
    placing = (targets[None, None, :] == stream_ids[:, None, None]) & (
        slot_rank[None, None, :] == slot_ids[None, :, None]
    )
    outgoing = jnp.einsum(
        "tkh,hxc->tkxc", placing.astype(jnp.bfloat16), chosen, preferred_element_type=jnp.float32
    ).astype(jnp.bfloat16)
    received = lax.all_to_all(outgoing, "stream", split_axis=0, concat_axis=0, tiled=True)
    slot_count = received.shape[1]
    flat = received.reshape(stream_count * slot_count, received.shape[2], received.shape[3])
    latent, class_scores = encode(
        flat,
        token_in[0],
        token_out[0],
        chan_in[0],
        chan_out[0],
        readout,
        latent_gain,
        class_weight,
        module_count,
    )
    slot_latents = latent.reshape(stream_count, slot_count, -1)
    slot_scores = class_scores.reshape(stream_count, slot_count, -1)
    back_latents, back_scores = (
        lax.all_to_all(slot_latents, "stream", split_axis=0, concat_axis=0, tiled=True),
        lax.all_to_all(slot_scores, "stream", split_axis=0, concat_axis=0, tiled=True),
    )
    placing_float = placing.astype(jnp.float32)
    hit_latents = jnp.einsum(
        "tkh,tkc->hc", placing_float, back_latents, precision=lax.Precision.HIGHEST
    )
    hit_scores = jnp.einsum(
        "tkh,tkc->hc", placing_float, back_scores, precision=lax.Precision.HIGHEST
    )
    return (veto_score[None], hit_latents[None], hit_scores[None])


def solution(mesh):
    in_specs = (
        P("stream", None, "mod", None),
        P(),
        P(),
        P("stream", None),
        P("stream", None, None),
        P("stream", None, None),
        P("stream", None, None),
        P("stream", None, None),
        P("stream", None, None),
        P(),
        P(),
        P(),
    )
    out_specs = (P("stream", "mod"), P("stream", "mod", None), P("stream", "mod", None))
    return jax.shard_map(local, mesh=mesh, in_specs=in_specs, out_specs=out_specs, check_vma=False)
```

profile of v0, /device:TPU:10, one launch (start us, length us, event | category | flops | bytes accessed | tf_op | source)
XLA Modules:
  0.0 287.8 jit_solution(17420514059617366917)
XLA Ops:
  0.6 0.0 copy-start
  0.6 0.0 copy-start.7
  0.7 13.5 %copy.71 = bf16[1,768,16,384]{1,3,2,0:T(8,128)(2,1)} copy(bf16[1,768,16,384]{3,2,1,0:T(8,128)(2,1)} %param.12) | data formatting | bytes 18874368 | tf_op args[0]
  14.2 0.0 copy-done.7
  14.2 7.4 %fusion.29 = bf16[768,24,128]{2,0,1:T(8,128)(2,1)S(1)} fusion(bf16[768,16,24,16]{0,3,2,1:T(8,128)(2,1)} %bitcast.105, bf16[16,16,128,1]{2,1,3,0:T(8,128)(2,1)S(1)} %bitcast.112), kind=kOutput, calls=%fused_computation.30 | convolution fusion | flops 1229193216 | bytes 14221312 | tf_op jit(solution)/shard_map/fapbq,pqc->fabc/dot_general | solution.py:18
  21.6 5.2 %copy.72 = bf16[768,24,128]{2,1,0:T(8,128)(2,1)} copy(bf16[768,24,128]{2,0,1:T(8,128)(2,1)S(1)} %fusion.29) | data formatting | bytes 9437184 | tf_op jit(solution)/shard_map/convert_element_type | solution.py:21
  26.8 7.7 %all-to-all-start = ((bf16[768,24,128]{2,1,0:T(8,128)(2,1)}), bf16[768,24,128]{2,1,0:T(8,128)(2,1)}, u32[]{:S(2)}, u32[]{:S(2)}) async-start(bf16[768,24,128]{2,1,0:T(8,128)(2,1)} %copy.72), calls=%async_computation | async-start | bytes 9437184 | tf_op jit(solution)/shard_map/all_to_all | solution.py:82
  34.5 0.0 copy-done.3
  34.5 0.1 fusion.60
  34.6 0.1 compare_and_fusion
  34.6 0.0 copy-done.10
  34.6 0.1 dynamic-slice_bitcast_fusion
  34.7 0.2 convert_reduce_fusion.1
  34.9 0.1 iota_compare_fusion.1
  35.0 55.3 %all-to-all-done = bf16[768,24,128]{2,1,0:T(8,128)(2,1)} async-done(((bf16[768,24,128]{2,1,0:T(8,128)(2,1)}), bf16[768,24,128]{2,1,0:T(8,128)(2,1)}, u32[]{:S(2)}, u32[]{:S(2)}) %all-to-all-start) | async-done | bytes 4718624 | tf_op jit(solution)/shard_map/all_to_all | solution.py:82
  90.3 5.8 %copy.73 = bf16[24,32,24,128]{3,2,1,0:T(8,128)(2,1)} copy(bf16[24,32,24,128]{3,2,0,1:T(8,128)(2,1)} %bitcast.6) | data formatting | bytes 9437184 | tf_op jit(solution)/shard_map/all_to_all | solution.py:82
  96.1 3.1 %gather_fusion = bf16[6,768,128]{2,1,0:T(8,128)(2,1)S(1)} fusion(bf16[24,768,128]{2,1,0:T(8,128)(2,1)} %bitcast.106, s32[1024]{0:T(1024)S(1)} %pad_clamp_fusion), kind=kCustom, calls=%fused_computation | custom fusion | bytes 2359320 | tf_op jit(solution)/shard_map/jit(_take)/gather | solution.py:87
  99.2 0.2 broadcast_select_fusion
  99.4 4.8 %convolution_convert_fusion = bf16[8,2,768,128]{3,0,2,1:T(8,128)(2,1)S(1)} fusion(bf16[6,768,128]{2,1,0:T(8,128)(2,1)S(1)} %broadcast_select_fusion, pred[2,6]{1,0:T(4,128)(4,1)S(1)} %iota_compare_fusion.2, pred[8,6]{0,1:T(8,128)(4,1)S(1)} %iota_compare_fusion.1), kind=kOutput, calls=%fused_computation.41 | convolution fusion | flops 20447328 | bytes 4325436 | tf_op jit(solution)/shard_map/tkh,hxc->tkxc/dot_general | solution.py:96
  104.3 0.0 copy-start.1
  104.3 2.3 copy.76
  106.6 8.5 %all-to-all-start.1 = ((bf16[8,2,768,128]{3,2,1,0:T(8,128)(2,1)}), bf16[8,2,768,128]{3,2,1,0:T(8,128)(2,1)}, u32[]{:S(2)}, u32[]{:S(2)}) async-start(bf16[8,2,768,128]{3,2,1,0:T(8,128)(2,1)} %copy.76), calls=%async_computation.1 | async-start | bytes 6291456 | tf_op jit(solution)/shard_map/all_to_all | solution.py:99
  115.0 0.0 copy-done.1
  115.1 0.0 copy-start.8
  115.1 0.0 copy-start.9
  115.1 4.1 %convert_reduce_fusion = f32[24,32,128]{2,0,1:T(8,128)S(1)} fusion(bf16[24,32,24,128]{3,2,0,1:T(8,128)(2,1)} %bitcast.6), kind=kLoop, calls=%fused_computation.31 | loop fusion | flops 4620288 | bytes 5111808 | tf_op jit(solution)/shard_map/reduce_sum | solution.py:83
  119.2 71.4 %all-to-all-done.1 = bf16[8,2,768,128]{3,2,1,0:T(8,128)(2,1)} async-done(((bf16[8,2,768,128]{3,2,1,0:T(8,128)(2,1)}), bf16[8,2,768,128]{3,2,1,0:T(8,128)(2,1)}, u32[]{:S(2)}, u32[]{:S(2)}) %all-to-all-start.1) | async-done | bytes 3145760 | tf_op jit(solution)/shard_map/all_to_all | solution.py:99
  190.6 3.6 %multiply_reduce_fusion.1 = f32[8,2,768]{2,1,0:T(2,128)S(1)} fusion(bf16[8,2,768,128]{3,2,1,0:T(8,128)(2,1)} %all-to-all-done.1), kind=kLoop, calls=%fused_computation.39 | loop fusion | flops 4706304 | bytes 3194880 | tf_op jit(solution)/shard_map/reduce_sum | solution.py:11
  194.3 5.2 %multiply_convert_fusion.1 = bf16[8,2,768,128]{3,2,1,0:T(8,128)(2,1)} fusion(bf16[8,2,768,128]{3,2,1,0:T(8,128)(2,1)} %all-to-all-done.1, f32[8,2,768]{2,1,0:T(2,128)S(1)} %add_rsqrt_fusion.1), kind=kLoop, calls=%fused_computation.38 | loop fusion | flops 4718592 | bytes 6340608 | tf_op jit(solution)/shard_map/convert_element_type | solution.py:31
  199.5 0.0 copy-done.8
  199.5 39.8 %multiply_reduce_fusion = (f32[16,32,24]{2,1,0:T(8,128)S(1)}, f32[16,32,24,128]{3,2,1,0:T(8,128)}) fusion(bf16[1,24,384]{2,1,0:T(8,128)(2,1)S(1)} %copy-done.8, bf16[16,32,24,128]{3,2,1,0:T(8,128)(2,1)} %bitcast.108, bf16[1,384,24]{1,2,0:T(8,128)(2,1)S(1)} %copy-done.9, bf16[16,32,24,128]{3,2,1,0:T(8,128)(2,1)} %bitcast.82), kind=kOutput, calls=%fused_computation.37 | convolution fusion | flops 2651836416 | bytes 12668928 | tf_op jit(solution)/shard_map/wm,brmc->brwc/dot_general | solution.py:37
  239.4 6.3 %multiply_convert_fusion = bf16[16,32,24,128]{3,2,1,0:T(8,128)(2,1)} fusion(f32[16,32,24,128]{3,2,1,0:T(8,128)} %get-tuple-element.22, f32[16,32,24]{2,1,0:T(8,128)S(1)} %add_rsqrt_fusion), kind=kLoop, calls=%fused_computation.36 | loop fusion | flops 3145728 | bytes 9486336 | tf_op jit(solution)/shard_map/convert_element_type | solution.py:40
  245.6 0.0 copy-done.5
  245.6 13.0 %bitcast_add_fusion = f32[16,768,128]{2,1,0:T(8,128)} fusion(f32[16,32,24,128]{3,2,1,0:T(8,128)} %get-tuple-element.22, bf16[16,768,128]{2,1,0:T(8,128)(2,1)} %bitcast.109, bf16[1,512,128]{2,1,0:T(8,128)(2,1)S(1)} %copy-done.5, bf16[1,128,512]{2,1,0:T(8,128)(2,1)S(1)} %copy-done.6), kind=kOutput, calls=%fused_computation.33 | convolution fusion | flops 3279421440 | bytes 15990784 | tf_op jit(solution)/shard_map/bth,hc->btc/dot_general | solution.py:44
  258.7 3.7 %reduce_sum.68 = f32[16,32,128]{2,1,0:T(8,128)S(1)} reduce(f32[16,32,24,128]{3,2,1,0:T(8,128)} %bitcast.107, f32[]{:T(128)} %constant.19.clone.1), dimensions={2}, to_apply=%region_5.6 | reduce | flops 1507328 | bytes 6553604 | tf_op jit(solution)/shard_map/reduce_sum | solution.py:48
  262.5 0.4 multiply_reduce_fusion.3
  262.9 0.7 multiply_multiply_fusion.3
  263.6 0.0 copy-done.2
  263.6 1.4 fusion.71
  265.0 3.3 %all-to-all-start.3 = ((f32[8,2,8]{2,1,0:T(2,128)}), f32[8,2,8]{2,1,0:T(2,128)S(1)}, u32[]{:S(2)}, u32[]{:S(2)}) async-start(f32[8,2,8]{2,1,0:T(2,128)} %bitcast.36), calls=%async_computation.3 | async-start | bytes 16384 | tf_op jit(solution)/shard_map/all_to_all | solution.py:117
  268.3 0.7 multiply_reduce_fusion.2
  269.0 7.0 %all-to-all-done.3 = f32[8,2,8]{2,1,0:T(2,128)S(1)} async-done(((f32[8,2,8]{2,1,0:T(2,128)}), f32[8,2,8]{2,1,0:T(2,128)S(1)}, u32[]{:S(2)}, u32[]{:S(2)}) %all-to-all-start.3) | async-done | bytes 544 | tf_op jit(solution)/shard_map/all_to_all | solution.py:117
  276.0 3.3 %all-to-all-start.2 = ((f32[8,2,128]{2,1,0:T(2,128)}), f32[8,2,128]{2,1,0:T(2,128)S(1)}, u32[]{:S(2)}, u32[]{:S(2)}) async-start(f32[8,2,128]{2,1,0:T(2,128)} %bitcast.33), calls=%async_computation.2 | async-start | bytes 16384 | tf_op jit(solution)/shard_map/all_to_all | solution.py:116
  279.3 0.3 convolution_bitcast_fusion
  279.5 0.6 copy.82
  280.1 6.8 %all-to-all-done.2 = f32[8,2,128]{2,1,0:T(2,128)S(1)} async-done(((f32[8,2,128]{2,1,0:T(2,128)}), f32[8,2,128]{2,1,0:T(2,128)S(1)}, u32[]{:S(2)}, u32[]{:S(2)}) %all-to-all-start.2) | async-done | bytes 8224 | tf_op jit(solution)/shard_map/all_to_all | solution.py:116
  286.9 0.3 convolution_bitcast_fusion.1
  287.2 0.6 copy.81
  (17 shorter events, 0.2 us)
Async XLA Ops:
  0.6 261.8 %copy-start = (bf16[4096,128]{1,0:T(8,128)(2,1)S(1)}, bf16[4096,128]{1,0:T(8,128)(2,1)}, u32[]{:S(2)}) copy-start(bf16[4096,128]{1,0:T(8,128)(2,1)} %param.21) | copy-start | bytes 3145732
  0.6 13.5 %copy-start.7 = (bf16[256,128]{1,0:T(8,128)(2,1)S(1)}, bf16[256,128]{1,0:T(8,128)(2,1)}, u32[]{:S(2)}) copy-start(bf16[256,128]{1,0:T(8,128)(2,1)} %param.13) | copy-start | bytes 196612
  26.8 7.7 %copy-start.3 = (s32[1,192]{1,0:T(1,128)S(1)}, s32[1,192]{1,0:T(1,128)}, u32[]{:S(2)}) copy-start(s32[1,192]{1,0:T(1,128)} %param.15) | copy-start | bytes 2308
  26.8 7.9 %copy-start.10 = (s32[1,192,1]{1,2,0:T(1,128)S(1)}, s32[1,192,1]{1,2,0:T(1,128)}, u32[]{:S(2)}) copy-start(s32[1,192,1]{1,2,0:T(1,128)} %param.16) | copy-start | bytes 2308
  26.8 63.5 %all-to-all-start = ((bf16[768,24,128]{2,1,0:T(8,128)(2,1)}), bf16[768,24,128]{2,1,0:T(8,128)(2,1)}, u32[]{:S(2)}, u32[]{:S(2)}) async-start(bf16[768,24,128]{2,1,0:T(8,128)(2,1)} %copy.72), calls=%async_computation | async-start | bytes 9437184 | tf_op jit(solution)/shard_map/all_to_all | solution.py:82
  104.3 10.8 %copy-start.1 = (f32[32,128]{1,0:T(8,128)S(1)}, f32[32,128]{1,0:T(8,128)}, u32[]{:S(2)}) copy-start(f32[32,128]{1,0:T(8,128)} %param.14) | copy-start | bytes 49156
  106.6 84.0 %all-to-all-start.1 = ((bf16[8,2,768,128]{3,2,1,0:T(8,128)(2,1)}), bf16[8,2,768,128]{3,2,1,0:T(8,128)(2,1)}, u32[]{:S(2)}, u32[]{:S(2)}) async-start(bf16[8,2,768,128]{3,2,1,0:T(8,128)(2,1)} %copy.76), calls=%async_computation.1 | async-start | bytes 6291456 | tf_op jit(solution)/shard_map/all_to_all | solution.py:99
  115.1 84.4 %copy-start.8 = (bf16[1,24,384]{2,1,0:T(8,128)(2,1)S(1)}, bf16[1,24,384]{2,1,0:T(8,128)(2,1)}, u32[]{:S(2)}) copy-start(bf16[1,24,384]{2,1,0:T(8,128)(2,1)} %param.18) | copy-start | bytes 55300
  115.1 84.4 %copy-start.9 = (bf16[1,384,24]{1,2,0:T(8,128)(2,1)S(1)}, bf16[1,384,24]{1,2,0:T(8,128)(2,1)}, u32[]{:S(2)}) copy-start(bf16[1,384,24]{1,2,0:T(8,128)(2,1)} %param.17) | copy-start | bytes 55300
  239.3 6.3 %copy-start.5 = (bf16[1,512,128]{2,1,0:T(8,128)(2,1)S(1)}, bf16[1,512,128]{2,1,0:T(8,128)(2,1)}, u32[]{:S(2)}) copy-start(bf16[1,512,128]{2,1,0:T(8,128)(2,1)} %param.20) | copy-start | bytes 393220
  239.3 6.3 %copy-start.6 = (bf16[1,128,512]{2,1,0:T(8,128)(2,1)S(1)}, bf16[1,128,512]{2,1,0:T(8,128)(2,1)}, u32[]{:S(2)}) copy-start(bf16[1,128,512]{2,1,0:T(8,128)(2,1)} %param.19) | copy-start | bytes 393220
  258.7 4.2 %copy-start.4 = (f32[128]{0:T(128)S(1)}, f32[128]{0:T(128)}, u32[]{:S(2)}) copy-start(f32[128]{0:T(128)} %param.22) | copy-start | bytes 1540
  258.7 4.9 %copy-start.2 = (f32[128,8]{0,1:T(8,128)S(1)}, f32[128,8]{0,1:T(8,128)}, u32[]{:S(2)}) copy-start(f32[128,8]{0,1:T(8,128)} %param.23) | copy-start | bytes 12292
  265.0 11.0 %all-to-all-start.3 = ((f32[8,2,8]{2,1,0:T(2,128)}), f32[8,2,8]{2,1,0:T(2,128)S(1)}, u32[]{:S(2)}, u32[]{:S(2)}) async-start(f32[8,2,8]{2,1,0:T(2,128)} %bitcast.36), calls=%async_computation.3 | async-start | bytes 16384 | tf_op jit(solution)/shard_map/all_to_all | solution.py:117
  276.0 11.0 %all-to-all-start.2 = ((f32[8,2,128]{2,1,0:T(2,128)}), f32[8,2,128]{2,1,0:T(2,128)S(1)}, u32[]{:S(2)}, u32[]{:S(2)}) async-start(f32[8,2,128]{2,1,0:T(2,128)} %bitcast.33), calls=%async_computation.2 | async-start | bytes 16384 | tf_op jit(solution)/shard_map/all_to_all | solution.py:116
where the time goes:
time: 289 us; the launch traced here: 288 us
  waiting for transfers between devices  141 us (49%)
  matrix products  67.4 us (23%)
  local copies, waits for them, and re-layouts  31.2 us (11%)
  other arithmetic  25 us (9%)
  starting transfers between devices  22.8 us (8%)
    all_to_all x1, waiting for transfers between devices, local(): lax.all_to_all(outgoing, 'stream', split_axis=0, concat_axis=0, tiled=True)  71.4 us
    all_to_all x1, waiting for transfers between devices, local(): lax.all_to_all(features, 'mod', split_axis=0, concat_axis=1, tiled=True)  55.3 us
    dot_general x1, matrix products, encode(): jnp.einsum('wm,brmc->brwc', mix_out, mixed_tok, preferred_element_type=jn...  39.8 us
    unnamed x25, local copies, waits for them, and re-layouts  14.7 us
    dot_general x1, matrix products, encode(): jnp.einsum('bth,hc->btc', hidden, chan_out, preferred_element_type=jnp.fl...  13 us
    all_to_all x1, starting transfers between devices, local(): lax.all_to_all(outgoing, 'stream', split_axis=0, concat_axis=0, tiled=True)  8.46 us
    all_to_all x1, starting transfers between devices, local(): lax.all_to_all(features, 'mod', split_axis=0, concat_axis=1, tiled=True)  7.69 us
    dot_general x1, matrix products, stem_layer(): jnp.einsum('fapbq,pqc->fabc', pixel_tiles, kernel, preferred_element_type...  7.39 us
  transfers between devices with their start and end apart: 4, of which 4 were waited for; matrix products, arithmetic and copies ran while one was open for 2% of the time, Pallas kernels for 0%

commit v1 on v0

v1 whole, which is shorter than its diff:
```python
import jax
import jax.numpy as jnp
from jax import lax
from jax.sharding import PartitionSpec as P

PATCH = 16


def rms_norm(values):
    return values * lax.rsqrt(jnp.mean(values * values, axis=-1, keepdims=True) + 1e-06)


def stem_layer(frame_pixels, stem_weight):
    count, height, width = frame_pixels.shape
    pixel_tiles = frame_pixels.reshape(count, height // PATCH, PATCH, width // PATCH, PATCH)
    kernel = stem_weight.reshape(PATCH, PATCH, -1)
    response = jnp.einsum(
        "fapbq,pqc->fabc", pixel_tiles, kernel, preferred_element_type=jnp.float32
    )
    return jax.nn.gelu(response).astype(jnp.bfloat16).reshape(count, -1, kernel.shape[-1])


def local(
    pixels,
    stem_weight,
    veto_weight,
    hit_frames,
    assign,
    token_in,
    token_out,
    chan_in,
    chan_out,
    readout,
    latent_gain,
    class_weight,
):
    f32 = jnp.float32
    bf16 = jnp.bfloat16
    stream_count = lax.axis_size("stream")
    mod_index = lax.axis_index("mod")

    pieces = (token_in[0], token_out[0], chan_in[0], chan_out[0])
    flat = jnp.concatenate([w.reshape(-1) for w in pieces])
    gathered = lax.all_gather(flat, "stream")
    weights, offset = [], 0
    for w in pieces:
        size = w.size
        weights.append(gathered[:, offset:offset + size].reshape((stream_count,) + w.shape))
        offset += size
    tin_all, tout_all, cin_all, cout_all = weights

    features = stem_layer(pixels[0], stem_weight)[:, :, :]
    channels = features.shape[-1]
    row_len = features.shape[1]

    means = jnp.mean(features.astype(f32), axis=1)
    row_weight = lax.dynamic_slice_in_dim(veto_weight, mod_index, 1, axis=0)
    veto_part = jnp.sum(means * row_weight, axis=1)
    veto = lax.psum_scatter(veto_part, "mod", scatter_dimension=0, tiled=True)

    hits = hit_frames[0]
    targets = assign[0, :, 0]
    order = jnp.argsort(targets, stable=True)
    sorted_targets = targets[order]
    x = jnp.take(features, hits[order], axis=0)
    resid = x.astype(f32)
    normed = rms_norm(resid).astype(bf16)
    tin_g = jnp.take(tin_all, sorted_targets, axis=0)
    tout_g = jnp.take(tout_all, sorted_targets, axis=0)
    mixed_tok = jax.nn.gelu(
        jnp.einsum("jmw,jwc->jmc", tin_g, normed, preferred_element_type=f32)
    ).astype(bf16)
    after_mix = (
        resid + jnp.einsum("jwm,jmc->jwc", tout_g, mixed_tok, preferred_element_type=f32)
    ).astype(bf16)
    hit_count = after_mix.shape[0]
    tokens = after_mix.reshape(hit_count * row_len, channels)
    group_sizes = (
        jnp.sum(targets[None, :] == jnp.arange(stream_count, dtype=targets.dtype)[:, None], axis=1)
        * row_len
    ).astype(jnp.int32)
    normed_two = rms_norm(tokens.astype(f32)).astype(bf16)
    hidden = jax.nn.gelu(
        lax.ragged_dot(normed_two, cin_all, group_sizes, preferred_element_type=f32)
    ).astype(bf16)
    after_mlp = tokens.astype(f32) + lax.ragged_dot(
        hidden, cout_all, group_sizes, preferred_element_type=f32
    )
    pooled_sorted = jnp.mean(after_mlp.reshape(hit_count, row_len, channels), axis=1).astype(bf16)
    pooled = jnp.zeros_like(pooled_sorted).at[order].set(pooled_sorted)
    row_readout = lax.dynamic_slice_in_dim(readout, mod_index * channels, channels, axis=0)
    projected_part = jnp.dot(pooled, row_readout, preferred_element_type=f32)
    projected = lax.psum_scatter(projected_part, "mod", scatter_dimension=0, tiled=True)
    latent = rms_norm(projected) * latent_gain
    class_scores = jnp.dot(latent, class_weight, precision=lax.Precision.HIGHEST)
    return (veto[None], latent[None], class_scores[None])


def solution(mesh):
    in_specs = (
        P("stream", None, "mod", None),
        P(),
        P(),
        P("stream", None),
        P("stream", None, None),
        P("stream", None, None),
        P("stream", None, None),
        P("stream", None, None),
        P("stream", None, None),
        P(),
        P(),
        P(),
    )
    out_specs = (P("stream", "mod"), P("stream", "mod", None), P("stream", "mod", None))
    return jax.shard_map(local, mesh=mesh, in_specs=in_specs, out_specs=out_specs, check_vma=False)
```

time: 289 us -> 331 us (1.15)
  the two profiles are of different devices: /device:TPU:10 before, /device:TPU:1 now
where the time goes in v1:
time: 331 us; the launch traced here: 329 us
  waiting for transfers between devices  108 us (33%)
  blocking collectives  65.4 us (20%)
  local copies, waits for them, and re-layouts  48.6 us (15%)
  Pallas kernels  39.1 us (12%)
  matrix products  27.8 us (8%)
  other arithmetic  25 us (8%)
  between operations  15.6 us (5%)
    unnamed x3, waiting for transfers between devices  108 us
    unnamed x1, blocking collectives  65.4 us
    another operation x2, Pallas kernels  37.5 us
    unnamed x32, local copies, waits for them, and re-layouts  22.9 us
    dot_general x1, matrix products, local(): jnp.einsum('jwm,jmc->jwc', tout_g, mixed_tok, preferred_element_type=f32)  19.8 us
    convert_element_type x1, other arithmetic, local(): hidden = jax.nn.gelu(lax.ragged_dot(normed_two, cin_all, group_sizes, pre...  8.14 us
  transfers between devices with their start and end apart: 2, of which 1 were waited for; matrix products, arithmetic and copies ran while one was open for 12% of the time, Pallas kernels for 0%

profile of v1, /device:TPU:1, one launch (start us, length us, event | category | flops | bytes accessed | tf_op | source)
XLA Modules:
  0.0 329.1 jit_solution(2520182828318324288)
XLA Ops:
  7.2 1.0 copy.41
  8.3 0.7 reshape_squeeze.14
  9.0 0.8 copy.36
  9.9 0.2 reshape_squeeze.13
  10.0 1.6 pad_maximum_fusion
  11.8 13.0 %copy.34 = bf16[1,768,16,384]{1,3,2,0:T(8,128)(2,1)} copy(bf16[1,768,16,384]{3,2,1,0:T(8,128)(2,1)} %param.12) | data formatting | bytes 18874368 | tf_op args[0]
  24.8 0.1 convert_reduce_fusion.1
  24.9 3.2 sort.17
  28.1 0.5 broadcast_multiply_fusion
  28.6 1.6 ragged-dot-metadata
  30.3 1.6 gather_fusion.2
  31.9 1.6 gather_fusion
  33.5 6.3 %convert_reduce_fusion = (f32[768,128]{1,0:T(8,128)S(1)}, bf16[768,24,128]{2,0,1:T(8,128)(2,1)S(1)}) fusion(bf16[768,16,24,16]{0,3,2,1:T(8,128)(2,1)} %bitcast.54, bf16[16,16,128,1]{2,1,3,0:T(8,128)(2,1)S(1)} %bitcast.67), kind=kOutput, calls=%fused_computation.35 | convolution fusion | flops 1233813504 | bytes 14614528 | tf_op jit(solution)/shard_map/fapbq,pqc->fabc/dot_general | solution.py:17
  39.9 5.2 %copy.35 = bf16[768,24,128]{2,1,0:T(8,128)(2,1)} copy(bf16[768,24,128]{2,0,1:T(8,128)(2,1)S(1)} %get-tuple-element.30) | data formatting | bytes 9437184 | tf_op jit(solution)/shard_map/convert_element_type | solution.py:20
  45.0 0.6 dynamic-slice
  46.3 3.3 %gather_fusion.1 = bf16[192,24,128]{2,1,0:T(8,128)(2,1)S(1)} fusion(bf16[768,24,128]{2,1,0:T(8,128)(2,1)} %copy.35, s32[1024]{0:T(1024)S(1)} %pad_clamp_fusion.1), kind=kCustom, calls=%fused_computation.1 | custom fusion | bytes 2360064 | tf_op jit(solution)/shard_map/jit(_take)/gather | solution.py:65
  49.6 0.7 multiply_bitcast_fusion
  50.4 0.2 multiply_reduce_fusion
  50.5 65.4 %all-reduce = f32[768]{0:T(1024)S(1)} all-reduce(f32[768]{0:T(1024)S(1)} %multiply_reduce_fusion), channel_id=3, replica_groups=mesh['stream'=8,'mod'=32] {'mod'}, use_global_device_ids=true, to_apply=%region_2.0.clone | all-reduce | flops 768 | bytes 6144
  116.0 0.5 compare_and_fusion
  116.5 0.9 fusion.34
  117.5 2.7 reshape.173
  120.2 0.7 fusion.69
  120.9 1.5 slice_bitcast_fusion
  122.5 2.1 reshape.120
  124.6 0.3 copy.37
  124.9 0.9 copy.50
  125.8 3.3 gather_fusion.4
  129.1 3.3 %gather_fusion.3 = bf16[192,24,384]{2,1,0:T(8,128)(2,1)} fusion(bf16[8,24,384]{2,1,0:T(8,128)(2,1)S(1)} %bitcast.53, s32[1024]{0:T(1024)S(1)} %pad_clamp_fusion), kind=kCustom, calls=%fused_computation.3 | custom fusion | bytes 7078656 | tf_op jit(solution)/shard_map/jit(_take)/gather | solution.py:69
  132.4 19.8 %fusion.37 = (f32[192,24]{1,0:T(8,128)S(1)}, bf16[192,24,128]{2,1,0:T(8,128)(2,1)}) fusion(bf16[192,384,24]{1,2,0:T(8,128)(2,1)} %gather_fusion.4, pred[192]{0:T(512)(128)(4,1)S(1)} %copy-done.7, f32[192,24]{1,0:T(8,128)S(1)} %add_rsqrt_fusion.1, bf16[192,24,128]{2,1,0:T(8,128)(2,1)S(1)} %copy-done.4, pred[192]{0:T(512)(128)(4,1)S(1)} %get-tuple-element.34, ...), kind=kOutput, calls=%fused_computation.49 | convolution fusion | flops 1000926720 | bytes 9474432 | tf_op jit(solution)/shard_map/jwm,jmc->jwc/dot_general | solution.py:74
  152.3 0.1 rsqrt.29
  152.4 2.5 copy.49
  154.9 3.8 %fusion.38 = bf16[4608,128]{1,0:T(8,128)(2,1)} fusion(bf16[192,24,128]{2,1,0:T(8,128)(2,1)} %get-tuple-element.32, f32[4608]{0:T(1024)S(1)} %rsqrt.29), kind=kLoop, calls=%fused_computation.50 | loop fusion | flops 1769472 | bytes 2377728 | tf_op jit(solution)/shard_map/convert_element_type | solution.py:82
  158.7 19.1 %ragged-dot-none.1 = f32[4608,512]{1,0:T(8,128)} custom-call(s32[1]{0:T(128)} %get-tuple-element.5, s32[9]{0:T(128)} %get-tuple-element.6, s32[25]{0:T(128)} %get-tuple-element.7, s32[25]{0:T(128)} %get-tuple-element.8, s32[1]{0:T(128)} %get-tuple-element.5, bf16[4608,128]{1,0:T(8,128)(2,1)} %fusion.38, bf16[8,128,512]{2,1,0:T(8,128)(2,1)} %bitcast.57), custom_call_target="tpu_custom_call" | custom-call | flops 603979776 | bytes 11665440 | tf_op jit(solution)/shard_map/ragged_dot_general/ragged-dot-none
  177.8 8.1 %fusion.27 = bf16[4608,512]{1,0:T(8,128)(2,1)} fusion(f32[4608,512]{1,0:T(8,128)} %ragged-dot-none.1), kind=kLoop, calls=%fused_computation.34 | loop fusion | flops 21233664 | bytes 14155776 | tf_op jit(solution)/shard_map/convert_element_type | solution.py:85
  186.0 1.1 copy.48
  187.1 18.4 %ragged-dot-none = f32[4608,128]{1,0:T(8,128)} custom-call(s32[1]{0:T(128)} %get-tuple-element.5, s32[9]{0:T(128)} %get-tuple-element.6, s32[25]{0:T(128)} %get-tuple-element.7, s32[25]{0:T(128)} %get-tuple-element.8, s32[1]{0:T(128)} %get-tuple-element.5, bf16[4608,512]{1,0:T(8,128)(2,1)} %fusion.27, bf16[8,512,128]{2,1,0:T(8,128)(2,1)} %bitcast.56), custom_call_target="tpu_custom_call" | custom-call | flops 603979776 | bytes 8126496 | tf_op jit(solution)/shard_map/ragged_dot_general/ragged-dot-none
  205.5 2.2 bitcast_add_fusion
  207.7 0.3 reduce_sum.68
  208.0 1.0 scatter_custom_fusion
  209.1 0.8 fusion.54
  209.9 0.6 dynamic-slice_bitcast_fusion
  211.1 107.5 %all-reduce.4.cloned.1.call-done = f32[192,128]{1,0:T(8,128)} async-done(((f32[192,128]{1,0:T(8,128)}), f32[192,128]{1,0:T(8,128)}) %all-reduce.4.cloned.1.call-update) | async-done | bytes 98320
  318.6 0.8 multiply_reduce_fusion.1
  319.4 0.8 fusion.57
  320.2 0.6 copy.38
  320.8 0.9 convolution_bitcast_fusion
  321.7 0.6 copy.39
  (37 shorter events, 0.3 us)
Async XLA Ops:
  7.2 201.9 %copy-start = (bf16[4096,128]{1,0:T(8,128)(2,1)S(1)}, bf16[4096,128]{1,0:T(8,128)(2,1)}, u32[]{:S(2)}) copy-start(bf16[4096,128]{1,0:T(8,128)(2,1)} %param.21) | copy-start | bytes 3145732
  7.2 110.3 %all-gather.3.cloned.1.call-start = ((), (), s32[]{:S(2)}) async-start(), calls=%async_computation | async-start | bytes 2691072 | tf_op jit(solution)/shard_map/all_gather | solution.py:44
  11.7 306.9 %all-reduce.4.cloned.1.call-start = ((), (), s32[]{:S(2)}) async-start(), calls=%async_computation.1 | async-start | bytes 196608
  11.7 13.1 %copy-start.1 = (s32[1,192,1]{1,2,0:T(1,128)S(1)}, s32[1,192,1]{1,2,0:T(1,128)}, u32[]{:S(2)}) copy-start(s32[1,192,1]{1,2,0:T(1,128)} %param.16) | copy-start | bytes 2308
  11.8 20.2 %copy-start.2 = (s32[1,192]{1,0:T(1,128)S(1)}, s32[1,192]{1,0:T(1,128)}, u32[]{:S(2)}) copy-start(s32[1,192]{1,0:T(1,128)} %param.15) | copy-start | bytes 2308
  11.8 21.8 %copy-start.8 = (bf16[256,128]{1,0:T(8,128)(2,1)S(1)}, bf16[256,128]{1,0:T(8,128)(2,1)}, u32[]{:S(2)}) copy-start(bf16[256,128]{1,0:T(8,128)(2,1)} %param.13) | copy-start | bytes 196612
  39.8 5.2 %copy-start.10 = (u32[256]{0:T(256)S(1)}, u32[256]{0:T(256)}, u32[]{:S(2)}) copy-start(u32[256]{0:T(256)} %constant.103) | copy-start | bytes 3076
  49.6 67.9 %copy-start.3 = (bf16[192,24,128]{2,1,0:T(8,128)(2,1)}, bf16[192,24,128]{2,1,0:T(8,128)(2,1)S(1)}, u32[]{:S(2)}) copy-start(bf16[192,24,128]{2,1,0:T(8,128)(2,1)S(1)} %gather_fusion.1) | copy-start | bytes 3538948
  129.1 3.3 %copy-start.4 = (bf16[192,24,128]{2,1,0:T(8,128)(2,1)S(1)}, bf16[192,24,128]{2,1,0:T(8,128)(2,1)}, u32[]{:S(2)}) copy-start(bf16[192,24,128]{2,1,0:T(8,128)(2,1)} %copy-done.3) | copy-start | bytes 3538948
  129.1 3.3 %copy-start.7 = (pred[192]{0:T(512)(128)(4,1)S(1)}, pred[192]{0:T(512)(128)(4,1)}, u32[]{:S(2)}) copy-start(pred[192]{0:T(512)(128)(4,1)} %get-tuple-element.33) | copy-start | bytes 580
  177.8 8.1 %copy-start.5 = (bf16[1,8,512,128]{3,1,2,0:T(8,128)(2,1)S(1)}, bf16[1,8,512,128]{3,1,2,0:T(8,128)(2,1)}, u32[]{:S(2)}) copy-start(bf16[1,8,512,128]{3,1,2,0:T(8,128)(2,1)} %get-tuple-element.25) | copy-start | bytes 3145732
  205.5 114.0 %copy-start.6 = (f32[128]{0:T(128)S(1)}, f32[128]{0:T(128)}, u32[]{:S(2)}) copy-start(f32[128]{0:T(128)} %param.22) | copy-start | bytes 1540
  205.5 115.3 %copy-start.9 = (f32[128,8]{0,1:T(8,128)S(1)}, f32[128,8]{0,1:T(8,128)}, u32[]{:S(2)}) copy-start(f32[128,8]{0,1:T(8,128)} %param.23) | copy-start | bytes 12292
Sparse Core Ops, SparseCore 0:
  11.8 42.5 all-gather.2
  210.0 108.5 all-reduce.3

commit v2 on v1

--- a/solution.py
+++ b/solution.py
@@ -56,7 +56,6 @@
     means = jnp.mean(features.astype(f32), axis=1)
     row_weight = lax.dynamic_slice_in_dim(veto_weight, mod_index, 1, axis=0)
     veto_part = jnp.sum(means * row_weight, axis=1)
-    veto = lax.psum_scatter(veto_part, "mod", scatter_dimension=0, tiled=True)
 
     hits = hit_frames[0]
     targets = assign[0, :, 0]
@@ -90,7 +89,19 @@
     pooled = jnp.zeros_like(pooled_sorted).at[order].set(pooled_sorted)
     row_readout = lax.dynamic_slice_in_dim(readout, mod_index * channels, channels, axis=0)
     projected_part = jnp.dot(pooled, row_readout, preferred_element_type=f32)
-    projected = lax.psum_scatter(projected_part, "mod", scatter_dimension=0, tiled=True)
+    module_count = lax.axis_size("mod")
+    packed = jnp.concatenate(
+        [
+            projected_part.reshape(module_count, -1),
+            veto_part.reshape(module_count, -1),
+        ],
+        axis=1,
+    )
+    received = lax.all_to_all(packed, "mod", split_axis=0, concat_axis=0, tiled=True)
+    totals = jnp.sum(received, axis=0)
+    split = projected_part.size // module_count
+    projected = totals[:split].reshape(-1, channels)
+    veto = totals[split:]
     latent = rms_norm(projected) * latent_gain
     class_scores = jnp.dot(latent, class_weight, precision=lax.Precision.HIGHEST)
     return (veto[None], latent[None], class_scores[None])

time: 331 us -> 173 us (0.52)
  waiting for transfers between devices: 108 us -> 0.04 us
  blocking collectives: 65.4 us -> 16.8 us
    unnamed x3 -> x1, waiting for transfers between devices: 108 us -> 0.02 us
    unnamed x1 -> x0, blocking collectives: 65.4 us -> none
    all_to_all x0 -> x1, blocking collectives: none -> 16.8 us  [local(): lax.all_to_all(packed, 'mod', split_axis=0, concat_axis=0, tiled=True)]
    unnamed x32 -> x34, local copies, waits for them, and re-layouts: 22.9 us -> 21.7 us
  transfers between devices with their start and end apart: 2 -> 1, of which waited for: 1 -> 0; matrix products, arithmetic and copies ran while one was open for 12% -> 24% of each run, Pallas kernels for 0% -> 1%
where the time goes in v2:
time: 173 us; the launch traced here: 171 us
  local copies, waits for them, and re-layouts  50.3 us (29%)
  Pallas kernels  37 us (21%)
  matrix products  28 us (16%)
  other arithmetic  25 us (14%)
  blocking collectives  16.8 us (10%)
  between operations  14.3 us (8%)
    another operation x2, Pallas kernels  35.2 us
    unnamed x34, local copies, waits for them, and re-layouts  21.7 us
    dot_general x1, matrix products, local(): jnp.einsum('jwm,jmc->jwc', tout_g, mixed_tok, preferred_element_type=f32)  19.8 us
    all_to_all x1, blocking collectives, local(): lax.all_to_all(packed, 'mod', split_axis=0, concat_axis=0, tiled=True)  16.8 us
    convert_element_type x1, other arithmetic, local(): hidden = jax.nn.gelu(lax.ragged_dot(normed_two, cin_all, group_sizes, pre...  8.14 us
    dot_general x1, matrix products, stem_layer(): jnp.einsum('fapbq,pqc->fabc', pixel_tiles, kernel, preferred_element_type...  7.81 us
    convert_element_type x1, local copies, waits for them, and re-layouts, stem_layer(): jax.nn.gelu(response).astype(jnp.bfloat16)  7.53 us
    gather x2, local copies, waits for them, and re-layouts, local(): x = jnp.take(features, hits[order], axis=0)  4.92 us
  transfers between devices with their start and end apart: 1, of which 0 were waited for; matrix products, arithmetic and copies ran while one was open for 24% of the time, Pallas kernels for 1%

profile of v2, /device:TPU:1, one launch (start us, length us, event | category | flops | bytes accessed | tf_op | source)
XLA Modules:
  0.0 171.4 jit_solution(4035876636906777080)
XLA Ops:
  7.2 1.0 copy.37
  8.3 0.7 reshape_squeeze.14
  9.0 0.8 copy.33
  9.9 0.2 reshape_squeeze.13
  10.0 1.7 pad_maximum_fusion
  11.7 13.0 %copy.31 = bf16[1,768,16,384]{1,3,2,0:T(8,128)(2,1)} copy(bf16[1,768,16,384]{3,2,1,0:T(8,128)(2,1)} %param.12) | data formatting | bytes 18874368 | tf_op args[0]
  24.8 0.7 multiply_bitcast_fusion
  25.5 7.8 %convert_reduce_fusion = (f32[768,128]{1,0:T(8,128)S(1)}, bf16[768,24,128]{2,0,1:T(8,128)(2,1)}) fusion(bf16[768,16,24,16]{0,3,2,1:T(8,128)(2,1)} %bitcast.60, bf16[16,16,128,1]{2,1,3,0:T(8,128)(2,1)S(1)} %bitcast.74), kind=kOutput, calls=%fused_computation.35 | convolution fusion | flops 1233813504 | bytes 14614528 | tf_op jit(solution)/shard_map/fapbq,pqc->fabc/dot_general | solution.py:17
  33.3 0.2 multiply_reduce_fusion
  33.6 3.2 %sort.17 = (s32[192]{0:T(256)}, s32[192]{0:T(256)S(1)}) sort(s32[192]{0:T(256)S(1)} %bitcast.55, s32[192]{0:T(256)S(1)} %iota.8), dimensions={0}, to_apply=%region_0.0 | sort | flops 1536 | bytes 3072 | tf_op jit(solution)/shard_map/jit(argsort)/sort | solution.py:62
  36.7 0.1 convert_reduce_fusion.1
  36.8 0.5 broadcast_multiply_fusion
  37.4 1.8 %ragged-dot-metadata = (s32[9]{0:T(128)}, s32[25]{0:T(128)}, s32[25]{0:T(128)}, s32[1]{0:T(128)}) custom-call(s32[8]{0:T(128)} %broadcast_multiply_fusion), custom_call_target="tpu_custom_call" | custom-call | tf_op ragged-dot-metadata
  39.2 1.6 gather_fusion.2
  40.8 1.6 gather_fusion
  42.5 7.5 %copy.32 = bf16[768,24,128]{2,1,0:T(8,128)(2,1)} copy(bf16[768,24,128]{2,0,1:T(8,128)(2,1)} %get-tuple-element.30) | data formatting | bytes 9437184 | tf_op jit(solution)/shard_map/convert_element_type | solution.py:20
  50.0 3.3 %gather_fusion.1 = bf16[192,24,128]{2,1,0:T(8,128)(2,1)S(1)} fusion(bf16[768,24,128]{2,1,0:T(8,128)(2,1)} %copy.32, s32[1024]{0:T(1024)S(1)} %pad_clamp_fusion.1), kind=kCustom, calls=%fused_computation.1 | custom fusion | bytes 2360064 | tf_op jit(solution)/shard_map/jit(_take)/gather | solution.py:64
  53.3 0.6 pad_clamp_fusion
  54.0 0.5 compare_and_fusion
  54.5 0.9 fusion.34
  55.5 2.7 %reshape.243 = bf16[8,149504]{1,0:T(8,128)(2,1)S(1)} reshape(bf16[1196032]{0:T(1024)(128)(2,1)} %all-gather.3.cloned.1.call-done) | data formatting | bytes 4784128 | tf_op jit(solution)/shard_map/all_gather | solution.py:44
  58.2 0.7 fusion.70
  58.9 1.5 slice_bitcast_fusion
  60.5 2.1 %reshape.186 = bf16[8,384,24]{2,1,0:T(8,128)(2,1)S(1)} reshape(bf16[8,9216]{1,0:T(8,128)(2,1)} %get-tuple-element.28) | data formatting | bytes 294912 | tf_op jit(solution)/shard_map/reshape | solution.py:48
  62.6 0.3 copy.34
  62.9 0.9 copy.46
  63.8 3.4 %gather_fusion.4 = bf16[192,384,24]{1,2,0:T(8,128)(2,1)} fusion(bf16[8,384,24]{1,2,0:T(8,128)(2,1)S(1)} %copy.34, s32[1024]{0:T(1024)} %pad_clamp_fusion), kind=kCustom, calls=%fused_computation.4 | custom fusion | bytes 7078656 | tf_op jit(solution)/shard_map/jit(_take)/gather | solution.py:67
  67.2 3.6 %gather_fusion.3 = bf16[192,24,384]{2,1,0:T(8,128)(2,1)} fusion(bf16[8,24,384]{2,1,0:T(8,128)(2,1)S(1)} %bitcast.59, s32[1024]{0:T(1024)} %pad_clamp_fusion), kind=kCustom, calls=%fused_computation.3 | custom fusion | bytes 7078656 | tf_op jit(solution)/shard_map/jit(_take)/gather | solution.py:68
  70.8 19.8 %fusion.37 = (f32[192,24]{1,0:T(8,128)S(1)}, bf16[192,24,128]{2,1,0:T(8,128)(2,1)}) fusion(bf16[192,384,24]{1,2,0:T(8,128)(2,1)} %gather_fusion.4, pred[192]{0:T(512)(128)(4,1)S(1)} %copy-done.10, f32[192,24]{1,0:T(8,128)S(1)} %add_rsqrt_fusion.1, bf16[192,24,128]{2,1,0:T(8,128)(2,1)S(1)} %copy-done.4, pred[192]{0:T(512)(128)(4,1)S(1)} %copy-done.8, ...), kind=kOutput, calls=%fused_computation.49 | convolution fusion | flops 1000926720 | bytes 9474432 | tf_op jit(solution)/shard_map/jwm,jmc->jwc/dot_general | solution.py:73
  90.7 0.1 rsqrt.29
  90.8 2.5 %copy.45 = bf16[1,8,128,512]{3,2,1,0:T(8,128)(2,1)} copy(bf16[1,8,128,512]{3,1,2,0:T(8,128)(2,1)} %bitcast.64) | data formatting | bytes 2097152
  93.3 3.8 %fusion.38 = bf16[4608,128]{1,0:T(8,128)(2,1)} fusion(bf16[192,24,128]{2,1,0:T(8,128)(2,1)} %get-tuple-element.32, f32[4608]{0:T(1024)S(1)} %rsqrt.29), kind=kLoop, calls=%fused_computation.50 | loop fusion | flops 1769472 | bytes 2377728 | tf_op jit(solution)/shard_map/convert_element_type | solution.py:81
  97.1 18.0 %ragged-dot-none.1 = f32[4608,512]{1,0:T(8,128)} custom-call(s32[1]{0:T(128)} %get-tuple-element.5, s32[9]{0:T(128)} %get-tuple-element.6, s32[25]{0:T(128)} %get-tuple-element.7, s32[25]{0:T(128)} %get-tuple-element.8, s32[1]{0:T(128)} %get-tuple-element.5, bf16[4608,128]{1,0:T(8,128)(2,1)} %fusion.38, bf16[8,128,512]{2,1,0:T(8,128)(2,1)} %bitcast.63), custom_call_target="tpu_custom_call" | custom-call | flops 603979776 | bytes 11665440 | tf_op jit(solution)/shard_map/ragged_dot_general/ragged-dot-none
  115.1 8.1 %fusion.27 = bf16[4608,512]{1,0:T(8,128)(2,1)} fusion(f32[4608,512]{1,0:T(8,128)} %ragged-dot-none.1), kind=kLoop, calls=%fused_computation.34 | loop fusion | flops 21233664 | bytes 14155776 | tf_op jit(solution)/shard_map/convert_element_type | solution.py:84
  123.2 1.1 copy.44
  124.4 17.2 %ragged-dot-none = f32[4608,128]{1,0:T(8,128)} custom-call(s32[1]{0:T(128)} %get-tuple-element.5, s32[9]{0:T(128)} %get-tuple-element.6, s32[25]{0:T(128)} %get-tuple-element.7, s32[25]{0:T(128)} %get-tuple-element.8, s32[1]{0:T(128)} %get-tuple-element.5, bf16[4608,512]{1,0:T(8,128)(2,1)} %fusion.27, bf16[8,512,128]{2,1,0:T(8,128)(2,1)} %bitcast.62), custom_call_target="tpu_custom_call" | custom-call | flops 603979776 | bytes 8126496 | tf_op jit(solution)/shard_map/ragged_dot_general/ragged-dot-none
  141.6 2.2 %bitcast_add_fusion = f32[4608,128]{1,0:T(8,128)S(1)} fusion(f32[4608,128]{1,0:T(8,128)} %ragged-dot-none, bf16[192,24,128]{2,1,0:T(8,128)(2,1)} %get-tuple-element.32), kind=kLoop, calls=%fused_computation.46 | loop fusion | flops 1179648 | bytes 5898240 | tf_op jit(solution)/shard_map/add | solution.py:85
  143.8 0.3 reduce_sum.75
  144.1 1.2 scatter_custom_fusion
  145.3 0.1 fusion.54
  145.5 0.1 all_to_all.6
  145.6 16.8 %all_to_all.9 = f32[32,1,792]{2,1,0:T(1,128)S(1)} all-to-all(f32[32,1,792]{2,1,0:T(1,128)S(1)} %all_to_all.6), channel_id=1, replica_groups=mesh['stream'=8,'mod'=32] {'mod'}, dimensions={0} | all-to-all | bytes 202752 | tf_op jit(solution)/shard_map/all_to_all | solution.py:100
  162.4 0.1 reduce_sum.78
  162.5 0.5 slice_bitcast_fusion.1
  163.0 0.1 fusion.57
  163.1 0.7 multiply_multiply_fusion.3
  163.8 0.2 convolution_bitcast_fusion
  164.0 0.6 copy.35
  (42 shorter events, 0.3 us)
Async XLA Ops:
  7.2 138.1 %copy-start = (bf16[4096,128]{1,0:T(8,128)(2,1)S(1)}, bf16[4096,128]{1,0:T(8,128)(2,1)}, u32[]{:S(2)}) copy-start(bf16[4096,128]{1,0:T(8,128)(2,1)} %param.21) | copy-start | bytes 3145732
  7.2 48.3 %all-gather.3.cloned.1.call-start = ((), (), s32[]{:S(2)}) async-start(), calls=%async_computation.1 | async-start | bytes 2691072 | tf_op jit(solution)/shard_map/all_gather | solution.py:44
  11.7 13.7 %copy-start.11 = (bf16[256,128]{1,0:T(8,128)(2,1)S(1)}, bf16[256,128]{1,0:T(8,128)(2,1)}, u32[]{:S(2)}) copy-start(bf16[256,128]{1,0:T(8,128)(2,1)} %param.13) | copy-start | bytes 196612
  25.5 8.1 %copy-start.1 = (s32[1,192,1]{1,2,0:T(1,128)S(1)}, s32[1,192,1]{1,2,0:T(1,128)}, u32[]{:S(2)}) copy-start(s32[1,192,1]{1,2,0:T(1,128)} %param.16) | copy-start | bytes 2308
  25.5 15.4 %copy-start.2 = (s32[1,192]{1,0:T(1,128)S(1)}, s32[1,192]{1,0:T(1,128)}, u32[]{:S(2)}) copy-start(s32[1,192]{1,0:T(1,128)} %param.15) | copy-start | bytes 2308
  39.2 10.8 %copy-start.6 = (s32[192]{0:T(256)}, s32[192]{0:T(256)S(1)}, u32[]{:S(2)}) copy-start(s32[192]{0:T(256)S(1)} %compare_select_fusion.4) | copy-start | bytes 2308
  53.3 2.1 %copy-start.3 = (bf16[192,24,128]{2,1,0:T(8,128)(2,1)}, bf16[192,24,128]{2,1,0:T(8,128)(2,1)S(1)}, u32[]{:S(2)}) copy-start(bf16[192,24,128]{2,1,0:T(8,128)(2,1)S(1)} %gather_fusion.1) | copy-start | bytes 3538948
  54.5 1.0 copy-start.7
  67.2 3.6 %copy-start.4 = (bf16[192,24,128]{2,1,0:T(8,128)(2,1)S(1)}, bf16[192,24,128]{2,1,0:T(8,128)(2,1)}, u32[]{:S(2)}) copy-start(bf16[192,24,128]{2,1,0:T(8,128)(2,1)} %copy-done.3) | copy-start | bytes 3538948
  67.2 3.6 %copy-start.8 = (pred[192]{0:T(512)(128)(4,1)S(1)}, pred[192]{0:T(512)(128)(4,1)}, u32[]{:S(2)}) copy-start(pred[192]{0:T(512)(128)(4,1)} %copy-done.7) | copy-start | bytes 580
  67.2 3.6 %copy-start.10 = (pred[192]{0:T(512)(128)(4,1)S(1)}, pred[192]{0:T(512)(128)(4,1)}, u32[]{:S(2)}) copy-start(pred[192]{0:T(512)(128)(4,1)} %get-tuple-element.33) | copy-start | bytes 580
  115.1 8.1 %copy-start.5 = (bf16[1,8,512,128]{3,1,2,0:T(8,128)(2,1)S(1)}, bf16[1,8,512,128]{3,1,2,0:T(8,128)(2,1)}, u32[]{:S(2)}) copy-start(bf16[1,8,512,128]{3,1,2,0:T(8,128)(2,1)} %get-tuple-element.25) | copy-start | bytes 3145732
  141.6 21.5 %copy-start.9 = (f32[128]{0:T(128)S(1)}, f32[128]{0:T(128)}, u32[]{:S(2)}) copy-start(f32[128]{0:T(128)} %param.22) | copy-start | bytes 1540
  141.6 22.2 %copy-start.12 = (f32[128,8]{0,1:T(8,128)S(1)}, f32[128,8]{0,1:T(8,128)}, u32[]{:S(2)}) copy-start(f32[128,8]{0,1:T(8,128)} %param.23) | copy-start | bytes 12292
Sparse Core Ops, SparseCore 0:
  11.8 42.7 all-gather.2

commit v3 on v2

v3 whole, which is shorter than its diff:
```python
import functools

import jax
import jax.numpy as jnp
from jax import lax
from jax.experimental import pallas as pl
from jax.experimental.pallas import tpu as pltpu
from jax.sharding import PartitionSpec as P

PATCH = 16
BLOCK_HITS = 16


def rms_norm(values):
    return values * lax.rsqrt(jnp.mean(values * values, axis=-1, keepdims=True) + 1e-06)


def stem_layer(frame_pixels, stem_weight):
    count, height, width = frame_pixels.shape
    pixel_tiles = frame_pixels.reshape(count, height // PATCH, PATCH, width // PATCH, PATCH)
    kernel = stem_weight.reshape(PATCH, PATCH, -1)
    response = jnp.einsum(
        "fapbq,pqc->fabc", pixel_tiles, kernel, preferred_element_type=jnp.float32
    )
    return jax.nn.gelu(response).astype(jnp.bfloat16).reshape(count, -1, kernel.shape[-1])


def encoder_kernel(
    tgt_ref, gstart_ref, gend_ref,
    x_ref, tin_ref, tout_ref, cin_ref, cout_ref, ro_ref,
    o_ref, mix_scr, hid_scr, out_scr,
):
    f32, bf16 = jnp.float32, jnp.bfloat16
    block = pl.program_id(0)
    hits, row_len, channels = x_ref.shape
    groups = cin_ref.shape[0]
    base = block * hits
    for h in range(hits):
        t = tgt_ref[base + h]
        xh = x_ref[h].astype(f32)
        normed = rms_norm(xh).astype(bf16)
        pre = jnp.dot(tin_ref[t], normed, preferred_element_type=f32)
        mixed = jax.nn.gelu(pre).astype(bf16)
        mix = jnp.dot(tout_ref[t], mixed, preferred_element_type=f32)
        mix_scr[h * row_len:(h + 1) * row_len, :] = (xh + mix).astype(bf16).astype(f32)
    after_mix = mix_scr[...]
    normed_two = rms_norm(after_mix).astype(bf16)
    token = base * row_len + lax.broadcasted_iota(jnp.int32, (hits * row_len, 1), 0)
    first = tgt_ref[base]
    last = tgt_ref[base + hits - 1]
    for g in range(groups):
        @pl.when((g >= first) & (g <= last))
        def _():
            inside = (token >= gstart_ref[g]) & (token < gend_ref[g])
            part = jnp.dot(normed_two, cin_ref[g], preferred_element_type=f32)
            hid_scr[...] = jnp.where(inside, part, hid_scr[...])
    hidden = jax.nn.gelu(hid_scr[...]).astype(bf16)
    for g in range(groups):
        @pl.when((g >= first) & (g <= last))
        def _():
            inside = (token >= gstart_ref[g]) & (token < gend_ref[g])
            part = jnp.dot(hidden, cout_ref[g], preferred_element_type=f32)
            out_scr[...] = jnp.where(inside, part, out_scr[...])
    after_mlp = after_mix + out_scr[...]
    pooled = jnp.mean(after_mlp.reshape(hits, row_len, channels), axis=1).astype(bf16)
    o_ref[...] = jnp.dot(pooled, ro_ref[...], preferred_element_type=f32)


def encode_rows(x, sorted_targets, gstart, gend, tin_all, tout_all, cin_all, cout_all, row_readout):
    hit_count, row_len, channels = x.shape
    steps = hit_count // BLOCK_HITS
    full = lambda a: pl.BlockSpec(a.shape, lambda i, *_: (0,) * a.ndim)
    grid_spec = pltpu.PrefetchScalarGridSpec(
        num_scalar_prefetch=3,
        grid=(steps,),
        in_specs=[
            pl.BlockSpec((BLOCK_HITS, row_len, channels), lambda i, *_: (i, 0, 0)),
            full(tin_all),
            full(tout_all),
            full(cin_all),
            full(cout_all),
            full(row_readout),
        ],
        out_specs=pl.BlockSpec((BLOCK_HITS, channels), lambda i, *_: (i, 0)),
        scratch_shapes=[
            pltpu.VMEM((BLOCK_HITS * row_len, channels), jnp.float32),
            pltpu.VMEM((BLOCK_HITS * row_len, cin_all.shape[-1]), jnp.float32),
            pltpu.VMEM((BLOCK_HITS * row_len, channels), jnp.float32),
        ],
    )
    return pl.pallas_call(
        encoder_kernel,
        grid_spec=grid_spec,
        out_shape=jax.ShapeDtypeStruct((hit_count, channels), jnp.float32),
        compiler_params=pltpu.CompilerParams(dimension_semantics=("arbitrary",)),
    )(sorted_targets, gstart, gend, x, tin_all, tout_all, cin_all, cout_all, row_readout)


def local(
    pixels,
    stem_weight,
    veto_weight,
    hit_frames,
    assign,
    token_in,
    token_out,
    chan_in,
    chan_out,
    readout,
    latent_gain,
    class_weight,
):
    f32 = jnp.float32
    stream_count = lax.axis_size("stream")
    module_count = lax.axis_size("mod")
    mod_index = lax.axis_index("mod")

    tin_all = lax.all_gather(token_in[0], "stream")
    tout_all = lax.all_gather(token_out[0], "stream")
    cin_all = lax.all_gather(chan_in[0], "stream")
    cout_all = lax.all_gather(chan_out[0], "stream")

    features = stem_layer(pixels[0], stem_weight)
    channels = features.shape[-1]
    row_len = features.shape[1]

    means = jnp.mean(features.astype(f32), axis=1)
    row_weight = lax.dynamic_slice_in_dim(veto_weight, mod_index, 1, axis=0)
    veto_part = jnp.sum(means * row_weight, axis=1)

    hits = hit_frames[0]
    targets = assign[0, :, 0].astype(jnp.int32)
    order = jnp.argsort(targets, stable=True)
    sorted_targets = targets[order]
    x = jnp.take(features, hits[order], axis=0)
    counts = jnp.sum(
        (targets[None, :] == jnp.arange(stream_count, dtype=jnp.int32)[:, None]).astype(jnp.int32),
        axis=1,
    )
    gend = jnp.cumsum(counts) * row_len
    gstart = gend - counts * row_len
    row_readout = lax.dynamic_slice_in_dim(readout, mod_index * channels, channels, axis=0)
    projected_sorted = encode_rows(
        x, sorted_targets, gstart.astype(jnp.int32), gend.astype(jnp.int32),
        tin_all, tout_all, cin_all, cout_all, row_readout,
    )
    projected_part = jnp.zeros_like(projected_sorted).at[order].set(projected_sorted)

    packed = jnp.concatenate(
        [
            projected_part.reshape(module_count, -1),
            veto_part.reshape(module_count, -1),
        ],
        axis=1,
    )
    received = lax.all_to_all(packed, "mod", split_axis=0, concat_axis=0, tiled=True)
    totals = jnp.sum(received, axis=0)
    split = projected_part.size // module_count
    projected = totals[:split].reshape(-1, channels)
    veto = totals[split:]
    latent = rms_norm(projected) * latent_gain
    class_scores = jnp.dot(latent, class_weight, precision=lax.Precision.HIGHEST)
    return (veto[None], latent[None], class_scores[None])


def solution(mesh):
    in_specs = (
        P("stream", None, "mod", None),
        P(),
        P(),
        P("stream", None),
        P("stream", None, None),
        P("stream", None, None),
        P("stream", None, None),
        P("stream", None, None),
        P("stream", None, None),
        P(),
        P(),
        P(),
    )
    out_specs = (P("stream", "mod"), P("stream", "mod", None), P("stream", "mod", None))
    return jax.shard_map(local, mesh=mesh, in_specs=in_specs, out_specs=out_specs, check_vma=False)
```

time: 173 us -> 196 us (1.13)
  blocking collectives: 16.8 us -> 71 us
  Pallas kernels: 37 us -> 61.5 us
  matrix products: 28 us -> 7.9 us
  local copies, waits for them, and re-layouts: 50.3 us -> 32.1 us
  other arithmetic: 25 us -> 7.59 us
    pallas_call x0 -> x1, Pallas kernels: none -> 61.5 us  [encode_rows(): pl.pallas_call(encoder_kernel, grid_spec=grid_spec, out_shape=jax.ShapeDt...]
    all_gather x0 -> x2, blocking collectives: none -> 45.4 us  [the longest x1 23.4 us: local(): tin_all = lax.all_gather(token_in[0], 'stream')]
    another operation x2 -> x0, Pallas kernels: 35.2 us -> none
    dot_general x2 -> x0, matrix products: 19.9 us -> none  [the longest x1 19.8 us: local(): jnp.einsum('jwm,jmc->jwc', tout_g, mixed_tok, preferred_element_type=f32)]
    convert_element_type x2 -> x0, other arithmetic: 12 us -> none  [the longest x1 8.14 us: local(): hidden = jax.nn.gelu(lax.ragged_dot(normed_two, cin_all, group_sizes, pre...]
    all_to_all x1, blocking collectives: 16.8 us -> 25.7 us  [local(): lax.all_to_all(packed, 'mod', split_axis=0, concat_axis=0, tiled=True)]
    unnamed x34 -> x18, local copies, waits for them, and re-layouts: 21.7 us -> 13.7 us
    gather x2 -> x0, local copies, waits for them, and re-layouts: 7 us -> none  [the longest x1 3.59 us: local(): tout_g = jnp.take(tout_all, sorted_targets, axis=0)]
  transfers between devices with their start and end apart: 1 -> 2, of which waited for: 0 -> 0; matrix products, arithmetic and copies ran while one was open for 24% -> 22% of each run, Pallas kernels for 1% -> 0%
where the time goes in v3:
time: 196 us
  blocking collectives  71 us (36%)
  Pallas kernels  61.5 us (31%)
  local copies, waits for them, and re-layouts  32.1 us (16%)
  between operations  14.2 us (7%)
  matrix products  7.9 us (4%)
  other arithmetic  7.59 us (4%)
    pallas_call x1, Pallas kernels, encode_rows(): pl.pallas_call(encoder_kernel, grid_spec=grid_spec, out_shape=jax.ShapeDt...  61.5 us
    all_to_all x1, blocking collectives, local(): lax.all_to_all(packed, 'mod', split_axis=0, concat_axis=0, tiled=True)  25.7 us
    all_gather x1, blocking collectives, local(): tin_all = lax.all_gather(token_in[0], 'stream')  23.4 us
    all_gather x1, blocking collectives, local(): tout_all = lax.all_gather(token_out[0], 'stream')  22 us
    unnamed x18, local copies, waits for them, and re-layouts  13.7 us
    dot_general x1, matrix products, stem_layer(): jnp.einsum('fapbq,pqc->fabc', pixel_tiles, kernel, preferred_element_type...  7.7 us
    convert_element_type x1, local copies, waits for them, and re-layouts, stem_layer(): jax.nn.gelu(response).astype(jnp.bfloat16)  7.53 us
    gather x2, local copies, waits for them, and re-layouts, local(): x = jnp.take(features, hits[order], axis=0)  4.89 us
  transfers between devices with their start and end apart: 2, of which 0 were waited for; matrix products, arithmetic and copies ran while one was open for 22% of the time, Pallas kernels for 0%

profile of v3, /device:TPU:1, one launch (start us, length us, event | category | flops | bytes accessed | tf_op | source)
XLA Modules:
  0.0 195.8 jit_solution(17868882431112956088)
XLA Ops:
  7.2 0.0 copy-start
  7.2 0.0 all-gather.3.cloned.1.call-start
  7.2 0.7 all-gather.3.cloned.1.call-update
  7.9 0.0 all-gather.5.cloned.1.call-start
  8.0 0.7 all-gather.5.cloned.1.call-update
  8.7 0.0 copy-start.1
  8.7 0.0 copy-start.6
  8.7 13.0 %copy.27 = bf16[1,768,16,384]{1,3,2,0:T(8,128)(2,1)} copy(bf16[1,768,16,384]{3,2,1,0:T(8,128)(2,1)} %param.12) | data formatting | bytes 18874368 | tf_op args[0]
  21.7 0.0 copy-done.1
  21.7 3.2 %sort.17 = (s32[192]{0:T(256)}, s32[192]{0:T(256)S(1)}) sort(s32[192]{0:T(256)S(1)} %bitcast.35, s32[192]{0:T(256)S(1)} %iota.8), dimensions={0}, to_apply=%region_0.0 | sort | flops 1536 | bytes 3072 | tf_op jit(solution)/shard_map/jit(argsort)/sort | solution.py:133
  24.9 0.0 copy-done.6
  24.9 7.7 %convert_reduce_fusion = (f32[768,128]{1,0:T(8,128)S(1)}, bf16[768,24,128]{2,0,1:T(8,128)(2,1)}) fusion(bf16[768,16,24,16]{0,3,2,1:T(8,128)(2,1)} %bitcast.39, bf16[16,16,128,1]{2,1,3,0:T(8,128)(2,1)S(1)} %bitcast.43), kind=kOutput, calls=%fused_computation.13 | convolution fusion | flops 1233813504 | bytes 14614528 | tf_op jit(solution)/shard_map/fapbq,pqc->fabc/dot_general | solution.py:22
  32.6 0.0 copy-start.3
  32.6 0.0 copy-start.4
  32.6 0.7 multiply_bitcast_fusion
  33.4 0.2 multiply_reduce_fusion
  33.5 0.1 reshape.152
  33.6 2.2 %gather_fusion = s32[192]{0:T(256)} fusion(s32[192]{0:T(256)S(1)} %bitcast.36, s32[1024]{0:T(1024)S(1)} %pad_clamp_fusion.1), kind=kCustom, calls=%fused_computation | custom fusion | bytes 2304 | tf_op jit(solution)/shard_map/gather | solution.py:134
  35.8 0.1 convert_reduce_fusion.1
  35.9 0.2 reduce-window.9
  36.1 0.0 copy-start.5
  36.1 0.0 copy-start.7
  36.1 7.5 %copy.28 = bf16[768,24,128]{2,1,0:T(8,128)(2,1)} copy(bf16[768,24,128]{2,0,1:T(8,128)(2,1)} %get-tuple-element.18) | data formatting | bytes 9437184 | tf_op jit(solution)/shard_map/convert_element_type | solution.py:25
  43.6 0.0 copy-done.2
  43.6 1.6 gather_fusion.1
  45.3 0.0 copy-done.3
  45.3 23.4 %all_gather.12 = bf16[8,384,24]{1,2,0:T(8,128)(2,1)S(1)} all-gather(bf16[1,384,24]{1,2,0:T(8,128)(2,1)S(1)} %copy-done.3), channel_id=1, replica_groups=mesh['stream'=8,'mod'=32] {'stream'}, dimensions={0}, use_global_device_ids=true | all-gather | bytes 165888 | tf_op jit(solution)/shard_map/all_gather | solution.py:118
  68.6 1.2 copy.29.tin_ref
  69.8 3.3 %gather_fusion.2 = bf16[192,24,128]{2,1,0:T(8,128)(2,1)S(1)} fusion(bf16[768,24,128]{2,1,0:T(8,128)(2,1)} %copy.28, s32[1024]{0:T(1024)S(1)} %pad_clamp_fusion), kind=kCustom, calls=%fused_computation.2 | custom fusion | bytes 2360064 | tf_op jit(solution)/shard_map/jit(_take)/gather | solution.py:135
  73.1 0.0 copy-done.4
  73.1 22.0 %all_gather.13.tout_ref = bf16[8,24,384]{2,1,0:T(8,128)(2,1)} all-gather(bf16[1,24,384]{2,1,0:T(8,128)(2,1)S(1)} %copy-done.4), channel_id=1, replica_groups=mesh['stream'=8,'mod'=32] {'stream'}, dimensions={0}, use_global_device_ids=true | all-gather | bytes 165888 | tf_op jit(solution)/shard_map/all_gather | solution.py:119
  95.1 0.0 copy-done
  95.1 0.6 constant_dynamic-slice_fusion.ro_ref
  95.7 0.5 multiply_bitcast_fusion.1.gend_ref
  96.2 0.5 multiply_subtract_fusion.gstart_ref
  96.8 1.3 broadcast_select_fusion.x_ref
  98.1 61.5 %shard_map.139 = f32[192,128]{1,0:T(8,128)} custom-call(s32[192]{0:T(256)} %gather_fusion, s32[8]{0:T(128)} %multiply_subtract_fusion.gstart_ref, s32[8]{0:T(128)} %multiply_bitcast_fusion.1.gend_ref, bf16[192,24,128]{2,1,0:T(8,128)(2,1)} %broadcast_select_fusion.x_ref, bf16[8,384,24]{2,1,0:T(8,128)(2,1)} %copy.29.tin_ref, ...), custom_call_target="tpu_custom_call" | custom-call | tf_op jit(solution)/shard_map/pallas_call | solution.py:91
  159.6 1.4 scatter_custom_fusion
  161.1 0.1 all_to_all.6
  161.1 25.7 %all_to_all.9 = f32[32,1,792]{2,1,0:T(1,128)S(1)} all-to-all(f32[32,1,792]{2,1,0:T(1,128)S(1)} %all_to_all.6), channel_id=1, replica_groups=mesh['stream'=8,'mod'=32] {'mod'}, dimensions={0} | all-to-all | bytes 202752 | tf_op jit(solution)/shard_map/all_to_all | solution.py:156
  186.8 0.1 reduce_sum.48
  186.9 0.5 slice_bitcast_fusion
  187.4 0.1 fusion.10
  187.6 0.0 copy-done.5
  187.6 0.7 multiply_multiply_fusion.1
  188.2 0.0 copy-done.7
  188.2 0.2 convolution_bitcast_fusion
  188.4 0.6 copy.30
  (13 shorter events, 0.1 us)
Async XLA Ops:
  7.2 88.0 %copy-start = (bf16[4096,128]{1,0:T(8,128)(2,1)S(1)}, bf16[4096,128]{1,0:T(8,128)(2,1)}, u32[]{:S(2)}) copy-start(bf16[4096,128]{1,0:T(8,128)(2,1)} %param.21) | copy-start | bytes 3145732
  7.2 90.9 %all-gather.3.cloned.1.call-start = ((), (), s32[]{:S(2)}) async-start(), calls=%async_computation.1 | async-start | bytes 1179648 | tf_op jit(solution)/shard_map/all_gather | solution.py:120
  7.9 90.1 %all-gather.5.cloned.1.call-start = ((), (), s32[]{:S(2)}) async-start(), calls=%async_computation.2 | async-start | bytes 1179648 | tf_op jit(solution)/shard_map/all_gather | solution.py:121
  8.7 13.1 %copy-start.1 = (s32[1,192,1]{1,2,0:T(1,128)S(1)}, s32[1,192,1]{1,2,0:T(1,128)}, u32[]{:S(2)}) copy-start(s32[1,192,1]{1,2,0:T(1,128)} %param.16) | copy-start | bytes 2308
  8.7 16.2 %copy-start.6 = (bf16[256,128]{1,0:T(8,128)(2,1)S(1)}, bf16[256,128]{1,0:T(8,128)(2,1)}, u32[]{:S(2)}) copy-start(bf16[256,128]{1,0:T(8,128)(2,1)} %param.13) | copy-start | bytes 196612
  32.6 11.0 %copy-start.2 = (s32[1,192]{1,0:T(1,128)S(1)}, s32[1,192]{1,0:T(1,128)}, u32[]{:S(2)}) copy-start(s32[1,192]{1,0:T(1,128)} %param.15) | copy-start | bytes 2308
  32.6 12.6 %copy-start.3 = (bf16[1,384,24]{1,2,0:T(8,128)(2,1)S(1)}, bf16[1,384,24]{1,2,0:T(8,128)(2,1)}, u32[]{:S(2)}) copy-start(bf16[1,384,24]{1,2,0:T(8,128)(2,1)} %param.17) | copy-start | bytes 55300
  32.6 40.5 %copy-start.4 = (bf16[1,24,384]{2,1,0:T(8,128)(2,1)S(1)}, bf16[1,24,384]{2,1,0:T(8,128)(2,1)}, u32[]{:S(2)}) copy-start(bf16[1,24,384]{2,1,0:T(8,128)(2,1)} %param.18) | copy-start | bytes 55300
  36.1 151.4 %copy-start.5 = (f32[128]{0:T(128)S(1)}, f32[128]{0:T(128)}, u32[]{:S(2)}) copy-start(f32[128]{0:T(128)} %param.22) | copy-start | bytes 1540
  36.1 152.1 %copy-start.7 = (f32[128,8]{0,1:T(8,128)S(1)}, f32[128,8]{0,1:T(8,128)}, u32[]{:S(2)}) copy-start(f32[128,8]{0,1:T(8,128)} %param.23) | copy-start | bytes 12292
Sparse Core Ops, SparseCore 0:
  9.8 38.8 all-gather.2
  50.5 36.8 all-gather.4

commit v4 on v3

--- a/solution.py
+++ b/solution.py
@@ -115,10 +115,13 @@
     module_count = lax.axis_size("mod")
     mod_index = lax.axis_index("mod")
 
-    tin_all = lax.all_gather(token_in[0], "stream")
-    tout_all = lax.all_gather(token_out[0], "stream")
-    cin_all = lax.all_gather(chan_in[0], "stream")
-    cout_all = lax.all_gather(chan_out[0], "stream")
+    pieces = (token_in[0], token_out[0], chan_in[0], chan_out[0])
+    gathered = lax.all_gather(jnp.concatenate([w.reshape(-1) for w in pieces]), "stream")
+    weights, offset = [], 0
+    for w in pieces:
+        weights.append(gathered[:, offset:offset + w.size].reshape((stream_count,) + w.shape))
+        offset += w.size
+    tin_all, tout_all, cin_all, cout_all = weights
 
     features = stem_layer(pixels[0], stem_weight)
     channels = features.shape[-1]

time: 196 us -> 160 us (0.82)
  blocking collectives: 71 us -> 17.5 us
  local copies, waits for them, and re-layouts: 32.1 us -> 48.2 us
    all_gather x2 -> x0, blocking collectives: 45.4 us -> none  [the longest x1 23.4 us: local(): tin_all = lax.all_gather(token_in[0], 'stream')]
    unnamed x18 -> x20, local copies, waits for them, and re-layouts: 13.7 us -> 23.5 us
    all_to_all x1, blocking collectives: 25.7 us -> 17.5 us  [local(): lax.all_to_all(packed, 'mod', split_axis=0, concat_axis=0, tiled=True)]
    reshape x0 -> x1, local copies, waits for them, and re-layouts: none -> 3.01 us  [local(): gathered[:, offset:offset + w.size].reshape((stream_count,) + w.shape)]
  transfers between devices with their start and end apart: 2 -> 1, of which waited for: 0 -> 0; matrix products, arithmetic and copies ran while one was open for 22% -> 27% of each run, Pallas kernels for 0% -> 0%
where the time goes in v4:
time: 160 us; the launch traced here: 159 us
  Pallas kernels  61.7 us (39%)
  local copies, waits for them, and re-layouts  48.2 us (30%)
  blocking collectives  17.5 us (11%)
  between operations  14.2 us (9%)
  other arithmetic  9.2 us (6%)
  matrix products  8 us (5%)
    pallas_call x1, Pallas kernels, encode_rows(): pl.pallas_call(encoder_kernel, grid_spec=grid_spec, out_shape=jax.ShapeDt...  61.7 us
    unnamed x20, local copies, waits for them, and re-layouts  23.5 us
    all_to_all x1, blocking collectives, local(): lax.all_to_all(packed, 'mod', split_axis=0, concat_axis=0, tiled=True)  17.5 us
    dot_general x1, matrix products, stem_layer(): jnp.einsum('fapbq,pqc->fabc', pixel_tiles, kernel, preferred_element_type...  7.8 us
    convert_element_type x1, local copies, waits for them, and re-layouts, stem_layer(): jax.nn.gelu(response).astype(jnp.bfloat16)  7.53 us
    gather x2, local copies, waits for them, and re-layouts, local(): x = jnp.take(features, hits[order], axis=0)  4.91 us
  transfers between devices with their start and end apart: 1, of which 0 were waited for; matrix products, arithmetic and copies ran while one was open for 27% of the time, Pallas kernels for 0%

profile of v4, /device:TPU:1, one launch (start us, length us, event | category | flops | bytes accessed | tf_op | source)
XLA Modules:
  0.0 158.9 jit_solution(12299999352567294612)
XLA Ops:
  7.2 0.0 copy-start
  7.2 0.0 all-gather.3.cloned.1.call-start
  7.2 1.0 copy.31
  8.3 0.7 reshape_squeeze.14
  9.0 0.8 copy.28
  9.9 0.2 reshape_squeeze.13
  10.0 1.7 %pad_maximum_fusion = bf16[149504]{0:T(1024)(128)(2,1)} fusion(bf16[65536]{0:T(1024)(128)(2,1)} %bitcast.63, bf16[65536]{0:T(1024)(128)(2,1)S(1)} %bitcast.61, bf16[9216]{0:T(1024)(128)(2,1)S(1)} %reshape_squeeze.14, bf16[9216]{0:T(1024)(128)(2,1)S(1)} %reshape_squeeze.13), kind=kLoop, calls=%fused_computation.20 | loop fusion | flops 1196032 | bytes 598016 | tf_op jit(solution)/shard_map/concatenate | solution.py:119
  11.7 0.0 all-gather.3.cloned.1.call-update
  11.7 0.0 copy-start.4
  11.7 13.0 %copy.26 = bf16[1,768,16,384]{1,3,2,0:T(8,128)(2,1)} copy(bf16[1,768,16,384]{3,2,1,0:T(8,128)(2,1)} %param.12) | data formatting | bytes 18874368 | tf_op args[0]
  24.8 0.7 multiply_bitcast_fusion
  25.4 0.0 copy-done.4
  25.5 7.8 %convert_reduce_fusion = (f32[768,128]{1,0:T(8,128)S(1)}, bf16[768,24,128]{2,0,1:T(8,128)(2,1)}) fusion(bf16[768,16,24,16]{0,3,2,1:T(8,128)(2,1)} %bitcast.55, bf16[16,16,128,1]{2,1,3,0:T(8,128)(2,1)S(1)} %bitcast.67), kind=kOutput, calls=%fused_computation.13 | convolution fusion | flops 1233813504 | bytes 14614528 | tf_op jit(solution)/shard_map/fapbq,pqc->fabc/dot_general | solution.py:22
  33.3 0.2 multiply_reduce_fusion
  33.4 0.1 reshape.168
  33.5 0.0 copy-done.1
  33.5 3.2 %sort.17 = (s32[192]{0:T(256)}, s32[192]{0:T(256)S(1)}) sort(s32[192]{0:T(256)S(1)} %bitcast.51, s32[192]{0:T(256)S(1)} %iota.8), dimensions={0}, to_apply=%region_0.0 | sort | flops 1536 | bytes 3072 | tf_op jit(solution)/shard_map/jit(argsort)/sort | solution.py:136
  36.7 2.2 %gather_fusion = s32[192]{0:T(256)} fusion(s32[192]{0:T(256)S(1)} %bitcast.52, s32[1024]{0:T(1024)S(1)} %pad_clamp_fusion.1), kind=kCustom, calls=%fused_computation | custom fusion | bytes 2304 | tf_op jit(solution)/shard_map/gather | solution.py:137
  38.9 0.1 convert_reduce_fusion.1
  39.0 0.2 reduce-window.9
  39.2 7.5 %copy.27 = bf16[768,24,128]{2,1,0:T(8,128)(2,1)} copy(bf16[768,24,128]{2,0,1:T(8,128)(2,1)} %get-tuple-element.22) | data formatting | bytes 9437184 | tf_op jit(solution)/shard_map/convert_element_type | solution.py:25
  46.7 0.0 copy-done.2
  46.7 1.6 %gather_fusion.1 = s32[192]{0:T(256)S(1)} fusion(s32[192]{0:T(256)S(1)} %bitcast.54, s32[1024]{0:T(1024)S(1)} %pad_clamp_fusion.1), kind=kCustom, calls=%fused_computation.1 | custom fusion | bytes 2304 | tf_op jit(solution)/shard_map/gather | solution.py:138
  48.4 3.3 %gather_fusion.2 = bf16[192,24,128]{2,1,0:T(8,128)(2,1)S(1)} fusion(bf16[768,24,128]{2,1,0:T(8,128)(2,1)} %copy.27, s32[1024]{0:T(1024)S(1)} %pad_clamp_fusion), kind=kCustom, calls=%fused_computation.2 | custom fusion | bytes 2360064 | tf_op jit(solution)/shard_map/jit(_take)/gather | solution.py:138
  51.7 0.0 copy-done
  51.7 0.6 constant_dynamic-slice_fusion.ro_ref
  52.3 0.5 multiply_bitcast_fusion.1.gend_ref
  52.8 0.5 multiply_subtract_fusion.gstart_ref
  53.4 1.3 broadcast_select_fusion.x_ref
  54.6 2.7 %reshape.203 = bf16[8,149504]{1,0:T(8,128)(2,1)S(1)} reshape(bf16[1196032]{0:T(1024)(128)(2,1)} %all-gather.3.cloned.1.call-done) | data formatting | bytes 4784128 | tf_op jit(solution)/shard_map/all_gather | solution.py:119
  57.3 0.7 fusion.16
  58.1 1.4 slice_bitcast_fusion
  59.5 3.0 %reshape.163.tin_ref = bf16[8,384,24]{2,1,0:T(8,128)(2,1)} reshape(bf16[8,9216]{1,0:T(8,128)(2,1)} %get-tuple-element.20) | data formatting | bytes 294912 | tf_op jit(solution)/shard_map/reshape | solution.py:122
  62.5 1.6 copy.40
  64.1 2.6 %copy.39 = bf16[1,8,128,512]{3,2,1,0:T(8,128)(2,1)} copy(bf16[1,8,128,512]{3,1,2,0:T(8,128)(2,1)} %bitcast.58) | data formatting | bytes 2097152
  66.7 2.3 %copy.38 = bf16[1,8,512,128]{3,2,1,0:T(8,128)(2,1)} copy(bf16[1,8,512,128]{3,1,2,0:T(8,128)(2,1)} %get-tuple-element.17) | data formatting | bytes 2097152
  69.0 61.7 %shard_map.139 = f32[192,128]{1,0:T(8,128)} custom-call(s32[192]{0:T(256)} %gather_fusion, s32[8]{0:T(128)} %multiply_subtract_fusion.gstart_ref, s32[8]{0:T(128)} %multiply_bitcast_fusion.1.gend_ref, bf16[192,24,128]{2,1,0:T(8,128)(2,1)} %broadcast_select_fusion.x_ref, bf16[8,384,24]{2,1,0:T(8,128)(2,1)} %reshape.163.tin_ref, bf16[8,24,384]{2,1,0:T(8,128)(2,1)} %bitcast.59, ...), custom_call_target="tpu_custom_call" | custom-call | tf_op jit(solution)/shard_map/pallas_call | solution.py:91
  130.8 1.4 scatter_custom_fusion
  132.2 0.1 all_to_all.6
  132.3 17.5 %all_to_all.9 = f32[32,1,792]{2,1,0:T(1,128)S(1)} all-to-all(f32[32,1,792]{2,1,0:T(1,128)S(1)} %all_to_all.6), channel_id=1, replica_groups=mesh['stream'=8,'mod'=32] {'mod'}, dimensions={0} | all-to-all | bytes 202752 | tf_op jit(solution)/shard_map/all_to_all | solution.py:159
  149.9 0.1 reduce_sum.48
  149.9 0.5 slice_bitcast_fusion.1
  150.5 0.1 fusion.10
  150.6 0.0 copy-done.3
  150.6 0.7 multiply_multiply_fusion.1
  151.3 0.0 copy-done.5
  151.3 0.2 convolution_bitcast_fusion
  151.5 0.6 copy.29
  (15 shorter events, 0.1 us)
Async XLA Ops:
  7.2 44.5 %copy-start = (bf16[4096,128]{1,0:T(8,128)(2,1)S(1)}, bf16[4096,128]{1,0:T(8,128)(2,1)}, u32[]{:S(2)}) copy-start(bf16[4096,128]{1,0:T(8,128)(2,1)} %param.21) | copy-start | bytes 3145732
  7.2 47.5 %all-gather.3.cloned.1.call-start = ((), (), s32[]{:S(2)}) async-start(), calls=%async_computation.1 | async-start | bytes 2691072 | tf_op jit(solution)/shard_map/all_gather | solution.py:119
  11.7 13.7 %copy-start.4 = (bf16[256,128]{1,0:T(8,128)(2,1)S(1)}, bf16[256,128]{1,0:T(8,128)(2,1)}, u32[]{:S(2)}) copy-start(bf16[256,128]{1,0:T(8,128)(2,1)} %param.13) | copy-start | bytes 196612
  25.5 8.1 %copy-start.1 = (s32[1,192,1]{1,2,0:T(1,128)S(1)}, s32[1,192,1]{1,2,0:T(1,128)}, u32[]{:S(2)}) copy-start(s32[1,192,1]{1,2,0:T(1,128)} %param.16) | copy-start | bytes 2308
  33.3 13.5 %copy-start.2 = (s32[1,192]{1,0:T(1,128)S(1)}, s32[1,192]{1,0:T(1,128)}, u32[]{:S(2)}) copy-start(s32[1,192]{1,0:T(1,128)} %param.15) | copy-start | bytes 2308
  54.6 96.0 %copy-start.3 = (f32[128]{0:T(128)S(1)}, f32[128]{0:T(128)}, u32[]{:S(2)}) copy-start(f32[128]{0:T(128)} %param.22) | copy-start | bytes 1540
  54.6 96.6 %copy-start.5 = (f32[128,8]{0,1:T(8,128)S(1)}, f32[128,8]{0,1:T(8,128)}, u32[]{:S(2)}) copy-start(f32[128,8]{0,1:T(8,128)} %param.23) | copy-start | bytes 12292
Sparse Core Ops, SparseCore 0:
  11.8 42.6 all-gather.2

commit v5 on v4

--- a/solution.py
+++ b/solution.py
@@ -115,13 +115,15 @@
     module_count = lax.axis_size("mod")
     mod_index = lax.axis_index("mod")
 
-    pieces = (token_in[0], token_out[0], chan_in[0], chan_out[0])
+    pieces = (token_in[0], token_out[0])
     gathered = lax.all_gather(jnp.concatenate([w.reshape(-1) for w in pieces]), "stream")
     weights, offset = [], 0
     for w in pieces:
         weights.append(gathered[:, offset:offset + w.size].reshape((stream_count,) + w.shape))
         offset += w.size
-    tin_all, tout_all, cin_all, cout_all = weights
+    tin_all, tout_all = weights
+    cin_all = lax.all_gather(chan_in[0], "stream")
+    cout_all = lax.all_gather(chan_out[0], "stream")
 
     features = stem_layer(pixels[0], stem_weight)
     channels = features.shape[-1]
@@ -133,9 +135,15 @@
 
     hits = hit_frames[0]
     targets = assign[0, :, 0].astype(jnp.int32)
-    order = jnp.argsort(targets, stable=True)
-    sorted_targets = targets[order]
-    x = jnp.take(features, hits[order], axis=0)
+    position = jnp.arange(targets.shape[0], dtype=jnp.int32)
+    before = (targets[None, :] < targets[:, None]) | (
+        (targets[None, :] == targets[:, None]) & (position[None, :] < position[:, None])
+    )
+    rank = jnp.sum(before.astype(jnp.int32), axis=1)
+    picks = rank[None, :] == position[:, None]
+    sorted_targets = jnp.sum(jnp.where(picks, targets[None, :], 0), axis=1)
+    sorted_frames = jnp.sum(jnp.where(picks, hits[None, :], 0), axis=1)
+    x = jnp.take(features, sorted_frames, axis=0)
     counts = jnp.sum(
         (targets[None, :] == jnp.arange(stream_count, dtype=jnp.int32)[:, None]).astype(jnp.int32),
         axis=1,
@@ -147,7 +155,7 @@
         x, sorted_targets, gstart.astype(jnp.int32), gend.astype(jnp.int32),
         tin_all, tout_all, cin_all, cout_all, row_readout,
     )
-    projected_part = jnp.zeros_like(projected_sorted).at[order].set(projected_sorted)
+    projected_part = jnp.take(projected_sorted, rank, axis=0)
 
     packed = jnp.concatenate(
         [

time: 160 us -> 179 us (1.12)
  blocking collectives: 17.5 us -> 44.9 us
  local copies, waits for them, and re-layouts: 48.2 us -> 30.9 us
  waiting for transfers between devices: 0.02 us -> 13.9 us
  other arithmetic: 9.2 us -> 5.31 us
    all_gather x0 -> x1, blocking collectives: none -> 25 us  [local(): lax.all_gather(jnp.concatenate([w.reshape(-1) for w in pieces]), 'stream')]
    all_gather x1 -> x2, waiting for transfers between devices: 0.01 us -> 12.5 us  [the longest x1 12.5 us: local(): cout_all = lax.all_gather(chan_out[0], 'stream')]
    unnamed x20, local copies, waits for them, and re-layouts: 23.5 us -> 14.5 us
    sort x1 -> x0, other arithmetic: 3.17 us -> none  [local(): order = jnp.argsort(targets, stable=True)]
    all_gather x1, local copies, waits for them, and re-layouts: 2.7 us -> 0.13 us  [local(): lax.all_gather(jnp.concatenate([w.reshape(-1) for w in pieces]), 'stream')]
    all_to_all x1, blocking collectives: 17.5 us -> 19.9 us  [local(): lax.all_to_all(packed, 'mod', split_axis=0, concat_axis=0, tiled=True)]
    gather x3, local copies, waits for them, and re-layouts: 7.08 us -> 4.88 us  [the longest x1 3.28 us: local(): x = jnp.take(features, sorted_frames, axis=0)]
  transfers between devices with their start and end apart: 1 -> 2, of which waited for: 0 -> 1; matrix products, arithmetic and copies ran while one was open for 27% -> 22% of each run, Pallas kernels for 0% -> 0%
where the time goes in v5:
time: 179 us; the launch traced here: 178 us
  Pallas kernels  61 us (34%)
  blocking collectives  44.9 us (25%)
  local copies, waits for them, and re-layouts  30.9 us (17%)
  between operations  14.2 us (8%)
  waiting for transfers between devices  13.9 us (8%)
  matrix products  7.89 us (4%)
  other arithmetic  5.31 us (3%)
    pallas_call x1, Pallas kernels, encode_rows(): pl.pallas_call(encoder_kernel, grid_spec=grid_spec, out_shape=jax.ShapeDt...  61 us
    all_gather x1, blocking collectives, local(): lax.all_gather(jnp.concatenate([w.reshape(-1) for w in pieces]), 'stream')  25 us
    all_to_all x1, blocking collectives, local(): lax.all_to_all(packed, 'mod', split_axis=0, concat_axis=0, tiled=True)  19.9 us
    unnamed x20, local copies, waits for them, and re-layouts  14.5 us
    all_gather x1, waiting for transfers between devices, local(): cout_all = lax.all_gather(chan_out[0], 'stream')  12.5 us
    dot_general x1, matrix products, stem_layer(): jnp.einsum('fapbq,pqc->fabc', pixel_tiles, kernel, preferred_element_type...  7.69 us
    convert_element_type x1, local copies, waits for them, and re-layouts, stem_layer(): jax.nn.gelu(response).astype(jnp.bfloat16)  7.53 us
  transfers between devices with their start and end apart: 2, of which 1 were waited for; matrix products, arithmetic and copies ran while one was open for 22% of the time, Pallas kernels for 0%

profile of v5, /device:TPU:1, one launch (start us, length us, event | category | flops | bytes accessed | tf_op | source)
XLA Modules:
  0.0 178.2 jit_solution(7996658446807355890)
XLA Ops:
  7.2 0.0 copy-start
  7.2 0.0 all-gather.4.cloned.1.call-start
  7.2 0.7 all-gather.4.cloned.1.call-update
  7.9 0.0 all-gather.6.cloned.1.call-start
  8.0 0.7 all-gather.6.cloned.1.call-update
  8.7 0.0 copy-start.6
  8.7 13.0 %copy.27 = bf16[1,768,16,384]{1,3,2,0:T(8,128)(2,1)} copy(bf16[1,768,16,384]{3,2,1,0:T(8,128)(2,1)} %param.12) | data formatting | bytes 18874368 | tf_op args[0]
  21.7 0.0 copy-done.6
  21.7 0.0 copy-start.2
  21.7 0.0 copy-start.1
  21.8 7.7 %convert_reduce_fusion = (f32[768,128]{1,0:T(8,128)S(1)}, bf16[768,24,128]{2,0,1:T(8,128)(2,1)}) fusion(bf16[768,16,24,16]{0,3,2,1:T(8,128)(2,1)} %bitcast.46, bf16[16,16,128,1]{2,1,3,0:T(8,128)(2,1)S(1)} %bitcast.59), kind=kOutput, calls=%fused_computation.11 | convolution fusion | flops 1233813504 | bytes 14614528 | tf_op jit(solution)/shard_map/fapbq,pqc->fabc/dot_general | solution.py:22
  29.4 0.7 multiply_bitcast_fusion
  30.1 0.2 multiply_reduce_fusion
  30.3 0.1 reshape.181
  30.4 0.0 copy-done.3
  30.4 0.2 convert_reduce_fusion.1
  30.6 0.1 reduce_sum.79
  30.7 0.0 copy-done.4
  30.7 0.7 select_reduce_fusion
  31.4 0.0 copy-done.2
  31.5 0.0 copy-done.1
  31.5 0.1 copy.29
  31.6 0.2 reshape_squeeze.7
  31.8 25.0 %all-gather = bf16[147456]{0:T(1024)(128)(2,1)S(1)} all-gather(bf16[18432]{0:T(1024)(128)(2,1)S(1)} %pad_maximum_fusion), channel_id=2, replica_groups=mesh['stream'=8,'mod'=32] {'stream'}, dimensions={0}, use_global_device_ids=true | all-gather | bytes 331776 | tf_op jit(solution)/shard_map/all_gather | solution.py:119
  56.8 0.1 reshape.200
  56.9 0.1 convert_reduce_fusion.2
  57.0 0.2 reduce-window.9
  57.2 7.5 %copy.28 = bf16[768,24,128]{2,1,0:T(8,128)(2,1)} copy(bf16[768,24,128]{2,0,1:T(8,128)(2,1)} %get-tuple-element.20) | data formatting | bytes 9437184 | tf_op jit(solution)/shard_map/convert_element_type | solution.py:25
  64.8 2.2 %reshape.179.tin_ref = bf16[8,384,24]{2,1,0:T(8,128)(2,1)} reshape(bf16[8,9216]{1,0:T(8,128)(2,1)S(1)} %get-tuple-element.18) | data formatting | bytes 294912 | tf_op jit(solution)/shard_map/reshape | solution.py:122
  66.9 0.7 copy.37
  67.6 3.3 %gather_fusion = bf16[192,24,128]{2,1,0:T(8,128)(2,1)S(1)} fusion(bf16[768,24,128]{2,1,0:T(8,128)(2,1)} %copy.28, s32[1024]{0:T(1024)S(1)} %pad_clamp_fusion.1), kind=kCustom, calls=%fused_computation | custom fusion | bytes 2360064 | tf_op jit(solution)/shard_map/jit(_take)/gather | solution.py:146
  70.9 0.0 copy-done
  70.9 0.6 constant_dynamic-slice_fusion.ro_ref
  71.6 0.5 multiply_bitcast_fusion.1.gend_ref
  72.1 0.5 multiply_subtract_fusion.gstart_ref
  72.6 1.3 broadcast_select_fusion.x_ref
  73.9 12.5 %all-gather.6.cloned.1.call-done.cout_ref = bf16[8,512,128]{2,1,0:T(8,128)(2,1)} async-done(((bf16[1,512,128]{2,1,0:T(8,128)(2,1)}), bf16[8,512,128]{2,1,0:T(8,128)(2,1)}) %all-gather.6.cloned.1.call-update) | async-done | bytes 1048592 | tf_op jit(solution)/shard_map/all_gather | solution.py:126
  86.4 61.0 %shard_map.139 = f32[192,128]{1,0:T(8,128)} custom-call(s32[192]{0:T(256)} %get-tuple-element.16.tgt_ref, s32[8]{0:T(128)} %multiply_subtract_fusion.gstart_ref, s32[8]{0:T(128)} %multiply_bitcast_fusion.1.gend_ref, bf16[192,24,128]{2,1,0:T(8,128)(2,1)} %broadcast_select_fusion.x_ref, bf16[8,384,24]{2,1,0:T(8,128)(2,1)} %reshape.179.tin_ref, ...), custom_call_target="tpu_custom_call" | custom-call | tf_op jit(solution)/shard_map/pallas_call | solution.py:91
  147.4 1.6 gather_fusion.1
  149.0 0.1 broadcast_in_dim.54
  149.2 0.1 copy.30
  149.3 19.9 %all_to_all.9 = f32[32,1,792]{2,1,0:T(1,128)S(1)} all-to-all(f32[32,1,792]{2,1,0:T(1,128)S(1)} %copy.30), channel_id=1, replica_groups=mesh['stream'=8,'mod'=32] {'mod'}, dimensions={0} | all-to-all | bytes 202752 | tf_op jit(solution)/shard_map/all_to_all | solution.py:167
  169.2 0.1 reduce_sum.87
  169.3 0.5 slice_bitcast_fusion
  169.8 0.1 fusion.10
  170.0 0.7 multiply_multiply_fusion.1
  170.6 0.2 convolution_bitcast_fusion
  170.8 0.6 copy.31
  (21 shorter events, 0.2 us)
Async XLA Ops:
  7.2 63.8 %copy-start = (bf16[4096,128]{1,0:T(8,128)(2,1)S(1)}, bf16[4096,128]{1,0:T(8,128)(2,1)}, u32[]{:S(2)}) copy-start(bf16[4096,128]{1,0:T(8,128)(2,1)} %param.21) | copy-start | bytes 3145732
  7.2 66.7 %all-gather.4.cloned.1.call-start = ((), (), s32[]{:S(2)}) async-start(), calls=%async_computation.1 | async-start | bytes 1179648 | tf_op jit(solution)/shard_map/all_gather | solution.py:125
  7.9 78.5 %all-gather.6.cloned.1.call-start = ((), (), s32[]{:S(2)}) async-start(), calls=%async_computation.2 | async-start | bytes 1179648 | tf_op jit(solution)/shard_map/all_gather | solution.py:126
  8.7 13.1 %copy-start.6 = (bf16[256,128]{1,0:T(8,128)(2,1)S(1)}, bf16[256,128]{1,0:T(8,128)(2,1)}, u32[]{:S(2)}) copy-start(bf16[256,128]{1,0:T(8,128)(2,1)} %param.13) | copy-start | bytes 196612
  21.7 8.7 %copy-start.3 = (s32[1,192,1]{1,2,0:T(1,128)S(1)}, s32[1,192,1]{1,2,0:T(1,128)}, u32[]{:S(2)}) copy-start(s32[1,192,1]{1,2,0:T(1,128)} %param.16) | copy-start | bytes 2308
  21.7 9.0 %copy-start.4 = (s32[1,192]{1,0:T(1,128)S(1)}, s32[1,192]{1,0:T(1,128)}, u32[]{:S(2)}) copy-start(s32[1,192]{1,0:T(1,128)} %param.15) | copy-start | bytes 2308
  21.7 9.7 %copy-start.2 = (bf16[1,24,384]{2,1,0:T(8,128)(2,1)S(1)}, bf16[1,24,384]{2,1,0:T(8,128)(2,1)}, u32[]{:S(2)}) copy-start(bf16[1,24,384]{2,1,0:T(8,128)(2,1)} %param.18) | copy-start | bytes 55300
  21.7 9.7 %copy-start.1 = (bf16[1,384,24]{1,2,0:T(8,128)(2,1)S(1)}, bf16[1,384,24]{1,2,0:T(8,128)(2,1)}, u32[]{:S(2)}) copy-start(bf16[1,384,24]{1,2,0:T(8,128)(2,1)} %param.17) | copy-start | bytes 55300
  57.2 112.7 %copy-start.5 = (f32[128]{0:T(128)S(1)}, f32[128]{0:T(128)}, u32[]{:S(2)}) copy-start(f32[128]{0:T(128)} %param.22) | copy-start | bytes 1540
  57.2 113.4 %copy-start.7 = (f32[128,8]{0,1:T(8,128)S(1)}, f32[128,8]{0,1:T(8,128)}, u32[]{:S(2)}) copy-start(f32[128,8]{0,1:T(8,128)} %param.23) | copy-start | bytes 12292
Sparse Core Ops, SparseCore 0:
  9.8 38.1 all-gather.3
  49.8 36.5 all-gather.5

commit v6 on v5

--- a/solution.py
+++ b/solution.py
@@ -115,15 +115,13 @@
     module_count = lax.axis_size("mod")
     mod_index = lax.axis_index("mod")
 
-    pieces = (token_in[0], token_out[0])
+    pieces = (token_in[0], token_out[0], chan_in[0], chan_out[0])
     gathered = lax.all_gather(jnp.concatenate([w.reshape(-1) for w in pieces]), "stream")
     weights, offset = [], 0
     for w in pieces:
         weights.append(gathered[:, offset:offset + w.size].reshape((stream_count,) + w.shape))
         offset += w.size
-    tin_all, tout_all = weights
-    cin_all = lax.all_gather(chan_in[0], "stream")
-    cout_all = lax.all_gather(chan_out[0], "stream")
+    tin_all, tout_all, cin_all, cout_all = weights
 
     features = stem_layer(pixels[0], stem_weight)
     channels = features.shape[-1]

time: 179 us -> 159 us (0.89)
  blocking collectives: 44.9 us -> 18.2 us
  local copies, waits for them, and re-layouts: 30.9 us -> 44.8 us
  waiting for transfers between devices: 13.9 us -> 5.21 us
    all_gather x1 -> x0, blocking collectives: 25 us -> none  [local(): lax.all_gather(jnp.concatenate([w.reshape(-1) for w in pieces]), 'stream')]
    unnamed x20, local copies, waits for them, and re-layouts: 14.5 us -> 23.5 us
    all_gather x2 -> x1, waiting for transfers between devices: 12.5 us -> 5.2 us  [local(): lax.all_gather(jnp.concatenate([w.reshape(-1) for w in pieces]), 'stream')]
    all_gather x1, local copies, waits for them, and re-layouts: 0.13 us -> 2.68 us  [local(): lax.all_gather(jnp.concatenate([w.reshape(-1) for w in pieces]), 'stream')]
  transfers between devices with their start and end apart: 2 -> 1, of which waited for: 1 -> 1; matrix products, arithmetic and copies ran while one was open for 22% -> 23% of each run, Pallas kernels for 0% -> 0%
where the time goes in v6:
time: 159 us
  Pallas kernels  61.2 us (38%)
  local copies, waits for them, and re-layouts  44.8 us (28%)
  blocking collectives  18.2 us (11%)
  between operations  14.2 us (9%)
  matrix products  8 us (5%)
  other arithmetic  6.96 us (4%)
  waiting for transfers between devices  5.21 us (3%)
    pallas_call x1, Pallas kernels, encode_rows(): pl.pallas_call(encoder_kernel, grid_spec=grid_spec, out_shape=jax.ShapeDt...  61.2 us
    unnamed x20, local copies, waits for them, and re-layouts  23.5 us
    all_to_all x1, blocking collectives, local(): lax.all_to_all(packed, 'mod', split_axis=0, concat_axis=0, tiled=True)  18.2 us
    dot_general x1, matrix products, stem_layer(): jnp.einsum('fapbq,pqc->fabc', pixel_tiles, kernel, preferred_element_type...  7.8 us
    convert_element_type x1, local copies, waits for them, and re-layouts, stem_layer(): jax.nn.gelu(response).astype(jnp.bfloat16)  7.55 us
    all_gather x1, waiting for transfers between devices, local(): lax.all_gather(jnp.concatenate([w.reshape(-1) for w in pieces]), 'stream')  5.2 us
    gather x1, local copies, waits for them, and re-layouts, local(): x = jnp.take(features, sorted_frames, axis=0)  3.31 us
  transfers between devices with their start and end apart: 1, of which 1 were waited for; matrix products, arithmetic and copies ran while one was open for 23% of the time, Pallas kernels for 0%

profile of v6, /device:TPU:1, one launch (start us, length us, event | category | flops | bytes accessed | tf_op | source)
XLA Modules:
  0.0 158.6 jit_solution(5022590687589309462)
XLA Ops:
  7.2 0.0 copy-start
  7.2 0.0 all-gather.3.cloned.1.call-start
  7.2 1.0 copy.34
  8.3 0.7 reshape_squeeze.14
  9.0 0.8 copy.29
  9.9 0.2 reshape_squeeze.13
  10.0 1.7 %pad_maximum_fusion = bf16[149504]{0:T(1024)(128)(2,1)} fusion(bf16[65536]{0:T(1024)(128)(2,1)} %bitcast.67, bf16[65536]{0:T(1024)(128)(2,1)S(1)} %bitcast.64, bf16[9216]{0:T(1024)(128)(2,1)S(1)} %reshape_squeeze.14, bf16[9216]{0:T(1024)(128)(2,1)S(1)} %reshape_squeeze.13), kind=kLoop, calls=%fused_computation.18 | loop fusion | flops 1196032 | bytes 598016 | tf_op jit(solution)/shard_map/concatenate | solution.py:119
  11.7 0.0 all-gather.3.cloned.1.call-update
  11.7 0.0 copy-start.4
  11.7 13.0 %copy.27 = bf16[1,768,16,384]{1,3,2,0:T(8,128)(2,1)} copy(bf16[1,768,16,384]{3,2,1,0:T(8,128)(2,1)} %param.12) | data formatting | bytes 18874368 | tf_op args[0]
  24.8 0.7 multiply_bitcast_fusion
  25.4 0.0 copy-done.4
  25.5 7.8 %convert_reduce_fusion = (f32[768,128]{1,0:T(8,128)S(1)}, bf16[768,24,128]{2,0,1:T(8,128)(2,1)}) fusion(bf16[768,16,24,16]{0,3,2,1:T(8,128)(2,1)} %bitcast.58, bf16[16,16,128,1]{2,1,3,0:T(8,128)(2,1)S(1)} %bitcast.77), kind=kOutput, calls=%fused_computation.11 | convolution fusion | flops 1233813504 | bytes 14614528 | tf_op jit(solution)/shard_map/fapbq,pqc->fabc/dot_general | solution.py:22
  33.3 0.2 multiply_reduce_fusion
  33.4 0.1 reshape.189
  33.5 0.0 copy-done.1
  33.5 0.1 convert_reduce_fusion.2
  33.7 0.2 reduce-window.9
  33.8 7.5 %copy.28 = bf16[768,24,128]{2,1,0:T(8,128)(2,1)} copy(bf16[768,24,128]{2,0,1:T(8,128)(2,1)} %get-tuple-element.22) | data formatting | bytes 9437184 | tf_op jit(solution)/shard_map/convert_element_type | solution.py:25
  41.4 0.2 convert_reduce_fusion.1
  41.6 0.1 reduce_sum.79
  41.7 0.7 select_reduce_fusion
  42.4 3.3 %gather_fusion = bf16[192,24,128]{2,1,0:T(8,128)(2,1)S(1)} fusion(bf16[768,24,128]{2,1,0:T(8,128)(2,1)} %copy.28, s32[1024]{0:T(1024)S(1)} %pad_clamp_fusion.1), kind=kCustom, calls=%fused_computation | custom fusion | bytes 2360064 | tf_op jit(solution)/shard_map/jit(_take)/gather | solution.py:144
  45.8 0.6 constant_dynamic-slice_fusion.ro_ref
  46.4 0.5 multiply_bitcast_fusion.1.gend_ref
  46.9 0.5 multiply_subtract_fusion.gstart_ref
  47.5 1.3 broadcast_select_fusion.x_ref
  48.7 5.2 %all-gather.3.cloned.1.call-done = bf16[1196032]{0:T(1024)(128)(2,1)} async-done(((bf16[149504]{0:T(1024)(128)(2,1)}), bf16[1196032]{0:T(1024)(128)(2,1)}) %all-gather.3.cloned.1.call-update) | async-done | bytes 2392080 | tf_op jit(solution)/shard_map/all_gather | solution.py:119
  53.9 2.7 %reshape.208 = bf16[8,149504]{1,0:T(8,128)(2,1)S(1)} reshape(bf16[1196032]{0:T(1024)(128)(2,1)} %all-gather.3.cloned.1.call-done) | data formatting | bytes 4784128 | tf_op jit(solution)/shard_map/all_gather | solution.py:119
  56.6 0.0 copy-start.3
  56.6 0.0 copy-start.5
  56.6 0.7 fusion.16
  57.4 1.4 slice_bitcast_fusion
  58.8 3.0 %reshape.185.tin_ref = bf16[8,384,24]{2,1,0:T(8,128)(2,1)} reshape(bf16[8,9216]{1,0:T(8,128)(2,1)} %get-tuple-element.20) | data formatting | bytes 294912 | tf_op jit(solution)/shard_map/reshape | solution.py:122
  61.8 1.6 copy.44
  63.4 2.6 %copy.43 = bf16[1,8,128,512]{3,2,1,0:T(8,128)(2,1)} copy(bf16[1,8,128,512]{3,1,2,0:T(8,128)(2,1)} %bitcast.61) | data formatting | bytes 2097152
  66.0 2.3 %copy.42 = bf16[1,8,512,128]{3,2,1,0:T(8,128)(2,1)} copy(bf16[1,8,512,128]{3,1,2,0:T(8,128)(2,1)} %get-tuple-element.17) | data formatting | bytes 2097152
  68.3 61.2 %shard_map.139 = f32[192,128]{1,0:T(8,128)} custom-call(s32[192]{0:T(256)} %get-tuple-element.16.tgt_ref, s32[8]{0:T(128)} %multiply_subtract_fusion.gstart_ref, s32[8]{0:T(128)} %multiply_bitcast_fusion.1.gend_ref, bf16[192,24,128]{2,1,0:T(8,128)(2,1)} %broadcast_select_fusion.x_ref, bf16[8,384,24]{2,1,0:T(8,128)(2,1)} %reshape.185.tin_ref, ...), custom_call_target="tpu_custom_call" | custom-call | tf_op jit(solution)/shard_map/pallas_call | solution.py:91
  129.5 1.6 gather_fusion.1
  131.1 0.1 broadcast_in_dim.54
  131.3 0.1 copy.30
  131.4 18.2 %all_to_all.9 = f32[32,1,792]{2,1,0:T(1,128)S(1)} all-to-all(f32[32,1,792]{2,1,0:T(1,128)S(1)} %copy.30), channel_id=1, replica_groups=mesh['stream'=8,'mod'=32] {'mod'}, dimensions={0} | all-to-all | bytes 202752 | tf_op jit(solution)/shard_map/all_to_all | solution.py:165
  149.6 0.1 reduce_sum.87
  149.7 0.5 slice_bitcast_fusion.1
  150.2 0.1 fusion.10
  150.3 0.7 multiply_multiply_fusion.1
  151.0 0.2 convolution_bitcast_fusion
  151.2 0.6 copy.31
  (17 shorter events, 0.1 us)
Async XLA Ops:
  7.2 38.6 %copy-start = (bf16[4096,128]{1,0:T(8,128)(2,1)S(1)}, bf16[4096,128]{1,0:T(8,128)(2,1)}, u32[]{:S(2)}) copy-start(bf16[4096,128]{1,0:T(8,128)(2,1)} %param.21) | copy-start | bytes 3145732
  7.2 46.8 %all-gather.3.cloned.1.call-start = ((), (), s32[]{:S(2)}) async-start(), calls=%async_computation.1 | async-start | bytes 2691072 | tf_op jit(solution)/shard_map/all_gather | solution.py:119
  11.7 13.7 %copy-start.4 = (bf16[256,128]{1,0:T(8,128)(2,1)S(1)}, bf16[256,128]{1,0:T(8,128)(2,1)}, u32[]{:S(2)}) copy-start(bf16[256,128]{1,0:T(8,128)(2,1)} %param.13) | copy-start | bytes 196612
  25.5 8.1 %copy-start.1 = (s32[1,192,1]{1,2,0:T(1,128)S(1)}, s32[1,192,1]{1,2,0:T(1,128)}, u32[]{:S(2)}) copy-start(s32[1,192,1]{1,2,0:T(1,128)} %param.16) | copy-start | bytes 2308
  33.3 8.4 %copy-start.2 = (s32[1,192]{1,0:T(1,128)S(1)}, s32[1,192]{1,0:T(1,128)}, u32[]{:S(2)}) copy-start(s32[1,192]{1,0:T(1,128)} %param.15) | copy-start | bytes 2308
  56.6 93.7 %copy-start.3 = (f32[128]{0:T(128)S(1)}, f32[128]{0:T(128)}, u32[]{:S(2)}) copy-start(f32[128]{0:T(128)} %param.22) | copy-start | bytes 1540
  56.6 94.4 %copy-start.5 = (f32[128,8]{0,1:T(8,128)S(1)}, f32[128,8]{0,1:T(8,128)}, u32[]{:S(2)}) copy-start(f32[128,8]{0,1:T(8,128)} %param.23) | copy-start | bytes 12292
Sparse Core Ops, SparseCore 0:
  11.8 42.0 all-gather.2

commit v7 on v6

--- a/solution.py
+++ b/solution.py
@@ -96,6 +96,53 @@
     )(sorted_targets, gstart, gend, x, tin_all, tout_all, cin_all, cout_all, row_readout)
 
 
+def exchange_kernel(n, x_ref, o_ref, recv, send_sems, recv_sems):
+    me = lax.axis_index("mod")
+    stream = lax.axis_index("stream")
+    barrier = pltpu.get_barrier_semaphore()
+    for d in range(1, n):
+        pl.semaphore_signal(
+            barrier, inc=1, device_id=(stream, lax.rem(me + d, n)),
+            device_id_type=pl.DeviceIdType.MESH,
+        )
+    pl.semaphore_wait(barrier, n - 1)
+    copies = []
+    for d in range(1, n):
+        target = lax.rem(me + d, n)
+        copy = pltpu.make_async_remote_copy(
+            src_ref=x_ref.at[target],
+            dst_ref=recv.at[d - 1],
+            send_sem=send_sems.at[d - 1],
+            recv_sem=recv_sems.at[d - 1],
+            device_id=(stream, target),
+            device_id_type=pl.DeviceIdType.MESH,
+        )
+        copy.start()
+        copies.append(copy)
+    for copy in copies:
+        copy.wait()
+    total = x_ref[me]
+    for d in range(n - 1):
+        total = total + recv[d]
+    o_ref[...] = total
+
+
+def exchange_sum(x):
+    n = x.shape[0]
+    return pl.pallas_call(
+        functools.partial(exchange_kernel, n),
+        out_shape=jax.ShapeDtypeStruct(x.shape[1:], x.dtype),
+        in_specs=[pl.BlockSpec(memory_space=pltpu.VMEM)],
+        out_specs=pl.BlockSpec(memory_space=pltpu.VMEM),
+        scratch_shapes=[
+            pltpu.VMEM((n - 1,) + x.shape[1:], x.dtype),
+            pltpu.SemaphoreType.DMA((n - 1,)),
+            pltpu.SemaphoreType.DMA((n - 1,)),
+        ],
+        compiler_params=pltpu.CompilerParams(collective_id=0, has_side_effects=True),
+    )(x)
+
+
 def local(
     pixels,
     stem_weight,
@@ -162,11 +209,14 @@
         ],
         axis=1,
     )
-    received = lax.all_to_all(packed, "mod", split_axis=0, concat_axis=0, tiled=True)
-    totals = jnp.sum(received, axis=0)
+    width = packed.shape[1]
+    lanes = 128
+    padded = -(-width // (8 * lanes)) * 8 * lanes
+    packed = jnp.pad(packed, ((0, 0), (0, padded - width)))
+    totals = exchange_sum(packed.reshape(module_count, -1, lanes)).reshape(-1)
     split = projected_part.size // module_count
     projected = totals[:split].reshape(-1, channels)
-    veto = totals[split:]
+    veto = totals[split:width]
     latent = rms_norm(projected) * latent_gain
     class_scores = jnp.dot(latent, class_weight, precision=lax.Precision.HIGHEST)
     return (veto[None], latent[None], class_scores[None])

time: 159 us -> 160 us (level)
  blocking collectives: 18.2 us -> 0 us
  Pallas kernels: 61.2 us -> 76.5 us
  local copies, waits for them, and re-layouts: 44.8 us -> 46.6 us
    all_to_all x1 -> x0, blocking collectives: 18.2 us -> none  [local(): lax.all_to_all(packed, 'mod', split_axis=0, concat_axis=0, tiled=True)]
    pallas_call x0 -> x1, Pallas kernels: none -> 15.2 us  [exchange_sum(): pl.pallas_call(functools.partial(exchange_kernel, n), out_shape=jax.Shape...]
    unnamed x20 -> x22, local copies, waits for them, and re-layouts: 23.5 us -> 24.7 us
where the time goes in v7:
time: 160 us; the launch traced here: 159 us
  Pallas kernels  76.5 us (48%)
  local copies, waits for them, and re-layouts  46.6 us (29%)
  between operations  14.2 us (9%)
  matrix products  8.67 us (5%)
  other arithmetic  7.64 us (5%)
  waiting for transfers between devices  5.21 us (3%)
    pallas_call x1, Pallas kernels, encode_rows(): pl.pallas_call(encoder_kernel, grid_spec=grid_spec, out_shape=jax.ShapeDt...  61.3 us
    unnamed x22, local copies, waits for them, and re-layouts  24.7 us
    pallas_call x1, Pallas kernels, exchange_sum(): pl.pallas_call(functools.partial(exchange_kernel, n), out_shape=jax.Shape...  15.2 us
    dot_general x1, matrix products, stem_layer(): jnp.einsum('fapbq,pqc->fabc', pixel_tiles, kernel, preferred_element_type...  7.8 us
    convert_element_type x1, local copies, waits for them, and re-layouts, stem_layer(): jax.nn.gelu(response).astype(jnp.bfloat16)  7.55 us
    all_gather x1, waiting for transfers between devices, local(): lax.all_gather(jnp.concatenate([w.reshape(-1) for w in pieces]), 'stream')  5.2 us
    gather x1, local copies, waits for them, and re-layouts, local(): x = jnp.take(features, sorted_frames, axis=0)  3.32 us
  transfers between devices with their start and end apart: 1, of which 1 were waited for; matrix products, arithmetic and copies ran while one was open for 23% of the time, Pallas kernels for 0%

profile of v7, /device:TPU:1, one launch (start us, length us, event | category | flops | bytes accessed | tf_op | source)
XLA Modules:
  0.0 158.8 jit_solution(17589260293994007563)
XLA Ops:
  7.2 0.0 copy-start
  7.2 0.0 all-gather.3.cloned.1.call-start
  7.2 1.0 copy.36
  8.3 0.7 reshape_squeeze.14
  9.0 0.8 copy.31
  9.9 0.2 reshape_squeeze.13
  10.0 1.7 %pad_maximum_fusion = bf16[149504]{0:T(1024)(128)(2,1)} fusion(bf16[65536]{0:T(1024)(128)(2,1)} %bitcast.63, bf16[65536]{0:T(1024)(128)(2,1)S(1)} %bitcast.60, bf16[9216]{0:T(1024)(128)(2,1)S(1)} %reshape_squeeze.14, bf16[9216]{0:T(1024)(128)(2,1)S(1)} %reshape_squeeze.13), kind=kLoop, calls=%fused_computation.18 | loop fusion | flops 1196032 | bytes 598016 | tf_op jit(solution)/shard_map/concatenate | solution.py:166
  11.7 0.0 all-gather.3.cloned.1.call-update
  11.7 0.0 copy-start.4
  11.7 13.0 %copy.29 = bf16[1,768,16,384]{1,3,2,0:T(8,128)(2,1)} copy(bf16[1,768,16,384]{3,2,1,0:T(8,128)(2,1)} %param.12) | data formatting | bytes 18874368 | tf_op args[0]
  24.8 0.7 multiply_bitcast_fusion
  25.4 0.0 copy-done.4
  25.5 7.8 %convert_reduce_fusion = (f32[768,128]{1,0:T(8,128)S(1)}, bf16[768,24,128]{2,0,1:T(8,128)(2,1)}) fusion(bf16[768,16,24,16]{0,3,2,1:T(8,128)(2,1)} %bitcast.53, bf16[16,16,128,1]{2,1,3,0:T(8,128)(2,1)S(1)} %bitcast.73), kind=kOutput, calls=%fused_computation.11 | convolution fusion | flops 1233813504 | bytes 14614528 | tf_op jit(solution)/shard_map/fapbq,pqc->fabc/dot_general | solution.py:22
  33.3 0.2 multiply_reduce_fusion
  33.4 0.1 reshape.138
  33.5 0.0 copy-done.1
  33.5 0.1 convert_reduce_fusion.2
  33.7 0.2 reduce-window.9
  33.8 7.5 %copy.30 = bf16[768,24,128]{2,1,0:T(8,128)(2,1)} copy(bf16[768,24,128]{2,0,1:T(8,128)(2,1)} %get-tuple-element.22) | data formatting | bytes 9437184 | tf_op jit(solution)/shard_map/convert_element_type | solution.py:25
  41.4 0.2 convert_reduce_fusion.1
  41.6 0.1 reduce_sum.70
  41.7 0.7 select_reduce_fusion
  42.4 3.3 %gather_fusion = bf16[192,24,128]{2,1,0:T(8,128)(2,1)S(1)} fusion(bf16[768,24,128]{2,1,0:T(8,128)(2,1)} %copy.30, s32[1024]{0:T(1024)S(1)} %pad_clamp_fusion.1), kind=kCustom, calls=%fused_computation | custom fusion | bytes 2360064 | tf_op jit(solution)/shard_map/jit(_take)/gather | solution.py:191
  45.8 0.6 constant_dynamic-slice_fusion.ro_ref
  46.4 0.5 multiply_bitcast_fusion.1.gend_ref
  46.9 0.5 multiply_subtract_fusion.gstart_ref
  47.5 1.3 broadcast_select_fusion.x_ref
  48.7 5.2 %all-gather.3.cloned.1.call-done = bf16[1196032]{0:T(1024)(128)(2,1)} async-done(((bf16[149504]{0:T(1024)(128)(2,1)}), bf16[1196032]{0:T(1024)(128)(2,1)}) %all-gather.3.cloned.1.call-update) | async-done | bytes 2392080 | tf_op jit(solution)/shard_map/all_gather | solution.py:166
  53.9 2.7 %reshape.157 = bf16[8,149504]{1,0:T(8,128)(2,1)S(1)} reshape(bf16[1196032]{0:T(1024)(128)(2,1)} %all-gather.3.cloned.1.call-done) | data formatting | bytes 4784128 | tf_op jit(solution)/shard_map/all_gather | solution.py:166
  56.6 0.0 copy-start.3
  56.6 0.0 copy-start.5
  56.6 0.7 fusion.14
  57.4 1.4 slice_bitcast_fusion
  58.8 3.0 %reshape.134.tin_ref = bf16[8,384,24]{2,1,0:T(8,128)(2,1)} reshape(bf16[8,9216]{1,0:T(8,128)(2,1)} %get-tuple-element.20) | data formatting | bytes 294912 | tf_op jit(solution)/shard_map/reshape | solution.py:169
  61.8 1.6 copy.47
  63.4 2.6 %copy.46 = bf16[1,8,128,512]{3,2,1,0:T(8,128)(2,1)} copy(bf16[1,8,128,512]{3,1,2,0:T(8,128)(2,1)} %bitcast.56) | data formatting | bytes 2097152
  66.0 2.3 %copy.45 = bf16[1,8,512,128]{3,2,1,0:T(8,128)(2,1)} copy(bf16[1,8,512,128]{3,1,2,0:T(8,128)(2,1)} %get-tuple-element.17) | data formatting | bytes 2097152
  68.3 61.3 %shard_map.139 = f32[192,128]{1,0:T(8,128)} custom-call(s32[192]{0:T(256)} %get-tuple-element.16.tgt_ref, s32[8]{0:T(128)} %multiply_subtract_fusion.gstart_ref, s32[8]{0:T(128)} %multiply_bitcast_fusion.1.gend_ref, bf16[192,24,128]{2,1,0:T(8,128)(2,1)} %broadcast_select_fusion.x_ref, bf16[8,384,24]{2,1,0:T(8,128)(2,1)} %reshape.134.tin_ref, ...), custom_call_target="tpu_custom_call" | custom-call | tf_op jit(solution)/shard_map/pallas_call | solution.py:91
  129.6 1.6 gather_fusion.1
  131.2 0.1 broadcast_in_dim.56
  131.4 0.7 copy.40
  132.0 15.2 %shard_map.140 = f32[8,128]{1,0:T(8,128)} custom-call(f32[32,8,128]{2,1,0:T(8,128)} %bitcast.59), custom_call_target="tpu_custom_call" | custom-call | tf_op jit(solution)/shard_map/pallas_call | solution.py:132
  147.2 0.8 multiply_reduce_fusion.1
  148.0 1.2 slice_bitcast_fusion.1
  149.2 0.7 fusion.11
  149.9 0.6 copy.32
  150.5 0.9 convolution_bitcast_fusion
  151.4 0.6 copy.33
  (16 shorter events, 0.1 us)
Async XLA Ops:
  7.2 38.6 %copy-start = (bf16[4096,128]{1,0:T(8,128)(2,1)S(1)}, bf16[4096,128]{1,0:T(8,128)(2,1)}, u32[]{:S(2)}) copy-start(bf16[4096,128]{1,0:T(8,128)(2,1)} %param.21) | copy-start | bytes 3145732
  7.2 46.8 %all-gather.3.cloned.1.call-start = ((), (), s32[]{:S(2)}) async-start(), calls=%async_computation | async-start | bytes 2691072 | tf_op jit(solution)/shard_map/all_gather | solution.py:166
  11.7 13.7 %copy-start.4 = (bf16[256,128]{1,0:T(8,128)(2,1)S(1)}, bf16[256,128]{1,0:T(8,128)(2,1)}, u32[]{:S(2)}) copy-start(bf16[256,128]{1,0:T(8,128)(2,1)} %param.13) | copy-start | bytes 196612
  25.5 8.1 %copy-start.1 = (s32[1,192,1]{1,2,0:T(1,128)S(1)}, s32[1,192,1]{1,2,0:T(1,128)}, u32[]{:S(2)}) copy-start(s32[1,192,1]{1,2,0:T(1,128)} %param.16) | copy-start | bytes 2308
  33.3 8.4 %copy-start.2 = (s32[1,192]{1,0:T(1,128)S(1)}, s32[1,192]{1,0:T(1,128)}, u32[]{:S(2)}) copy-start(s32[1,192]{1,0:T(1,128)} %param.15) | copy-start | bytes 2308
  56.6 92.6 %copy-start.3 = (f32[128]{0:T(128)S(1)}, f32[128]{0:T(128)}, u32[]{:S(2)}) copy-start(f32[128]{0:T(128)} %param.22) | copy-start | bytes 1540
  56.6 93.9 %copy-start.5 = (f32[128,8]{0,1:T(8,128)S(1)}, f32[128,8]{0,1:T(8,128)}, u32[]{:S(2)}) copy-start(f32[128,8]{0,1:T(8,128)} %param.23) | copy-start | bytes 12292
Sparse Core Ops, SparseCore 0:
  11.8 42.0 all-gather.2

commit v8 on v7

--- a/solution.py
+++ b/solution.py
@@ -163,11 +163,18 @@
     mod_index = lax.axis_index("mod")
 
     pieces = (token_in[0], token_out[0], chan_in[0], chan_out[0])
-    gathered = lax.all_gather(jnp.concatenate([w.reshape(-1) for w in pieces]), "stream")
-    weights, offset = [], 0
+    lanes, align = 128, 16
+    blocks, spans, start = [], [], 0
     for w in pieces:
-        weights.append(gathered[:, offset:offset + w.size].reshape((stream_count,) + w.shape))
-        offset += w.size
+        rows = -(-(-(-w.size // lanes)) // align) * align
+        blocks.append(jnp.pad(w.reshape(-1), (0, rows * lanes - w.size)).reshape(rows, lanes))
+        spans.append((start, rows))
+        start += rows
+    gathered = lax.all_gather(jnp.concatenate(blocks, axis=0), "stream")
+    weights = []
+    for w, (first_row, rows) in zip(pieces, spans):
+        part = gathered[:, first_row:first_row + rows, :].reshape(stream_count, -1)
+        weights.append(part[:, :w.size].reshape((stream_count,) + w.shape))
     tin_all, tout_all, cin_all, cout_all = weights
 
     features = stem_layer(pixels[0], stem_weight)

time: 160 us -> 154 us (0.963)
  local copies, waits for them, and re-layouts: 46.6 us -> 40.4 us
    unnamed x22 -> x21, local copies, waits for them, and re-layouts: 24.7 us -> 17.5 us
    all_gather x1 -> x0, local copies, waits for them, and re-layouts: 2.68 us -> none  [local(): lax.all_gather(jnp.concatenate([w.reshape(-1) for w in pieces]), 'stream')]
    slice x1 -> x3, local copies, waits for them, and re-layouts: 0.74 us -> 2.79 us  [the longest x1 2.76 us: local(): part = gathered[:, first_row:first_row + rows, :].reshape(stream_count, -1)]
    reshape x1 -> x3, local copies, waits for them, and re-layouts: 3.01 us -> 3.22 us  [the longest x1 2.14 us: local(): weights.append(part[:, :w.size].reshape((stream_count,) + w.shape))]
  transfers between devices with their start and end apart: 1 -> 1, of which waited for: 1 -> 1; matrix products, arithmetic and copies ran while one was open for 23% -> 24% of each run, Pallas kernels for 0% -> 0%
where the time goes in v8:
time: 154 us; the launch traced here: 153 us
  Pallas kernels  76.9 us (50%)
  local copies, waits for them, and re-layouts  40.4 us (26%)
  between operations  14.2 us (9%)
  matrix products  8.67 us (6%)
  other arithmetic  7.64 us (5%)
  waiting for transfers between devices  5.55 us (4%)
    pallas_call x1, Pallas kernels, encode_rows(): pl.pallas_call(encoder_kernel, grid_spec=grid_spec, out_shape=jax.ShapeDt...  61.8 us
    unnamed x21, local copies, waits for them, and re-layouts  17.5 us
    pallas_call x1, Pallas kernels, exchange_sum(): pl.pallas_call(functools.partial(exchange_kernel, n), out_shape=jax.Shape...  15.1 us
    dot_general x1, matrix products, stem_layer(): jnp.einsum('fapbq,pqc->fabc', pixel_tiles, kernel, preferred_element_type...  7.81 us
    convert_element_type x1, local copies, waits for them, and re-layouts, stem_layer(): jax.nn.gelu(response).astype(jnp.bfloat16)  7.55 us
    all_gather x1, waiting for transfers between devices, local(): gathered = lax.all_gather(jnp.concatenate(blocks, axis=0), 'stream')  5.53 us
    gather x1, local copies, waits for them, and re-layouts, local(): x = jnp.take(features, sorted_frames, axis=0)  3.32 us
  transfers between devices with their start and end apart: 1, of which 1 were waited for; matrix products, arithmetic and copies ran while one was open for 24% of the time, Pallas kernels for 0%

profile of v8, /device:TPU:1, one launch (start us, length us, event | category | flops | bytes accessed | tf_op | source)
XLA Modules:
  0.0 153.5 jit_solution(3710132264591257426)
XLA Ops:
  7.2 0.0 copy-start
  7.2 0.0 all-gather.3.cloned.1.call-start
  7.2 1.1 reshape.150
  8.3 0.7 reshape_squeeze.10
  9.0 0.8 copy.26
  9.9 0.2 reshape_squeeze.4
  10.1 1.7 %pad_maximum_fusion = bf16[1184,128]{1,0:T(8,128)(2,1)} fusion(bf16[512,128]{1,0:T(8,128)(2,1)} %bitcast.65, bf16[512,128]{1,0:T(8,128)(2,1)S(1)} %reshape.150, bf16[80,128]{1,0:T(8,128)(2,1)S(1)} %get-tuple-element.20, bf16[80,128]{1,0:T(8,128)(2,1)S(1)} %get-tuple-element.21), kind=kLoop, calls=%fused_computation.15 | loop fusion | flops 1212416 | bytes 606208 | tf_op jit(solution)/shard_map/concatenate | solution.py:173
  11.7 0.0 all-gather.3.cloned.1.call-update
  11.8 0.0 copy-start.4
  11.8 13.0 %copy.24 = bf16[1,768,16,384]{1,3,2,0:T(8,128)(2,1)} copy(bf16[1,768,16,384]{3,2,1,0:T(8,128)(2,1)} %param.12) | data formatting | bytes 18874368 | tf_op args[0]
  24.8 0.7 multiply_bitcast_fusion
  25.5 0.0 copy-done.4
  25.5 7.8 %convert_reduce_fusion = (f32[768,128]{1,0:T(8,128)S(1)}, bf16[768,24,128]{2,0,1:T(8,128)(2,1)}) fusion(bf16[768,16,24,16]{0,3,2,1:T(8,128)(2,1)} %bitcast.57, bf16[16,16,128,1]{2,1,3,0:T(8,128)(2,1)S(1)} %bitcast.76), kind=kOutput, calls=%fused_computation.11 | convolution fusion | flops 1233813504 | bytes 14614528 | tf_op jit(solution)/shard_map/fapbq,pqc->fabc/dot_general | solution.py:22
  33.3 0.2 multiply_reduce_fusion
  33.5 0.1 reshape.156
  33.6 0.0 copy-done.1
  33.6 0.1 convert_reduce_fusion.2
  33.7 0.2 reduce-window.9
  33.9 7.6 %copy.25 = bf16[768,24,128]{2,1,0:T(8,128)(2,1)} copy(bf16[768,24,128]{2,0,1:T(8,128)(2,1)} %get-tuple-element.19) | data formatting | bytes 9437184 | tf_op jit(solution)/shard_map/convert_element_type | solution.py:25
  41.4 0.2 convert_reduce_fusion.1
  41.6 0.1 reduce_sum.70
  41.7 0.0 copy-done.2
  41.8 0.7 select_reduce_fusion
  42.5 3.3 %gather_fusion = bf16[192,24,128]{2,1,0:T(8,128)(2,1)S(1)} fusion(bf16[768,24,128]{2,1,0:T(8,128)(2,1)} %copy.25, s32[1024]{0:T(1024)S(1)} %pad_clamp_fusion.1), kind=kCustom, calls=%fused_computation | custom fusion | bytes 2360064 | tf_op jit(solution)/shard_map/jit(_take)/gather | solution.py:198
  45.8 0.0 copy-start.3
  45.8 0.0 copy-start.5
  45.9 0.0 copy-done
  45.9 0.6 constant_dynamic-slice_fusion.ro_ref
  46.5 0.5 multiply_bitcast_fusion.1.gend_ref
  47.0 0.5 multiply_subtract_fusion.gstart_ref
  47.5 1.3 broadcast_select_fusion.x_ref
  48.8 5.5 %all-gather.3.cloned.1.call-done = bf16[9472,128]{1,0:T(8,128)(2,1)} async-done(((bf16[1184,128]{1,0:T(8,128)(2,1)}), bf16[9472,128]{1,0:T(8,128)(2,1)}) %all-gather.3.cloned.1.call-update) | async-done | bytes 2424848 | tf_op jit(solution)/shard_map/all_gather | solution.py:173
  54.4 1.0 slice_bitcast_fusion
  55.4 2.8 %fusion.14 = (bf16[8,512,128]{2,1,0:T(8,128)(2,1)}, bf16[8,512,128]{2,1,0:T(8,128)(2,1)S(1)}) fusion(bf16[8,1184,128]{2,1,0:T(8,128)(2,1)} %bitcast.59), kind=kLoop, calls=%fused_computation.55 | loop fusion | bytes 4194304 | tf_op jit(solution)/shard_map/slice | solution.py:176
  58.2 2.1 %reshape.153.tin_ref = bf16[8,384,24]{2,1,0:T(8,128)(2,1)} reshape(bf16[8,9216]{1,0:T(8,128)(2,1)S(1)} %slice.38) | data formatting | bytes 294912 | tf_op jit(solution)/shard_map/reshape | solution.py:177
  60.4 0.7 copy.41
  61.1 1.4 reshape_reshape.3.cin_ref
  62.5 61.8 %shard_map.139 = f32[192,128]{1,0:T(8,128)} custom-call(s32[192]{0:T(256)} %get-tuple-element.13.tgt_ref, s32[8]{0:T(128)} %multiply_subtract_fusion.gstart_ref, s32[8]{0:T(128)} %multiply_bitcast_fusion.1.gend_ref, bf16[192,24,128]{2,1,0:T(8,128)(2,1)} %broadcast_select_fusion.x_ref, bf16[8,384,24]{2,1,0:T(8,128)(2,1)} %reshape.153.tin_ref, ...), custom_call_target="tpu_custom_call" | custom-call | tf_op jit(solution)/shard_map/pallas_call | solution.py:91
  124.3 1.6 %gather_fusion.1 = f32[192,128]{1,0:T(8,128)S(1)} fusion(f32[192,128]{1,0:T(8,128)} %shard_map.139, s32[1024]{0:T(1024)S(1)} %pad_clamp_fusion), kind=kCustom, calls=%fused_computation.1 | custom fusion | bytes 197376 | tf_op jit(solution)/shard_map/jit(_take)/gather | solution.py:210
  125.9 0.1 broadcast_in_dim.56
  126.1 0.7 copy.34
  126.8 15.1 %shard_map.140 = f32[8,128]{1,0:T(8,128)} custom-call(f32[32,8,128]{2,1,0:T(8,128)} %bitcast.64), custom_call_target="tpu_custom_call" | custom-call | tf_op jit(solution)/shard_map/pallas_call | solution.py:132
  141.9 0.8 multiply_reduce_fusion.1
  142.7 1.2 slice_bitcast_fusion.2
  143.9 0.7 fusion.11
  144.6 0.6 copy.27
  145.2 0.9 convolution_bitcast_fusion
  146.1 0.6 copy.28
  (19 shorter events, 0.2 us)
Async XLA Ops:
  7.2 38.7 %copy-start = (bf16[4096,128]{1,0:T(8,128)(2,1)S(1)}, bf16[4096,128]{1,0:T(8,128)(2,1)}, u32[]{:S(2)}) copy-start(bf16[4096,128]{1,0:T(8,128)(2,1)} %param.21) | copy-start | bytes 3145732
  7.2 47.2 %all-gather.3.cloned.1.call-start = ((), (), s32[]{:S(2)}) async-start(), calls=%async_computation | async-start | bytes 2727936 | tf_op jit(solution)/shard_map/all_gather | solution.py:173
  11.8 13.7 %copy-start.4 = (bf16[256,128]{1,0:T(8,128)(2,1)S(1)}, bf16[256,128]{1,0:T(8,128)(2,1)}, u32[]{:S(2)}) copy-start(bf16[256,128]{1,0:T(8,128)(2,1)} %param.13) | copy-start | bytes 196612
  25.5 8.1 %copy-start.1 = (s32[1,192,1]{1,2,0:T(1,128)S(1)}, s32[1,192,1]{1,2,0:T(1,128)}, u32[]{:S(2)}) copy-start(s32[1,192,1]{1,2,0:T(1,128)} %param.16) | copy-start | bytes 2308
  33.3 8.4 %copy-start.2 = (s32[1,192]{1,0:T(1,128)S(1)}, s32[1,192]{1,0:T(1,128)}, u32[]{:S(2)}) copy-start(s32[1,192]{1,0:T(1,128)} %param.15) | copy-start | bytes 2308
  45.8 98.0 %copy-start.3 = (f32[128]{0:T(128)S(1)}, f32[128]{0:T(128)}, u32[]{:S(2)}) copy-start(f32[128]{0:T(128)} %param.22) | copy-start | bytes 1540
  45.8 99.4 %copy-start.5 = (f32[128,8]{0,1:T(8,128)S(1)}, f32[128,8]{0,1:T(8,128)}, u32[]{:S(2)}) copy-start(f32[128,8]{0,1:T(8,128)} %param.23) | copy-start | bytes 12292
Sparse Core Ops, SparseCore 0:
  11.9 42.4 all-gather.2

commit v9 on v8

--- a/solution.py
+++ b/solution.py
@@ -48,15 +48,26 @@
     token = base * row_len + lax.broadcasted_iota(jnp.int32, (hits * row_len, 1), 0)
     first = tgt_ref[base]
     last = tgt_ref[base + hits - 1]
+    head = token < gend_ref[first]
+    hid_scr[...] = jnp.where(
+        head,
+        jnp.dot(normed_two, cin_ref[first], preferred_element_type=f32),
+        jnp.dot(normed_two, cin_ref[last], preferred_element_type=f32),
+    )
     for g in range(groups):
-        @pl.when((g >= first) & (g <= last))
+        @pl.when((g > first) & (g < last))
         def _():
             inside = (token >= gstart_ref[g]) & (token < gend_ref[g])
             part = jnp.dot(normed_two, cin_ref[g], preferred_element_type=f32)
             hid_scr[...] = jnp.where(inside, part, hid_scr[...])
     hidden = jax.nn.gelu(hid_scr[...]).astype(bf16)
+    out_scr[...] = jnp.where(
+        head,
+        jnp.dot(hidden, cout_ref[first], preferred_element_type=f32),
+        jnp.dot(hidden, cout_ref[last], preferred_element_type=f32),
+    )
     for g in range(groups):
-        @pl.when((g >= first) & (g <= last))
+        @pl.when((g > first) & (g < last))
         def _():
             inside = (token >= gstart_ref[g]) & (token < gend_ref[g])
             part = jnp.dot(hidden, cout_ref[g], preferred_element_type=f32)

time: 154 us -> 148 us (0.961)
  Pallas kernels: 76.9 us -> 70.3 us
    pallas_call x1, Pallas kernels: 61.8 us -> 55.2 us  [encode_rows(): pl.pallas_call(encoder_kernel, grid_spec=grid_spec, out_shape=jax.ShapeDt...]
  transfers between devices with their start and end apart: 1 -> 1, of which waited for: 1 -> 1; matrix products, arithmetic and copies ran while one was open for 24% -> 25% of each run, Pallas kernels for 0% -> 0%
where the time goes in v9:
time: 148 us; the launch traced here: 147 us
  Pallas kernels  70.3 us (48%)
  local copies, waits for them, and re-layouts  40.4 us (27%)
  between operations  14.2 us (10%)
  matrix products  8.67 us (6%)
  other arithmetic  7.64 us (5%)
  waiting for transfers between devices  5.55 us (4%)
    pallas_call x1, Pallas kernels, encode_rows(): pl.pallas_call(encoder_kernel, grid_spec=grid_spec, out_shape=jax.ShapeDt...  55.2 us
    unnamed x21, local copies, waits for them, and re-layouts  17.5 us
    pallas_call x1, Pallas kernels, exchange_sum(): pl.pallas_call(functools.partial(exchange_kernel, n), out_shape=jax.Shape...  15.1 us
    dot_general x1, matrix products, stem_layer(): jnp.einsum('fapbq,pqc->fabc', pixel_tiles, kernel, preferred_element_type...  7.81 us
    convert_element_type x1, local copies, waits for them, and re-layouts, stem_layer(): jax.nn.gelu(response).astype(jnp.bfloat16)  7.55 us
    all_gather x1, waiting for transfers between devices, local(): gathered = lax.all_gather(jnp.concatenate(blocks, axis=0), 'stream')  5.53 us
    gather x1, local copies, waits for them, and re-layouts, local(): x = jnp.take(features, sorted_frames, axis=0)  3.32 us
  transfers between devices with their start and end apart: 1, of which 1 were waited for; matrix products, arithmetic and copies ran while one was open for 25% of the time, Pallas kernels for 0%

profile of v9, /device:TPU:1, one launch (start us, length us, event | category | flops | bytes accessed | tf_op | source)
XLA Modules:
  0.0 146.8 jit_solution(10021815673874762778)
XLA Ops:
  7.2 0.0 copy-start
  7.2 0.0 all-gather.3.cloned.1.call-start
  7.2 1.1 reshape.150
  8.3 0.7 reshape_squeeze.10
  9.0 0.8 copy.26
  9.9 0.2 reshape_squeeze.4
  10.1 1.7 %pad_maximum_fusion = bf16[1184,128]{1,0:T(8,128)(2,1)} fusion(bf16[512,128]{1,0:T(8,128)(2,1)} %bitcast.65, bf16[512,128]{1,0:T(8,128)(2,1)S(1)} %reshape.150, bf16[80,128]{1,0:T(8,128)(2,1)S(1)} %get-tuple-element.20, bf16[80,128]{1,0:T(8,128)(2,1)S(1)} %get-tuple-element.21), kind=kLoop, calls=%fused_computation.15 | loop fusion | flops 1212416 | bytes 606208 | tf_op jit(solution)/shard_map/concatenate | solution.py:184
  11.7 0.0 all-gather.3.cloned.1.call-update
  11.8 0.0 copy-start.4
  11.8 13.0 %copy.24 = bf16[1,768,16,384]{1,3,2,0:T(8,128)(2,1)} copy(bf16[1,768,16,384]{3,2,1,0:T(8,128)(2,1)} %param.12) | data formatting | bytes 18874368 | tf_op args[0]
  24.8 0.7 multiply_bitcast_fusion
  25.5 0.0 copy-done.4
  25.5 7.8 %convert_reduce_fusion = (f32[768,128]{1,0:T(8,128)S(1)}, bf16[768,24,128]{2,0,1:T(8,128)(2,1)}) fusion(bf16[768,16,24,16]{0,3,2,1:T(8,128)(2,1)} %bitcast.57, bf16[16,16,128,1]{2,1,3,0:T(8,128)(2,1)S(1)} %bitcast.76), kind=kOutput, calls=%fused_computation.11 | convolution fusion | flops 1233813504 | bytes 14614528 | tf_op jit(solution)/shard_map/fapbq,pqc->fabc/dot_general | solution.py:22
  33.3 0.2 multiply_reduce_fusion
  33.5 0.1 reshape.156
  33.6 0.0 copy-done.1
  33.6 0.1 convert_reduce_fusion.2
  33.7 0.2 reduce-window.9
  33.9 7.6 %copy.25 = bf16[768,24,128]{2,1,0:T(8,128)(2,1)} copy(bf16[768,24,128]{2,0,1:T(8,128)(2,1)} %get-tuple-element.19) | data formatting | bytes 9437184 | tf_op jit(solution)/shard_map/convert_element_type | solution.py:25
  41.4 0.2 convert_reduce_fusion.1
  41.6 0.1 reduce_sum.70
  41.7 0.0 copy-done.2
  41.8 0.7 select_reduce_fusion
  42.5 3.3 %gather_fusion = bf16[192,24,128]{2,1,0:T(8,128)(2,1)S(1)} fusion(bf16[768,24,128]{2,1,0:T(8,128)(2,1)} %copy.25, s32[1024]{0:T(1024)S(1)} %pad_clamp_fusion.1), kind=kCustom, calls=%fused_computation | custom fusion | bytes 2360064 | tf_op jit(solution)/shard_map/jit(_take)/gather | solution.py:209
  45.8 0.0 copy-start.3
  45.8 0.0 copy-start.5
  45.9 0.0 copy-done
  45.9 0.6 constant_dynamic-slice_fusion.ro_ref
  46.5 0.5 multiply_bitcast_fusion.1.gend_ref
  47.0 0.5 multiply_subtract_fusion.gstart_ref
  47.5 1.3 broadcast_select_fusion.x_ref
  48.8 5.5 %all-gather.3.cloned.1.call-done = bf16[9472,128]{1,0:T(8,128)(2,1)} async-done(((bf16[1184,128]{1,0:T(8,128)(2,1)}), bf16[9472,128]{1,0:T(8,128)(2,1)}) %all-gather.3.cloned.1.call-update) | async-done | bytes 2424848 | tf_op jit(solution)/shard_map/all_gather | solution.py:184
  54.4 1.0 slice_bitcast_fusion
  55.4 2.8 %fusion.14 = (bf16[8,512,128]{2,1,0:T(8,128)(2,1)}, bf16[8,512,128]{2,1,0:T(8,128)(2,1)S(1)}) fusion(bf16[8,1184,128]{2,1,0:T(8,128)(2,1)} %bitcast.59), kind=kLoop, calls=%fused_computation.55 | loop fusion | bytes 4194304 | tf_op jit(solution)/shard_map/slice | solution.py:187
  58.2 2.1 %reshape.153.tin_ref = bf16[8,384,24]{2,1,0:T(8,128)(2,1)} reshape(bf16[8,9216]{1,0:T(8,128)(2,1)S(1)} %slice.38) | data formatting | bytes 294912 | tf_op jit(solution)/shard_map/reshape | solution.py:188
  60.4 0.7 copy.41
  61.1 1.4 reshape_reshape.3.cin_ref
  62.5 55.2 %shard_map.139 = f32[192,128]{1,0:T(8,128)} custom-call(s32[192]{0:T(256)} %get-tuple-element.13.tgt_ref, s32[8]{0:T(128)} %multiply_subtract_fusion.gstart_ref, s32[8]{0:T(128)} %multiply_bitcast_fusion.1.gend_ref, bf16[192,24,128]{2,1,0:T(8,128)(2,1)} %broadcast_select_fusion.x_ref, bf16[8,384,24]{2,1,0:T(8,128)(2,1)} %reshape.153.tin_ref, ...), custom_call_target="tpu_custom_call" | custom-call | tf_op jit(solution)/shard_map/pallas_call | solution.py:102
  117.7 1.6 %gather_fusion.1 = f32[192,128]{1,0:T(8,128)S(1)} fusion(f32[192,128]{1,0:T(8,128)} %shard_map.139, s32[1024]{0:T(1024)S(1)} %pad_clamp_fusion), kind=kCustom, calls=%fused_computation.1 | custom fusion | bytes 197376 | tf_op jit(solution)/shard_map/jit(_take)/gather | solution.py:221
  119.3 0.1 broadcast_in_dim.56
  119.4 0.7 copy.34
  120.1 15.1 %shard_map.140 = f32[8,128]{1,0:T(8,128)} custom-call(f32[32,8,128]{2,1,0:T(8,128)} %bitcast.64), custom_call_target="tpu_custom_call" | custom-call | tf_op jit(solution)/shard_map/pallas_call | solution.py:143
  135.2 0.8 multiply_reduce_fusion.1
  136.0 1.2 slice_bitcast_fusion.2
  137.2 0.7 fusion.11
  137.9 0.6 copy.27
  138.5 0.9 convolution_bitcast_fusion
  139.4 0.6 copy.28
  (19 shorter events, 0.2 us)
Async XLA Ops:
  7.2 38.7 %copy-start = (bf16[4096,128]{1,0:T(8,128)(2,1)S(1)}, bf16[4096,128]{1,0:T(8,128)(2,1)}, u32[]{:S(2)}) copy-start(bf16[4096,128]{1,0:T(8,128)(2,1)} %param.21) | copy-start | bytes 3145732
  7.2 47.2 %all-gather.3.cloned.1.call-start = ((), (), s32[]{:S(2)}) async-start(), calls=%async_computation | async-start | bytes 2727936 | tf_op jit(solution)/shard_map/all_gather | solution.py:184
  11.8 13.7 %copy-start.4 = (bf16[256,128]{1,0:T(8,128)(2,1)S(1)}, bf16[256,128]{1,0:T(8,128)(2,1)}, u32[]{:S(2)}) copy-start(bf16[256,128]{1,0:T(8,128)(2,1)} %param.13) | copy-start | bytes 196612
  25.5 8.1 %copy-start.1 = (s32[1,192,1]{1,2,0:T(1,128)S(1)}, s32[1,192,1]{1,2,0:T(1,128)}, u32[]{:S(2)}) copy-start(s32[1,192,1]{1,2,0:T(1,128)} %param.16) | copy-start | bytes 2308
  33.3 8.4 %copy-start.2 = (s32[1,192]{1,0:T(1,128)S(1)}, s32[1,192]{1,0:T(1,128)}, u32[]{:S(2)}) copy-start(s32[1,192]{1,0:T(1,128)} %param.15) | copy-start | bytes 2308
  45.8 91.4 %copy-start.3 = (f32[128]{0:T(128)S(1)}, f32[128]{0:T(128)}, u32[]{:S(2)}) copy-start(f32[128]{0:T(128)} %param.22) | copy-start | bytes 1540
  45.8 92.7 %copy-start.5 = (f32[128,8]{0,1:T(8,128)S(1)}, f32[128,8]{0,1:T(8,128)}, u32[]{:S(2)}) copy-start(f32[128,8]{0,1:T(8,128)} %param.23) | copy-start | bytes 12292
Sparse Core Ops, SparseCore 0:
  11.9 42.4 all-gather.2

commit v10 on v9

--- a/solution.py
+++ b/solution.py
@@ -23,6 +23,13 @@
         "fapbq,pqc->fabc", pixel_tiles, kernel, preferred_element_type=jnp.float32
     )
     return jax.nn.gelu(response).astype(jnp.bfloat16).reshape(count, -1, kernel.shape[-1])
+
+
+def gelu_tanh(x):
+    k = 0.7978845608028654
+    inner = x * (k + (k * 0.044715) * (x * x))
+    half = 0.5 * x
+    return half + half * jnp.tanh(inner)
 
 
 def encoder_kernel(
@@ -40,7 +47,7 @@
         xh = x_ref[h].astype(f32)
         normed = rms_norm(xh).astype(bf16)
         pre = jnp.dot(tin_ref[t], normed, preferred_element_type=f32)
-        mixed = jax.nn.gelu(pre).astype(bf16)
+        mixed = gelu_tanh(pre.astype(bf16)).astype(bf16)
         mix = jnp.dot(tout_ref[t], mixed, preferred_element_type=f32)
         mix_scr[h * row_len:(h + 1) * row_len, :] = (xh + mix).astype(bf16).astype(f32)
     after_mix = mix_scr[...]

time: 148 us -> 146 us (0.986)
  Pallas kernels: 70.3 us -> 68.2 us
    pallas_call x1, Pallas kernels: 55.2 us -> 53.1 us  [encode_rows(): pl.pallas_call(encoder_kernel, grid_spec=grid_spec, out_shape=jax.ShapeDt...]
  transfers between devices with their start and end apart: 1 -> 1, of which waited for: 1 -> 1; matrix products, arithmetic and copies ran while one was open for 25% -> 26% of each run, Pallas kernels for 0% -> 0%
where the time goes in v10:
time: 146 us; the launch traced here: 145 us
  Pallas kernels  68.2 us (47%)
  local copies, waits for them, and re-layouts  40.4 us (28%)
  between operations  14.2 us (10%)
  matrix products  8.67 us (6%)
  other arithmetic  7.64 us (5%)
  waiting for transfers between devices  5.55 us (4%)
    pallas_call x1, Pallas kernels, encode_rows(): pl.pallas_call(encoder_kernel, grid_spec=grid_spec, out_shape=jax.ShapeDt...  53.1 us
    unnamed x21, local copies, waits for them, and re-layouts  17.5 us
    pallas_call x1, Pallas kernels, exchange_sum(): pl.pallas_call(functools.partial(exchange_kernel, n), out_shape=jax.Shape...  15.1 us
    dot_general x1, matrix products, stem_layer(): jnp.einsum('fapbq,pqc->fabc', pixel_tiles, kernel, preferred_element_type...  7.81 us
    convert_element_type x1, local copies, waits for them, and re-layouts, stem_layer(): jax.nn.gelu(response).astype(jnp.bfloat16)  7.55 us
    all_gather x1, waiting for transfers between devices, local(): gathered = lax.all_gather(jnp.concatenate(blocks, axis=0), 'stream')  5.53 us
    gather x1, local copies, waits for them, and re-layouts, local(): x = jnp.take(features, sorted_frames, axis=0)  3.32 us
  transfers between devices with their start and end apart: 1, of which 1 were waited for; matrix products, arithmetic and copies ran while one was open for 26% of the time, Pallas kernels for 0%

profile of v10, /device:TPU:1, one launch (start us, length us, event | category | flops | bytes accessed | tf_op | source)
XLA Modules:
  0.0 144.8 jit_solution(6475137822688658430)
XLA Ops:
  7.2 0.0 copy-start
  7.2 0.0 all-gather.3.cloned.1.call-start
  7.2 1.1 reshape.150
  8.3 0.7 reshape_squeeze.10
  9.0 0.8 copy.26
  9.9 0.2 reshape_squeeze.4
  10.1 1.7 %pad_maximum_fusion = bf16[1184,128]{1,0:T(8,128)(2,1)} fusion(bf16[512,128]{1,0:T(8,128)(2,1)} %bitcast.65, bf16[512,128]{1,0:T(8,128)(2,1)S(1)} %reshape.150, bf16[80,128]{1,0:T(8,128)(2,1)S(1)} %get-tuple-element.20, bf16[80,128]{1,0:T(8,128)(2,1)S(1)} %get-tuple-element.21), kind=kLoop, calls=%fused_computation.15 | loop fusion | flops 1212416 | bytes 606208 | tf_op jit(solution)/shard_map/concatenate | solution.py:191
  11.7 0.0 all-gather.3.cloned.1.call-update
  11.8 0.0 copy-start.4
  11.8 13.0 %copy.24 = bf16[1,768,16,384]{1,3,2,0:T(8,128)(2,1)} copy(bf16[1,768,16,384]{3,2,1,0:T(8,128)(2,1)} %param.12) | data formatting | bytes 18874368 | tf_op args[0]
  24.8 0.7 multiply_bitcast_fusion
  25.5 0.0 copy-done.4
  25.5 7.8 %convert_reduce_fusion = (f32[768,128]{1,0:T(8,128)S(1)}, bf16[768,24,128]{2,0,1:T(8,128)(2,1)}) fusion(bf16[768,16,24,16]{0,3,2,1:T(8,128)(2,1)} %bitcast.57, bf16[16,16,128,1]{2,1,3,0:T(8,128)(2,1)S(1)} %bitcast.76), kind=kOutput, calls=%fused_computation.11 | convolution fusion | flops 1233813504 | bytes 14614528 | tf_op jit(solution)/shard_map/fapbq,pqc->fabc/dot_general | solution.py:22
  33.3 0.2 multiply_reduce_fusion
  33.5 0.1 reshape.156
  33.6 0.0 copy-done.1
  33.6 0.1 convert_reduce_fusion.2
  33.7 0.2 reduce-window.9
  33.9 7.6 %copy.25 = bf16[768,24,128]{2,1,0:T(8,128)(2,1)} copy(bf16[768,24,128]{2,0,1:T(8,128)(2,1)} %get-tuple-element.19) | data formatting | bytes 9437184 | tf_op jit(solution)/shard_map/convert_element_type | solution.py:25
  41.4 0.2 convert_reduce_fusion.1
  41.6 0.1 reduce_sum.70
  41.8 0.7 select_reduce_fusion
  42.5 3.3 %gather_fusion = bf16[192,24,128]{2,1,0:T(8,128)(2,1)S(1)} fusion(bf16[768,24,128]{2,1,0:T(8,128)(2,1)} %copy.25, s32[1024]{0:T(1024)S(1)} %pad_clamp_fusion.1), kind=kCustom, calls=%fused_computation | custom fusion | bytes 2360064 | tf_op jit(solution)/shard_map/jit(_take)/gather | solution.py:216
  45.8 0.0 copy-start.3
  45.8 0.0 copy-start.5
  45.9 0.0 copy-done
  45.9 0.6 constant_dynamic-slice_fusion.ro_ref
  46.5 0.5 multiply_bitcast_fusion.1.gend_ref
  47.0 0.5 multiply_subtract_fusion.gstart_ref
  47.5 1.3 broadcast_select_fusion.x_ref
  48.8 5.5 %all-gather.3.cloned.1.call-done = bf16[9472,128]{1,0:T(8,128)(2,1)} async-done(((bf16[1184,128]{1,0:T(8,128)(2,1)}), bf16[9472,128]{1,0:T(8,128)(2,1)}) %all-gather.3.cloned.1.call-update) | async-done | bytes 2424848 | tf_op jit(solution)/shard_map/all_gather | solution.py:191
  54.4 1.0 slice_bitcast_fusion
  55.4 2.8 %fusion.14 = (bf16[8,512,128]{2,1,0:T(8,128)(2,1)}, bf16[8,512,128]{2,1,0:T(8,128)(2,1)S(1)}) fusion(bf16[8,1184,128]{2,1,0:T(8,128)(2,1)} %bitcast.59), kind=kLoop, calls=%fused_computation.55 | loop fusion | bytes 4194304 | tf_op jit(solution)/shard_map/slice | solution.py:194
  58.2 2.1 %reshape.153.tin_ref = bf16[8,384,24]{2,1,0:T(8,128)(2,1)} reshape(bf16[8,9216]{1,0:T(8,128)(2,1)S(1)} %slice.38) | data formatting | bytes 294912 | tf_op jit(solution)/shard_map/reshape | solution.py:195
  60.4 0.7 copy.41
  61.1 1.4 reshape_reshape.3.cin_ref
  62.5 53.1 %shard_map.139 = f32[192,128]{1,0:T(8,128)} custom-call(s32[192]{0:T(256)} %get-tuple-element.13.tgt_ref, s32[8]{0:T(128)} %multiply_subtract_fusion.gstart_ref, s32[8]{0:T(128)} %multiply_bitcast_fusion.1.gend_ref, bf16[192,24,128]{2,1,0:T(8,128)(2,1)} %broadcast_select_fusion.x_ref, bf16[8,384,24]{2,1,0:T(8,128)(2,1)} %reshape.153.tin_ref, ...), custom_call_target="tpu_custom_call" | custom-call | tf_op jit(solution)/shard_map/pallas_call | solution.py:109
  115.6 1.6 %gather_fusion.1 = f32[192,128]{1,0:T(8,128)S(1)} fusion(f32[192,128]{1,0:T(8,128)} %shard_map.139, s32[1024]{0:T(1024)S(1)} %pad_clamp_fusion), kind=kCustom, calls=%fused_computation.1 | custom fusion | bytes 197376 | tf_op jit(solution)/shard_map/jit(_take)/gather | solution.py:228
  117.3 0.1 broadcast_in_dim.56
  117.4 0.7 copy.34
  118.1 15.1 %shard_map.140 = f32[8,128]{1,0:T(8,128)} custom-call(f32[32,8,128]{2,1,0:T(8,128)} %bitcast.64), custom_call_target="tpu_custom_call" | custom-call | tf_op jit(solution)/shard_map/pallas_call | solution.py:150
  133.2 0.8 multiply_reduce_fusion.1
  133.9 1.2 slice_bitcast_fusion.2
  135.1 0.0 copy-done.3
  135.1 0.7 fusion.11
  135.9 0.6 copy.27
  136.5 0.9 convolution_bitcast_fusion
  137.3 0.6 copy.28
  (19 shorter events, 0.2 us)
Async XLA Ops:
  7.2 38.7 %copy-start = (bf16[4096,128]{1,0:T(8,128)(2,1)S(1)}, bf16[4096,128]{1,0:T(8,128)(2,1)}, u32[]{:S(2)}) copy-start(bf16[4096,128]{1,0:T(8,128)(2,1)} %param.21) | copy-start | bytes 3145732
  7.2 47.2 %all-gather.3.cloned.1.call-start = ((), (), s32[]{:S(2)}) async-start(), calls=%async_computation | async-start | bytes 2727936 | tf_op jit(solution)/shard_map/all_gather | solution.py:191
  11.8 13.7 %copy-start.4 = (bf16[256,128]{1,0:T(8,128)(2,1)S(1)}, bf16[256,128]{1,0:T(8,128)(2,1)}, u32[]{:S(2)}) copy-start(bf16[256,128]{1,0:T(8,128)(2,1)} %param.13) | copy-start | bytes 196612
  25.5 8.1 %copy-start.1 = (s32[1,192,1]{1,2,0:T(1,128)S(1)}, s32[1,192,1]{1,2,0:T(1,128)}, u32[]{:S(2)}) copy-start(s32[1,192,1]{1,2,0:T(1,128)} %param.16) | copy-start | bytes 2308
  33.3 8.4 %copy-start.2 = (s32[1,192]{1,0:T(1,128)S(1)}, s32[1,192]{1,0:T(1,128)}, u32[]{:S(2)}) copy-start(s32[1,192]{1,0:T(1,128)} %param.15) | copy-start | bytes 2308
  45.8 89.3 %copy-start.3 = (f32[128]{0:T(128)S(1)}, f32[128]{0:T(128)}, u32[]{:S(2)}) copy-start(f32[128]{0:T(128)} %param.22) | copy-start | bytes 1540
  45.8 90.6 %copy-start.5 = (f32[128,8]{0,1:T(8,128)S(1)}, f32[128,8]{0,1:T(8,128)}, u32[]{:S(2)}) copy-start(f32[128,8]{0,1:T(8,128)} %param.23) | copy-start | bytes 12292
Sparse Core Ops, SparseCore 0:
  11.9 42.4 all-gather.2

commit v11 on v10

--- a/solution.py
+++ b/solution.py
@@ -213,7 +213,7 @@
     picks = rank[None, :] == position[:, None]
     sorted_targets = jnp.sum(jnp.where(picks, targets[None, :], 0), axis=1)
     sorted_frames = jnp.sum(jnp.where(picks, hits[None, :], 0), axis=1)
-    x = jnp.take(features, sorted_frames, axis=0)
+    x = stem_layer(jnp.take(pixels[0], sorted_frames, axis=0), stem_weight)
     counts = jnp.sum(
         (targets[None, :] == jnp.arange(stream_count, dtype=jnp.int32)[:, None]).astype(jnp.int32),
         axis=1,

time: 146 us -> 163 us (1.12)
  local copies, waits for them, and re-layouts: 40.4 us -> 53.2 us
  matrix products: 8.67 us -> 17.4 us
  waiting for transfers between devices: 5.55 us -> 0.02 us
  other arithmetic: 7.64 us -> 10.3 us
  Pallas kernels: 68.2 us -> 66.2 us
    select_n x0 -> x2, local copies, waits for them, and re-layouts: none -> 18.9 us  [local(): x = stem_layer(jnp.take(pixels[0], sorted_frames, axis=0), stem_weight)]
    dot_general x1 -> x2, matrix products: 7.81 us -> 16.5 us  [stem_layer(): jnp.einsum('fapbq,pqc->fabc', pixel_tiles, kernel, preferred_element_type...]
    convert_element_type x1 -> x0, local copies, waits for them, and re-layouts: 7.55 us -> none  [stem_layer(): jax.nn.gelu(response).astype(jnp.bfloat16)]
    all_gather x1, waiting for transfers between devices: 5.53 us -> 0.01 us  [local(): gathered = lax.all_gather(jnp.concatenate(blocks, axis=0), 'stream')]
    pallas_call x1, Pallas kernels: 15.1 us -> 13 us  [exchange_sum(): pl.pallas_call(functools.partial(exchange_kernel, n), out_shape=jax.Shape...]
    unnamed x21 -> x17, local copies, waits for them, and re-layouts: 17.5 us -> 17.4 us
  transfers between devices with their start and end apart: 1 -> 1, of which waited for: 1 -> 0; matrix products, arithmetic and copies ran while one was open for 26% -> 38% of each run, Pallas kernels for 0% -> 0%
where the time goes in v11:
time: 163 us; the launch traced here: 161 us
  Pallas kernels  66.2 us (41%)
  local copies, waits for them, and re-layouts  53.2 us (33%)
  matrix products  17.4 us (11%)
  between operations  14.2 us (9%)
  other arithmetic  10.3 us (6%)
    pallas_call x1, Pallas kernels, encode_rows(): pl.pallas_call(encoder_kernel, grid_spec=grid_spec, out_shape=jax.ShapeDt...  53.2 us
    select_n x2, local copies, waits for them, and re-layouts, local(): x = stem_layer(jnp.take(pixels[0], sorted_frames, axis=0), stem_weight)  18.9 us
    unnamed x17, local copies, waits for them, and re-layouts  17.4 us
    dot_general x2, matrix products, stem_layer(): jnp.einsum('fapbq,pqc->fabc', pixel_tiles, kernel, preferred_element_type...  16.5 us
    pallas_call x1, Pallas kernels, exchange_sum(): pl.pallas_call(functools.partial(exchange_kernel, n), out_shape=jax.Shape...  13 us
    gather x1, local copies, waits for them, and re-layouts, local(): x = stem_layer(jnp.take(pixels[0], sorted_frames, axis=0), stem_weight)  4.9 us
  transfers between devices with their start and end apart: 1, of which 0 were waited for; matrix products, arithmetic and copies ran while one was open for 38% of the time, Pallas kernels for 0%

profile of v11, /device:TPU:1, one launch (start us, length us, event | category | flops | bytes accessed | tf_op | source)
XLA Modules:
  0.0 161.3 jit_solution(6969667066496516160)
XLA Ops:
  7.2 0.0 copy-start
  7.2 0.0 all-gather.3.cloned.1.call-start
  7.2 0.9 copy.33
  8.1 0.2 reshape_squeeze.4
  8.3 0.7 reshape_squeeze.10
  9.1 1.0 reshape.174
  10.1 1.6 %pad_maximum_fusion = bf16[1184,128]{1,0:T(8,128)(2,1)} fusion(bf16[512,128]{1,0:T(8,128)(2,1)} %bitcast.76, bf16[512,128]{1,0:T(8,128)(2,1)S(1)} %reshape.174, bf16[80,128]{1,0:T(8,128)(2,1)S(1)} %get-tuple-element.21, bf16[80,128]{1,0:T(8,128)(2,1)S(1)} %get-tuple-element.22), kind=kLoop, calls=%fused_computation.24 | loop fusion | flops 1212416 | bytes 606208 | tf_op jit(solution)/shard_map/concatenate | solution.py:191
  11.7 0.0 all-gather.3.cloned.1.call-update
  11.7 0.9 convert_reduce_fusion.1
  12.7 0.8 convert_reduce_fusion.2
  13.5 0.1 reduce_sum.70
  13.6 1.4 select_reduce_fusion
  15.0 12.9 %copy.34 = bf16[1,768,16,384]{1,3,2,0:T(8,128)(2,1)} copy(bf16[1,768,16,384]{3,2,1,0:T(8,128)(2,1)} %param.12) | data formatting | bytes 18874368 | tf_op args[0]
  27.9 4.9 %gather_fusion = bf16[192,16,384]{2,1,0:T(8,128)(2,1)S(1)} fusion(bf16[768,16,384]{2,1,0:T(8,128)(2,1)} %bitcast.66, s32[1024]{0:T(1024)S(1)} %pad_clamp_fusion.1), kind=kCustom, calls=%fused_computation | custom fusion | bytes 4719360 | tf_op jit(solution)/shard_map/jit(_take)/gather | solution.py:216
  32.8 1.8 %broadcast_select_fusion = bf16[192,16,384]{2,1,0:T(8,128)(2,1)} fusion(bf16[192,16,384]{2,1,0:T(8,128)(2,1)S(1)} %gather_fusion, pred[192]{0:T(512)(128)(4,1)S(1)} %compare_and_fusion.1), kind=kLoop, calls=%fused_computation.21 | loop fusion | flops 1179648 | bytes 4718784 | tf_op jit(solution)/shard_map/jit(_take)/select_n | solution.py:216
  34.6 5.0 %copy.31 = bf16[192,16,384]{0,2,1:T(8,128)(2,1)} copy(bf16[192,16,384]{2,1,0:T(8,128)(2,1)} %broadcast_select_fusion) | data formatting | bytes 4718592 | tf_op jit(solution)/shard_map/jit(_take)/select_n | solution.py:216
  39.6 0.0 copy-start.2
  39.6 13.9 %copy.32 = bf16[192,16,24,16]{2,3,1,0:T(8,128)(2,1)} copy(bf16[192,16,24,16]{0,3,2,1:T(8,128)(2,1)} %bitcast.67) | data formatting | bytes 4718592 | tf_op jit(solution)/shard_map/jit(_take)/select_n | solution.py:216
  53.5 0.2 reduce-window.9
  53.7 0.7 multiply_bitcast_fusion
  54.4 0.0 copy-done.2
  54.4 7.4 %convert_reduce_fusion = f32[768,128]{1,0:T(8,128)S(1)} fusion(bf16[768,16,24,16]{0,3,2,1:T(8,128)(2,1)} %bitcast.68, bf16[16,16,128,1]{2,1,3,0:T(8,128)(2,1)S(1)} %bitcast.87), kind=kOutput, calls=%fused_computation.11 | convolution fusion | flops 1233813504 | bytes 9895936 | tf_op jit(solution)/shard_map/fapbq,pqc->fabc/dot_general | solution.py:22
  61.8 0.2 multiply_reduce_fusion
  62.0 0.1 reshape.181
  62.1 0.0 copy-done
  62.1 0.6 constant_dynamic-slice_fusion.ro_ref
  62.7 0.5 multiply_bitcast_fusion.1.gend_ref
  63.2 0.5 multiply_subtract_fusion.gstart_ref
  63.8 9.1 %fusion.15.x_ref = bf16[192,24,128]{2,1,0:T(8,128)(2,1)} fusion(bf16[192,16,24,16]{2,3,1,0:T(8,128)(2,1)} %copy.32, bf16[16,16,128,1]{2,1,0,3:T(8,128)(2,1)S(1)} %bitcast.88), kind=kOutput, calls=%fused_computation.20 | convolution fusion | flops 307298304 | bytes 3604480 | tf_op jit(solution)/shard_map/fapbq,pqc->fabc/dot_general | solution.py:22
  72.9 2.7 %fusion.22 = (bf16[8,512,128]{2,1,0:T(8,128)(2,1)}, bf16[8,512,128]{2,1,0:T(8,128)(2,1)S(1)}) fusion(bf16[8,1184,128]{2,1,0:T(8,128)(2,1)} %bitcast.69), kind=kLoop, calls=%fused_computation.64 | loop fusion | bytes 4194304 | tf_op jit(solution)/shard_map/slice | solution.py:194
  75.6 1.0 slice_bitcast_fusion
  76.6 1.5 reshape_reshape.3.cin_ref
  78.1 2.2 %reshape.177.tin_ref = bf16[8,384,24]{2,1,0:T(8,128)(2,1)} reshape(bf16[8,9216]{1,0:T(8,128)(2,1)S(1)} %slice.38) | data formatting | bytes 294912 | tf_op jit(solution)/shard_map/reshape | solution.py:195
  80.4 0.7 copy.50
  81.1 0.0 copy-start.1
  81.1 53.2 %shard_map.139 = f32[192,128]{1,0:T(8,128)} custom-call(s32[192]{0:T(256)} %get-tuple-element.16.tgt_ref, s32[8]{0:T(128)} %multiply_subtract_fusion.gstart_ref, s32[8]{0:T(128)} %multiply_bitcast_fusion.1.gend_ref, bf16[192,24,128]{2,1,0:T(8,128)(2,1)} %fusion.15.x_ref, bf16[8,384,24]{2,1,0:T(8,128)(2,1)} %reshape.177.tin_ref, ...), custom_call_target="tpu_custom_call" | custom-call | tf_op jit(solution)/shard_map/pallas_call | solution.py:109
  134.3 1.6 gather_fusion.1
  135.9 0.1 broadcast_in_dim.56
  136.1 0.7 copy.43
  136.7 13.0 %shard_map.140 = f32[8,128]{1,0:T(8,128)} custom-call(f32[32,8,128]{2,1,0:T(8,128)} %bitcast.75), custom_call_target="tpu_custom_call" | custom-call | tf_op jit(solution)/shard_map/pallas_call | solution.py:150
  149.7 0.8 multiply_reduce_fusion.1
  150.5 0.0 copy-done.1
  150.5 0.7 fusion.19
  151.2 0.0 copy-done.3
  151.2 0.9 convolution_bitcast_fusion
  152.1 0.6 copy.36
  152.7 0.6 copy.35
  153.3 1.2 slice_bitcast_fusion.2
  (17 shorter events, 0.2 us)
Async XLA Ops:
  7.2 54.9 %copy-start = (bf16[4096,128]{1,0:T(8,128)(2,1)S(1)}, bf16[4096,128]{1,0:T(8,128)(2,1)}, u32[]{:S(2)}) copy-start(bf16[4096,128]{1,0:T(8,128)(2,1)} %param.21) | copy-start | bytes 3145732
  7.2 65.7 %all-gather.3.cloned.1.call-start = ((), (), s32[]{:S(2)}) async-start(), calls=%async_computation | async-start | bytes 2727936 | tf_op jit(solution)/shard_map/all_gather | solution.py:191
  39.6 14.8 %copy-start.2 = (bf16[256,128]{1,0:T(8,128)(2,1)S(1)}, bf16[256,128]{1,0:T(8,128)(2,1)}, u32[]{:S(2)}) copy-start(bf16[256,128]{1,0:T(8,128)(2,1)} %param.13) | copy-start | bytes 196612
  81.1 69.4 %copy-start.1 = (f32[128]{0:T(128)S(1)}, f32[128]{0:T(128)}, u32[]{:S(2)}) copy-start(f32[128]{0:T(128)} %param.22) | copy-start | bytes 1540
  81.1 70.2 %copy-start.3 = (f32[128,8]{0,1:T(8,128)S(1)}, f32[128,8]{0,1:T(8,128)}, u32[]{:S(2)}) copy-start(f32[128,8]{0,1:T(8,128)} %param.23) | copy-start | bytes 12292
Sparse Core Ops, SparseCore 0:
  11.8 42.3 all-gather.2

commit v12 on v10

--- a/solution.py
+++ b/solution.py
@@ -8,7 +8,7 @@
 from jax.sharding import PartitionSpec as P
 
 PATCH = 16
-BLOCK_HITS = 16
+BLOCK_HITS = 32
 
 
 def rms_norm(values):

time: 146 us -> 142 us (0.973)
  Pallas kernels: 68.2 us -> 64.9 us
    pallas_call x1, Pallas kernels: 53.1 us -> 49.8 us  [encode_rows(): pl.pallas_call(encoder_kernel, grid_spec=grid_spec, out_shape=jax.ShapeDt...]
where the time goes in v12:
time: 142 us
  Pallas kernels  64.9 us (46%)
  local copies, waits for them, and re-layouts  40.4 us (28%)
  between operations  14.2 us (10%)
  matrix products  8.67 us (6%)
  other arithmetic  7.64 us (5%)
  waiting for transfers between devices  5.55 us (4%)
    pallas_call x1, Pallas kernels, encode_rows(): pl.pallas_call(encoder_kernel, grid_spec=grid_spec, out_shape=jax.ShapeDt...  49.8 us
    unnamed x21, local copies, waits for them, and re-layouts  17.5 us
    pallas_call x1, Pallas kernels, exchange_sum(): pl.pallas_call(functools.partial(exchange_kernel, n), out_shape=jax.Shape...  15.1 us
    dot_general x1, matrix products, stem_layer(): jnp.einsum('fapbq,pqc->fabc', pixel_tiles, kernel, preferred_element_type...  7.81 us
    convert_element_type x1, local copies, waits for them, and re-layouts, stem_layer(): jax.nn.gelu(response).astype(jnp.bfloat16)  7.55 us
    all_gather x1, waiting for transfers between devices, local(): gathered = lax.all_gather(jnp.concatenate(blocks, axis=0), 'stream')  5.53 us
    gather x1, local copies, waits for them, and re-layouts, local(): x = jnp.take(features, sorted_frames, axis=0)  3.32 us
  transfers between devices with their start and end apart: 1, of which 1 were waited for; matrix products, arithmetic and copies ran while one was open for 26% of the time, Pallas kernels for 0%

profile of v12, /device:TPU:1, one launch (start us, length us, event | category | flops | bytes accessed | tf_op | source)
XLA Modules:
  0.0 141.5 jit_solution(15573149334055127529)
XLA Ops:
  7.2 0.0 copy-start
  7.2 0.0 all-gather.3.cloned.1.call-start
  7.2 1.1 reshape.150
  8.3 0.7 reshape_squeeze.10
  9.0 0.8 copy.26
  9.9 0.2 reshape_squeeze.4
  10.1 1.7 %pad_maximum_fusion = bf16[1184,128]{1,0:T(8,128)(2,1)} fusion(bf16[512,128]{1,0:T(8,128)(2,1)} %bitcast.65, bf16[512,128]{1,0:T(8,128)(2,1)S(1)} %reshape.150, bf16[80,128]{1,0:T(8,128)(2,1)S(1)} %get-tuple-element.20, bf16[80,128]{1,0:T(8,128)(2,1)S(1)} %get-tuple-element.21), kind=kLoop, calls=%fused_computation.15 | loop fusion | flops 1212416 | bytes 606208 | tf_op jit(solution)/shard_map/concatenate | solution.py:191
  11.7 0.0 all-gather.3.cloned.1.call-update
  11.8 0.0 copy-start.4
  11.8 13.0 %copy.24 = bf16[1,768,16,384]{1,3,2,0:T(8,128)(2,1)} copy(bf16[1,768,16,384]{3,2,1,0:T(8,128)(2,1)} %param.12) | data formatting | bytes 18874368 | tf_op args[0]
  24.8 0.7 multiply_bitcast_fusion
  25.5 0.0 copy-done.4
  25.5 7.8 %convert_reduce_fusion = (f32[768,128]{1,0:T(8,128)S(1)}, bf16[768,24,128]{2,0,1:T(8,128)(2,1)}) fusion(bf16[768,16,24,16]{0,3,2,1:T(8,128)(2,1)} %bitcast.57, bf16[16,16,128,1]{2,1,3,0:T(8,128)(2,1)S(1)} %bitcast.76), kind=kOutput, calls=%fused_computation.11 | convolution fusion | flops 1233813504 | bytes 14614528 | tf_op jit(solution)/shard_map/fapbq,pqc->fabc/dot_general | solution.py:22
  33.3 0.2 multiply_reduce_fusion
  33.5 0.1 reshape.156
  33.6 0.0 copy-done.1
  33.6 0.1 convert_reduce_fusion.2
  33.7 0.2 reduce-window.9
  33.9 7.6 %copy.25 = bf16[768,24,128]{2,1,0:T(8,128)(2,1)} copy(bf16[768,24,128]{2,0,1:T(8,128)(2,1)} %get-tuple-element.19) | data formatting | bytes 9437184 | tf_op jit(solution)/shard_map/convert_element_type | solution.py:25
  41.4 0.2 convert_reduce_fusion.1
  41.6 0.1 reduce_sum.70
  41.7 0.0 copy-done.2
  41.8 0.7 select_reduce_fusion
  42.5 3.3 %gather_fusion = bf16[192,24,128]{2,1,0:T(8,128)(2,1)S(1)} fusion(bf16[768,24,128]{2,1,0:T(8,128)(2,1)} %copy.25, s32[1024]{0:T(1024)S(1)} %pad_clamp_fusion.1), kind=kCustom, calls=%fused_computation | custom fusion | bytes 2360064 | tf_op jit(solution)/shard_map/jit(_take)/gather | solution.py:216
  45.8 0.0 copy-start.3
  45.8 0.0 copy-start.5
  45.9 0.0 copy-done
  45.9 0.6 constant_dynamic-slice_fusion.ro_ref
  46.5 0.5 multiply_bitcast_fusion.1.gend_ref
  47.0 0.5 multiply_subtract_fusion.gstart_ref
  47.5 1.3 broadcast_select_fusion.x_ref
  48.8 5.5 %all-gather.3.cloned.1.call-done = bf16[9472,128]{1,0:T(8,128)(2,1)} async-done(((bf16[1184,128]{1,0:T(8,128)(2,1)}), bf16[9472,128]{1,0:T(8,128)(2,1)}) %all-gather.3.cloned.1.call-update) | async-done | bytes 2424848 | tf_op jit(solution)/shard_map/all_gather | solution.py:191
  54.4 1.0 slice_bitcast_fusion
  55.4 2.8 %fusion.14 = (bf16[8,512,128]{2,1,0:T(8,128)(2,1)}, bf16[8,512,128]{2,1,0:T(8,128)(2,1)S(1)}) fusion(bf16[8,1184,128]{2,1,0:T(8,128)(2,1)} %bitcast.59), kind=kLoop, calls=%fused_computation.55 | loop fusion | bytes 4194304 | tf_op jit(solution)/shard_map/slice | solution.py:194
  58.2 2.1 %reshape.153.tin_ref = bf16[8,384,24]{2,1,0:T(8,128)(2,1)} reshape(bf16[8,9216]{1,0:T(8,128)(2,1)S(1)} %slice.38) | data formatting | bytes 294912 | tf_op jit(solution)/shard_map/reshape | solution.py:195
  60.4 0.7 copy.41
  61.1 1.4 %reshape_reshape.3.cin_ref = bf16[8,128,512]{2,1,0:T(8,128)(2,1)} reshape(bf16[8,512,128]{2,1,0:T(8,128)(2,1)S(1)} %get-tuple-element.15) | data formatting | bytes 2097152 | tf_op jit(solution)/shard_map/reshape;reshape | solution.py:195
  62.5 49.8 %shard_map.139 = f32[192,128]{1,0:T(8,128)} custom-call(s32[192]{0:T(256)} %get-tuple-element.13.tgt_ref, s32[8]{0:T(128)} %multiply_subtract_fusion.gstart_ref, s32[8]{0:T(128)} %multiply_bitcast_fusion.1.gend_ref, bf16[192,24,128]{2,1,0:T(8,128)(2,1)} %broadcast_select_fusion.x_ref, bf16[8,384,24]{2,1,0:T(8,128)(2,1)} %reshape.153.tin_ref, ...), custom_call_target="tpu_custom_call" | custom-call | tf_op jit(solution)/shard_map/pallas_call | solution.py:109
  112.3 1.6 %gather_fusion.1 = f32[192,128]{1,0:T(8,128)S(1)} fusion(f32[192,128]{1,0:T(8,128)} %shard_map.139, s32[1024]{0:T(1024)S(1)} %pad_clamp_fusion), kind=kCustom, calls=%fused_computation.1 | custom fusion | bytes 197376 | tf_op jit(solution)/shard_map/jit(_take)/gather | solution.py:228
  113.9 0.1 broadcast_in_dim.56
  114.1 0.7 copy.34
  114.8 15.1 %shard_map.140 = f32[8,128]{1,0:T(8,128)} custom-call(f32[32,8,128]{2,1,0:T(8,128)} %bitcast.64), custom_call_target="tpu_custom_call" | custom-call | tf_op jit(solution)/shard_map/pallas_call | solution.py:150
  129.9 0.8 multiply_reduce_fusion.1
  130.7 1.2 slice_bitcast_fusion.2
  131.9 0.7 fusion.11
  132.6 0.6 copy.27
  133.2 0.9 convolution_bitcast_fusion
  134.1 0.6 copy.28
  (19 shorter events, 0.2 us)
Async XLA Ops:
  7.2 38.7 %copy-start = (bf16[4096,128]{1,0:T(8,128)(2,1)S(1)}, bf16[4096,128]{1,0:T(8,128)(2,1)}, u32[]{:S(2)}) copy-start(bf16[4096,128]{1,0:T(8,128)(2,1)} %param.21) | copy-start | bytes 3145732
  7.2 47.2 %all-gather.3.cloned.1.call-start = ((), (), s32[]{:S(2)}) async-start(), calls=%async_computation | async-start | bytes 2727936 | tf_op jit(solution)/shard_map/all_gather | solution.py:191
  11.8 13.7 %copy-start.4 = (bf16[256,128]{1,0:T(8,128)(2,1)S(1)}, bf16[256,128]{1,0:T(8,128)(2,1)}, u32[]{:S(2)}) copy-start(bf16[256,128]{1,0:T(8,128)(2,1)} %param.13) | copy-start | bytes 196612
  25.5 8.1 %copy-start.1 = (s32[1,192,1]{1,2,0:T(1,128)S(1)}, s32[1,192,1]{1,2,0:T(1,128)}, u32[]{:S(2)}) copy-start(s32[1,192,1]{1,2,0:T(1,128)} %param.16) | copy-start | bytes 2308
  33.3 8.4 %copy-start.2 = (s32[1,192]{1,0:T(1,128)S(1)}, s32[1,192]{1,0:T(1,128)}, u32[]{:S(2)}) copy-start(s32[1,192]{1,0:T(1,128)} %param.15) | copy-start | bytes 2308
  45.8 86.1 %copy-start.3 = (f32[128]{0:T(128)S(1)}, f32[128]{0:T(128)}, u32[]{:S(2)}) copy-start(f32[128]{0:T(128)} %param.22) | copy-start | bytes 1540
  45.8 87.4 %copy-start.5 = (f32[128,8]{0,1:T(8,128)S(1)}, f32[128,8]{0,1:T(8,128)}, u32[]{:S(2)}) copy-start(f32[128,8]{0,1:T(8,128)} %param.23) | copy-start | bytes 12292
Sparse Core Ops, SparseCore 0:
  11.9 42.4 all-gather.2

commit v13 on v12

--- a/solution.py
+++ b/solution.py
@@ -8,7 +8,7 @@
 from jax.sharding import PartitionSpec as P
 
 PATCH = 16
-BLOCK_HITS = 32
+BLOCK_HITS = 64
 
 
 def rms_norm(values):

time: 142 us -> 144 us (1.014)
  Pallas kernels: 64.9 us -> 66.5 us
    pallas_call x1, Pallas kernels: 49.8 us -> 51.4 us  [encode_rows(): pl.pallas_call(encoder_kernel, grid_spec=grid_spec, out_shape=jax.ShapeDt...]
where the time goes in v13:
time: 144 us; the launch traced here: 143 us
  Pallas kernels  66.5 us (46%)
  local copies, waits for them, and re-layouts  40.4 us (28%)
  between operations  14.2 us (10%)
  matrix products  8.67 us (6%)
  other arithmetic  7.64 us (5%)
  waiting for transfers between devices  5.55 us (4%)
    pallas_call x1, Pallas kernels, encode_rows(): pl.pallas_call(encoder_kernel, grid_spec=grid_spec, out_shape=jax.ShapeDt...  51.4 us
    unnamed x21, local copies, waits for them, and re-layouts  17.5 us
    pallas_call x1, Pallas kernels, exchange_sum(): pl.pallas_call(functools.partial(exchange_kernel, n), out_shape=jax.Shape...  15.1 us
    dot_general x1, matrix products, stem_layer(): jnp.einsum('fapbq,pqc->fabc', pixel_tiles, kernel, preferred_element_type...  7.81 us
    convert_element_type x1, local copies, waits for them, and re-layouts, stem_layer(): jax.nn.gelu(response).astype(jnp.bfloat16)  7.55 us
    all_gather x1, waiting for transfers between devices, local(): gathered = lax.all_gather(jnp.concatenate(blocks, axis=0), 'stream')  5.53 us
    gather x1, local copies, waits for them, and re-layouts, local(): x = jnp.take(features, sorted_frames, axis=0)  3.32 us
  transfers between devices with their start and end apart: 1, of which 1 were waited for; matrix products, arithmetic and copies ran while one was open for 26% of the time, Pallas kernels for 0%

profile of v13, /device:TPU:1, one launch (start us, length us, event | category | flops | bytes accessed | tf_op | source)
XLA Modules:
  0.0 143.1 jit_solution(7958345192160584435)
XLA Ops:
  7.2 0.0 copy-start
  7.2 0.0 all-gather.3.cloned.1.call-start
  7.2 1.1 reshape.150
  8.3 0.7 reshape_squeeze.10
  9.0 0.8 copy.26
  9.9 0.2 reshape_squeeze.4
  10.1 1.7 %pad_maximum_fusion = bf16[1184,128]{1,0:T(8,128)(2,1)} fusion(bf16[512,128]{1,0:T(8,128)(2,1)} %bitcast.65, bf16[512,128]{1,0:T(8,128)(2,1)S(1)} %reshape.150, bf16[80,128]{1,0:T(8,128)(2,1)S(1)} %get-tuple-element.20, bf16[80,128]{1,0:T(8,128)(2,1)S(1)} %get-tuple-element.21), kind=kLoop, calls=%fused_computation.15 | loop fusion | flops 1212416 | bytes 606208 | tf_op jit(solution)/shard_map/concatenate | solution.py:191
  11.7 0.0 all-gather.3.cloned.1.call-update
  11.8 0.0 copy-start.4
  11.8 13.0 %copy.24 = bf16[1,768,16,384]{1,3,2,0:T(8,128)(2,1)} copy(bf16[1,768,16,384]{3,2,1,0:T(8,128)(2,1)} %param.12) | data formatting | bytes 18874368 | tf_op args[0]
  24.8 0.7 multiply_bitcast_fusion
  25.5 0.0 copy-done.4
  25.5 7.8 %convert_reduce_fusion = (f32[768,128]{1,0:T(8,128)S(1)}, bf16[768,24,128]{2,0,1:T(8,128)(2,1)}) fusion(bf16[768,16,24,16]{0,3,2,1:T(8,128)(2,1)} %bitcast.57, bf16[16,16,128,1]{2,1,3,0:T(8,128)(2,1)S(1)} %bitcast.76), kind=kOutput, calls=%fused_computation.11 | convolution fusion | flops 1233813504 | bytes 14614528 | tf_op jit(solution)/shard_map/fapbq,pqc->fabc/dot_general | solution.py:22
  33.3 0.2 multiply_reduce_fusion
  33.5 0.1 reshape.156
  33.6 0.0 copy-done.1
  33.6 0.1 convert_reduce_fusion.2
  33.7 0.2 reduce-window.9
  33.9 7.6 %copy.25 = bf16[768,24,128]{2,1,0:T(8,128)(2,1)} copy(bf16[768,24,128]{2,0,1:T(8,128)(2,1)} %get-tuple-element.19) | data formatting | bytes 9437184 | tf_op jit(solution)/shard_map/convert_element_type | solution.py:25
  41.4 0.2 convert_reduce_fusion.1
  41.6 0.1 reduce_sum.70
  41.8 0.7 select_reduce_fusion
  42.5 3.3 %gather_fusion = bf16[192,24,128]{2,1,0:T(8,128)(2,1)S(1)} fusion(bf16[768,24,128]{2,1,0:T(8,128)(2,1)} %copy.25, s32[1024]{0:T(1024)S(1)} %pad_clamp_fusion.1), kind=kCustom, calls=%fused_computation | custom fusion | bytes 2360064 | tf_op jit(solution)/shard_map/jit(_take)/gather | solution.py:216
  45.8 0.0 copy-start.3
  45.8 0.0 copy-start.5
  45.9 0.0 copy-done
  45.9 0.6 constant_dynamic-slice_fusion.ro_ref
  46.5 0.5 multiply_bitcast_fusion.1.gend_ref
  47.0 0.5 multiply_subtract_fusion.gstart_ref
  47.5 1.3 broadcast_select_fusion.x_ref
  48.8 5.5 %all-gather.3.cloned.1.call-done = bf16[9472,128]{1,0:T(8,128)(2,1)} async-done(((bf16[1184,128]{1,0:T(8,128)(2,1)}), bf16[9472,128]{1,0:T(8,128)(2,1)}) %all-gather.3.cloned.1.call-update) | async-done | bytes 2424848 | tf_op jit(solution)/shard_map/all_gather | solution.py:191
  54.4 1.0 slice_bitcast_fusion
  55.4 2.8 %fusion.14 = (bf16[8,512,128]{2,1,0:T(8,128)(2,1)}, bf16[8,512,128]{2,1,0:T(8,128)(2,1)S(1)}) fusion(bf16[8,1184,128]{2,1,0:T(8,128)(2,1)} %bitcast.59), kind=kLoop, calls=%fused_computation.55 | loop fusion | bytes 4194304 | tf_op jit(solution)/shard_map/slice | solution.py:194
  58.2 2.1 %reshape.153.tin_ref = bf16[8,384,24]{2,1,0:T(8,128)(2,1)} reshape(bf16[8,9216]{1,0:T(8,128)(2,1)S(1)} %slice.38) | data formatting | bytes 294912 | tf_op jit(solution)/shard_map/reshape | solution.py:195
  60.4 0.7 copy.41
  61.1 1.4 %reshape_reshape.3.cin_ref = bf16[8,128,512]{2,1,0:T(8,128)(2,1)} reshape(bf16[8,512,128]{2,1,0:T(8,128)(2,1)S(1)} %get-tuple-element.15) | data formatting | bytes 2097152 | tf_op jit(solution)/shard_map/reshape;reshape | solution.py:195
  62.5 51.4 %shard_map.139 = f32[192,128]{1,0:T(8,128)} custom-call(s32[192]{0:T(256)} %get-tuple-element.13.tgt_ref, s32[8]{0:T(128)} %multiply_subtract_fusion.gstart_ref, s32[8]{0:T(128)} %multiply_bitcast_fusion.1.gend_ref, bf16[192,24,128]{2,1,0:T(8,128)(2,1)} %broadcast_select_fusion.x_ref, bf16[8,384,24]{2,1,0:T(8,128)(2,1)} %reshape.153.tin_ref, ...), custom_call_target="tpu_custom_call" | custom-call | tf_op jit(solution)/shard_map/pallas_call | solution.py:109
  113.9 1.6 %gather_fusion.1 = f32[192,128]{1,0:T(8,128)S(1)} fusion(f32[192,128]{1,0:T(8,128)} %shard_map.139, s32[1024]{0:T(1024)S(1)} %pad_clamp_fusion), kind=kCustom, calls=%fused_computation.1 | custom fusion | bytes 197376 | tf_op jit(solution)/shard_map/jit(_take)/gather | solution.py:228
  115.5 0.1 broadcast_in_dim.56
  115.7 0.7 copy.34
  116.3 15.1 %shard_map.140 = f32[8,128]{1,0:T(8,128)} custom-call(f32[32,8,128]{2,1,0:T(8,128)} %bitcast.64), custom_call_target="tpu_custom_call" | custom-call | tf_op jit(solution)/shard_map/pallas_call | solution.py:150
  131.4 0.8 multiply_reduce_fusion.1
  132.2 1.2 slice_bitcast_fusion.2
  133.4 0.0 copy-done.3
  133.4 0.7 fusion.11
  134.2 0.6 copy.27
  134.8 0.9 convolution_bitcast_fusion
  135.6 0.6 copy.28
  (19 shorter events, 0.2 us)
Async XLA Ops:
  7.2 38.7 %copy-start = (bf16[4096,128]{1,0:T(8,128)(2,1)S(1)}, bf16[4096,128]{1,0:T(8,128)(2,1)}, u32[]{:S(2)}) copy-start(bf16[4096,128]{1,0:T(8,128)(2,1)} %param.21) | copy-start | bytes 3145732
  7.2 47.2 %all-gather.3.cloned.1.call-start = ((), (), s32[]{:S(2)}) async-start(), calls=%async_computation | async-start | bytes 2727936 | tf_op jit(solution)/shard_map/all_gather | solution.py:191
  11.8 13.7 %copy-start.4 = (bf16[256,128]{1,0:T(8,128)(2,1)S(1)}, bf16[256,128]{1,0:T(8,128)(2,1)}, u32[]{:S(2)}) copy-start(bf16[256,128]{1,0:T(8,128)(2,1)} %param.13) | copy-start | bytes 196612
  25.5 8.1 %copy-start.1 = (s32[1,192,1]{1,2,0:T(1,128)S(1)}, s32[1,192,1]{1,2,0:T(1,128)}, u32[]{:S(2)}) copy-start(s32[1,192,1]{1,2,0:T(1,128)} %param.16) | copy-start | bytes 2308
  33.3 8.4 %copy-start.2 = (s32[1,192]{1,0:T(1,128)S(1)}, s32[1,192]{1,0:T(1,128)}, u32[]{:S(2)}) copy-start(s32[1,192]{1,0:T(1,128)} %param.15) | copy-start | bytes 2308
  45.8 87.6 %copy-start.3 = (f32[128]{0:T(128)S(1)}, f32[128]{0:T(128)}, u32[]{:S(2)}) copy-start(f32[128]{0:T(128)} %param.22) | copy-start | bytes 1540
  45.8 88.9 %copy-start.5 = (f32[128,8]{0,1:T(8,128)S(1)}, f32[128,8]{0,1:T(8,128)}, u32[]{:S(2)}) copy-start(f32[128,8]{0,1:T(8,128)} %param.23) | copy-start | bytes 12292
Sparse Core Ops, SparseCore 0:
  11.9 42.4 all-gather.2

commit v14 on v12

--- a/solution.py
+++ b/solution.py
@@ -33,7 +33,7 @@
 
 
 def encoder_kernel(
-    tgt_ref, gstart_ref, gend_ref,
+    tgt_ref, gstart_ref, gend_ref, order_ref,
     x_ref, tin_ref, tout_ref, cin_ref, cout_ref, ro_ref,
     o_ref, mix_scr, hid_scr, out_scr,
 ):
@@ -81,15 +81,24 @@
             out_scr[...] = jnp.where(inside, part, out_scr[...])
     after_mlp = after_mix + out_scr[...]
     pooled = jnp.mean(after_mlp.reshape(hits, row_len, channels), axis=1).astype(bf16)
-    o_ref[...] = jnp.dot(pooled, ro_ref[...], preferred_element_type=f32)
-
-
-def encode_rows(x, sorted_targets, gstart, gend, tin_all, tout_all, cin_all, cout_all, row_readout):
+    projected = jnp.dot(pooled, ro_ref[...], preferred_element_type=f32)
+
+    @pl.when(block == 0)
+    def _():
+        o_ref[...] = jnp.zeros_like(o_ref)
+
+    per_owner = order_ref.shape[0] // o_ref.shape[0]
+    for h in range(hits):
+        hit = order_ref[base + h]
+        o_ref[hit // per_owner, pl.ds(hit % per_owner, 1), :] = projected[h:h + 1, :]
+
+
+def encode_rows(x, sorted_targets, gstart, gend, order, owners, tin_all, tout_all, cin_all, cout_all, row_readout):
     hit_count, row_len, channels = x.shape
     steps = hit_count // BLOCK_HITS
     full = lambda a: pl.BlockSpec(a.shape, lambda i, *_: (0,) * a.ndim)
     grid_spec = pltpu.PrefetchScalarGridSpec(
-        num_scalar_prefetch=3,
+        num_scalar_prefetch=4,
         grid=(steps,),
         in_specs=[
             pl.BlockSpec((BLOCK_HITS, row_len, channels), lambda i, *_: (i, 0, 0)),
@@ -99,7 +108,7 @@
             full(cout_all),
             full(row_readout),
         ],
-        out_specs=pl.BlockSpec((BLOCK_HITS, channels), lambda i, *_: (i, 0)),
+        out_specs=pl.BlockSpec((owners, 8, channels), lambda i, *_: (0, 0, 0)),
         scratch_shapes=[
             pltpu.VMEM((BLOCK_HITS * row_len, channels), jnp.float32),
             pltpu.VMEM((BLOCK_HITS * row_len, cin_all.shape[-1]), jnp.float32),
@@ -109,9 +118,9 @@
     return pl.pallas_call(
         encoder_kernel,
         grid_spec=grid_spec,
-        out_shape=jax.ShapeDtypeStruct((hit_count, channels), jnp.float32),
+        out_shape=jax.ShapeDtypeStruct((owners, 8, channels), jnp.float32),
         compiler_params=pltpu.CompilerParams(dimension_semantics=("arbitrary",)),
-    )(sorted_targets, gstart, gend, x, tin_all, tout_all, cin_all, cout_all, row_readout)
+    )(sorted_targets, gstart, gend, order, x, tin_all, tout_all, cin_all, cout_all, row_readout)
 
 
 def exchange_kernel(n, x_ref, o_ref, recv, send_sems, recv_sems):
@@ -221,25 +230,19 @@
     gend = jnp.cumsum(counts) * row_len
     gstart = gend - counts * row_len
     row_readout = lax.dynamic_slice_in_dim(readout, mod_index * channels, channels, axis=0)
-    projected_sorted = encode_rows(
+    order = jnp.sum(jnp.where(picks, position[None, :], 0), axis=1)
+    hits_per_owner = targets.shape[0] // module_count
+    packed = encode_rows(
         x, sorted_targets, gstart.astype(jnp.int32), gend.astype(jnp.int32),
+        order.astype(jnp.int32), module_count,
         tin_all, tout_all, cin_all, cout_all, row_readout,
     )
-    projected_part = jnp.take(projected_sorted, rank, axis=0)
-
-    packed = jnp.concatenate(
-        [
-            projected_part.reshape(module_count, -1),
-            veto_part.reshape(module_count, -1),
-        ],
-        axis=1,
-    )
-    width = packed.shape[1]
+    veto_rows = veto_part.reshape(module_count, 1, -1)
+    packed = lax.dynamic_update_slice(packed, veto_rows, (0, hits_per_owner, 0))
     lanes = 128
-    padded = -(-width // (8 * lanes)) * 8 * lanes
-    packed = jnp.pad(packed, ((0, 0), (0, padded - width)))
-    totals = exchange_sum(packed.reshape(module_count, -1, lanes)).reshape(-1)
-    split = projected_part.size // module_count
+    split = hits_per_owner * channels
+    width = split + veto_rows.shape[-1]
+    totals = exchange_sum(packed).reshape(-1)
     projected = totals[:split].reshape(-1, channels)
     veto = totals[split:width]
     latent = rms_norm(projected) * latent_gain

time: 142 us -> 143 us (level)
  waiting for transfers between devices: 5.55 us -> 9.67 us
  local copies, waits for them, and re-layouts: 40.4 us -> 37.3 us
  matrix products: 8.67 us -> 7.1 us
    all_gather x1, waiting for transfers between devices: 5.53 us -> 9.65 us  [local(): gathered = lax.all_gather(jnp.concatenate(blocks, axis=0), 'stream')]
    convert_element_type x1, local copies, waits for them, and re-layouts: 7.55 us -> 5.16 us  [stem_layer(): jax.nn.gelu(response).astype(jnp.bfloat16)]
    dynamic_update_slice x0 -> x1, local copies, waits for them, and re-layouts: none -> 1.75 us  [local(): packed = lax.dynamic_update_slice(packed, veto_rows, (0, hits_per_owner, 0))]
    gather x2 -> x0, local copies, waits for them, and re-layouts: 1.6 us -> none  [local(): projected_part = jnp.take(projected_sorted, rank, axis=0)]
    dot_general x1, matrix products: 7.81 us -> 6.23 us  [stem_layer(): jnp.einsum('fapbq,pqc->fabc', pixel_tiles, kernel, preferred_element_type...]
    unnamed x21 -> x20, local copies, waits for them, and re-layouts: 17.5 us -> 16.9 us
  transfers between devices with their start and end apart: 1 -> 1, of which waited for: 1 -> 1; matrix products, arithmetic and copies ran while one was open for 26% -> 23% of each run, Pallas kernels for 0% -> 0%
where the time goes in v14:
time: 143 us; the launch traced here: 142 us
  Pallas kernels  65.7 us (46%)
  local copies, waits for them, and re-layouts  37.3 us (26%)
  between operations  14.2 us (10%)
  waiting for transfers between devices  9.67 us (7%)
  other arithmetic  7.73 us (5%)
  matrix products  7.1 us (5%)
    pallas_call x1, Pallas kernels, encode_rows(): pl.pallas_call(encoder_kernel, grid_spec=grid_spec, out_shape=jax.ShapeDt...  50.7 us
    unnamed x20, local copies, waits for them, and re-layouts  16.9 us
    pallas_call x1, Pallas kernels, exchange_sum(): pl.pallas_call(functools.partial(exchange_kernel, n), out_shape=jax.Shape...  14.9 us
    all_gather x1, waiting for transfers between devices, local(): gathered = lax.all_gather(jnp.concatenate(blocks, axis=0), 'stream')  9.65 us
    dot_general x1, matrix products, stem_layer(): jnp.einsum('fapbq,pqc->fabc', pixel_tiles, kernel, preferred_element_type...  6.23 us
    convert_element_type x1, local copies, waits for them, and re-layouts, stem_layer(): jax.nn.gelu(response).astype(jnp.bfloat16)  5.16 us
    gather x1, local copies, waits for them, and re-layouts, local(): x = jnp.take(features, sorted_frames, axis=0)  3.31 us
  transfers between devices with their start and end apart: 1, of which 1 were waited for; matrix products, arithmetic and copies ran while one was open for 23% of the time, Pallas kernels for 0%

profile of v14, /device:TPU:1, one launch (start us, length us, event | category | flops | bytes accessed | tf_op | source)
XLA Modules:
  0.0 141.7 jit_solution(9404746298011562873)
XLA Ops:
  7.2 0.0 copy-start
  7.2 0.0 all-gather.3.cloned.1.call-start
  7.2 1.1 reshape.124
  8.3 0.7 reshape_squeeze.10
  9.0 0.8 copy.27
  9.9 0.2 reshape_squeeze.4
  10.1 1.6 %pad_maximum_fusion = bf16[1184,128]{1,0:T(8,128)(2,1)} fusion(bf16[512,128]{1,0:T(8,128)(2,1)} %bitcast.57, bf16[512,128]{1,0:T(8,128)(2,1)S(1)} %reshape.124, bf16[80,128]{1,0:T(8,128)(2,1)S(1)} %get-tuple-element.21, bf16[80,128]{1,0:T(8,128)(2,1)S(1)} %get-tuple-element.22), kind=kLoop, calls=%fused_computation.14 | loop fusion | flops 1212416 | bytes 606208 | tf_op jit(solution)/shard_map/concatenate | solution.py:200
  11.7 0.0 all-gather.3.cloned.1.call-update
  11.7 0.0 copy-start.4
  11.7 13.0 %copy.25 = bf16[1,768,16,384]{1,3,2,0:T(8,128)(2,1)} copy(bf16[1,768,16,384]{3,2,1,0:T(8,128)(2,1)} %param.12) | data formatting | bytes 18874368 | tf_op args[0]
  24.8 0.0 copy-done.4
  24.8 6.2 %convert_reduce_fusion = (f32[768,128]{1,0:T(8,128)S(1)}, bf16[768,24,128]{2,0,1:T(8,128)(2,1)S(1)}) fusion(bf16[768,16,24,16]{0,3,2,1:T(8,128)(2,1)} %bitcast.50, bf16[16,16,128,1]{2,1,3,0:T(8,128)(2,1)S(1)} %bitcast.66), kind=kOutput, calls=%fused_computation.10 | convolution fusion | flops 1233813504 | bytes 14614528 | tf_op jit(solution)/shard_map/fapbq,pqc->fabc/dot_general | solution.py:22
  31.0 0.0 copy-start.1
  31.0 0.0 copy-start.2
  31.0 5.2 %copy.26 = bf16[768,24,128]{2,1,0:T(8,128)(2,1)} copy(bf16[768,24,128]{2,0,1:T(8,128)(2,1)S(1)} %get-tuple-element.20) | data formatting | bytes 9437184 | tf_op jit(solution)/shard_map/convert_element_type | solution.py:25
  36.2 0.0 copy-done.1
  36.2 0.1 convert_reduce_fusion.2
  36.3 0.2 reduce-window.9
  36.5 0.7 multiply_bitcast_fusion
  37.2 0.2 multiply_reduce_fusion
  37.4 0.0 copy-start.3
  37.4 0.0 copy-start.5
  37.4 0.1 reshape.130
  37.5 0.2 convert_reduce_fusion.1
  37.7 0.0 copy-done.2
  37.7 0.8 select_reduce_fusion
  38.5 3.3 %gather_fusion = bf16[192,24,128]{2,1,0:T(8,128)(2,1)S(1)} fusion(bf16[768,24,128]{2,1,0:T(8,128)(2,1)} %copy.26, s32[1024]{0:T(1024)S(1)} %pad_clamp_fusion), kind=kCustom, calls=%fused_computation | custom fusion | bytes 2360064 | tf_op jit(solution)/shard_map/jit(_take)/gather | solution.py:225
  41.8 0.0 copy-done
  41.8 0.6 constant_dynamic-slice_fusion.ro_ref
  42.4 0.6 multiply_bitcast_fusion.1.gend_ref
  43.0 0.5 multiply_subtract_fusion.gstart_ref
  43.5 1.3 broadcast_select_fusion.x_ref
  44.8 9.6 %all-gather.3.cloned.1.call-done = bf16[9472,128]{1,0:T(8,128)(2,1)} async-done(((bf16[1184,128]{1,0:T(8,128)(2,1)}), bf16[9472,128]{1,0:T(8,128)(2,1)}) %all-gather.3.cloned.1.call-update) | async-done | bytes 2424848 | tf_op jit(solution)/shard_map/all_gather | solution.py:200
  54.5 1.0 slice_bitcast_fusion
  55.5 2.8 %fusion.13 = (bf16[8,512,128]{2,1,0:T(8,128)(2,1)}, bf16[8,512,128]{2,1,0:T(8,128)(2,1)S(1)}) fusion(bf16[8,1184,128]{2,1,0:T(8,128)(2,1)} %bitcast.52), kind=kLoop, calls=%fused_computation.47 | loop fusion | bytes 4194304 | tf_op jit(solution)/shard_map/slice | solution.py:203
  58.3 2.1 %reshape.127.tin_ref = bf16[8,384,24]{2,1,0:T(8,128)(2,1)} reshape(bf16[8,9216]{1,0:T(8,128)(2,1)S(1)} %slice.36) | data formatting | bytes 294912 | tf_op jit(solution)/shard_map/reshape | solution.py:204
  60.5 0.7 copy.40
  61.2 1.4 %reshape_reshape.3.cin_ref = bf16[8,128,512]{2,1,0:T(8,128)(2,1)} reshape(bf16[8,512,128]{2,1,0:T(8,128)(2,1)S(1)} %get-tuple-element.16) | data formatting | bytes 2097152 | tf_op jit(solution)/shard_map/reshape;reshape | solution.py:204
  62.7 50.7 %shard_map.139 = f32[32,8,128]{2,1,0:T(8,128)} custom-call(s32[192]{0:T(256)} %get-tuple-element.14.tgt_ref, s32[8]{0:T(128)} %multiply_subtract_fusion.gstart_ref, s32[8]{0:T(128)} %multiply_bitcast_fusion.1.gend_ref, s32[192]{0:T(256)} %get-tuple-element.13.order_ref, bf16[192,24,128]{2,1,0:T(8,128)(2,1)} %broadcast_select_fusion.x_ref, ...), custom_call_target="tpu_custom_call" | custom-call | tf_op jit(solution)/shard_map/pallas_call | solution.py:118
  113.4 1.8 %dynamic_update_slice.3.x_ref = f32[32,8,128]{2,1,0:T(8,128)} dynamic-update-slice(f32[32,8,128]{2,1,0:T(8,128)} %shard_map.139, f32[32,1,24]{2,1,0:T(1,128)S(1)} %bitcast.58, s32[]{:T(128)} %constant.19.clone.1, s32[]{:T(128)} %constant.51.clone.1, s32[]{:T(128)} %constant.19.clone.1) | dynamic-update-slice | bytes 6148 | tf_op jit(solution)/shard_map/dynamic_update_slice | solution.py:241
  115.2 14.9 %shard_map.140 = f32[8,128]{1,0:T(8,128)} custom-call(f32[32,8,128]{2,1,0:T(8,128)} %dynamic_update_slice.3.x_ref), custom_call_target="tpu_custom_call" | custom-call | tf_op jit(solution)/shard_map/pallas_call | solution.py:159
  130.1 0.8 multiply_reduce_fusion.1
  130.9 1.2 slice_bitcast_fusion.2
  132.1 0.8 fusion.10
  132.8 0.6 copy.29
  133.4 0.0 copy-done.5
  133.4 0.9 convolution_bitcast_fusion
  134.3 0.6 copy.30
  (10 shorter events, 0.1 us)
Async XLA Ops:
  7.2 34.7 %copy-start = (bf16[4096,128]{1,0:T(8,128)(2,1)S(1)}, bf16[4096,128]{1,0:T(8,128)(2,1)}, u32[]{:S(2)}) copy-start(bf16[4096,128]{1,0:T(8,128)(2,1)} %param.21) | copy-start | bytes 3145732
  7.2 47.3 %all-gather.3.cloned.1.call-start = ((), (), s32[]{:S(2)}) async-start(), calls=%async_computation | async-start | bytes 2727936 | tf_op jit(solution)/shard_map/all_gather | solution.py:200
  11.7 13.1 %copy-start.4 = (bf16[256,128]{1,0:T(8,128)(2,1)S(1)}, bf16[256,128]{1,0:T(8,128)(2,1)}, u32[]{:S(2)}) copy-start(bf16[256,128]{1,0:T(8,128)(2,1)} %param.13) | copy-start | bytes 196612
  31.0 5.2 %copy-start.1 = (s32[1,192,1]{1,2,0:T(1,128)S(1)}, s32[1,192,1]{1,2,0:T(1,128)}, u32[]{:S(2)}) copy-start(s32[1,192,1]{1,2,0:T(1,128)} %param.16) | copy-start | bytes 2308
  31.0 6.7 %copy-start.2 = (s32[1,192]{1,0:T(1,128)S(1)}, s32[1,192]{1,0:T(1,128)}, u32[]{:S(2)}) copy-start(s32[1,192]{1,0:T(1,128)} %param.15) | copy-start | bytes 2308
  37.4 94.7 %copy-start.3 = (f32[128]{0:T(128)S(1)}, f32[128]{0:T(128)}, u32[]{:S(2)}) copy-start(f32[128]{0:T(128)} %param.22) | copy-start | bytes 1540
  37.4 96.0 %copy-start.5 = (f32[128,8]{0,1:T(8,128)S(1)}, f32[128,8]{0,1:T(8,128)}, u32[]{:S(2)}) copy-start(f32[128,8]{0,1:T(8,128)} %param.23) | copy-start | bytes 12292
Sparse Core Ops, SparseCore 0:
  11.8 42.5 all-gather.2

commit v15 on v13

--- a/solution.py
+++ b/solution.py
@@ -8,7 +8,7 @@
 from jax.sharding import PartitionSpec as P
 
 PATCH = 16
-BLOCK_HITS = 64
+BLOCK_HITS = 24
 
 
 def rms_norm(values):

time: 144 us -> 143 us (level)
  no operation moved by 1% of the time
where the time goes in v15:
time: 143 us; the launch traced here: 142 us
  Pallas kernels  65.7 us (46%)
  local copies, waits for them, and re-layouts  40.4 us (28%)
  between operations  14.2 us (10%)
  matrix products  8.67 us (6%)
  other arithmetic  7.64 us (5%)
  waiting for transfers between devices  5.55 us (4%)
    pallas_call x1, Pallas kernels, encode_rows(): pl.pallas_call(encoder_kernel, grid_spec=grid_spec, out_shape=jax.ShapeDt...  50.6 us
    unnamed x21, local copies, waits for them, and re-layouts  17.5 us
    pallas_call x1, Pallas kernels, exchange_sum(): pl.pallas_call(functools.partial(exchange_kernel, n), out_shape=jax.Shape...  15.1 us
    dot_general x1, matrix products, stem_layer(): jnp.einsum('fapbq,pqc->fabc', pixel_tiles, kernel, preferred_element_type...  7.81 us
    convert_element_type x1, local copies, waits for them, and re-layouts, stem_layer(): jax.nn.gelu(response).astype(jnp.bfloat16)  7.55 us
    all_gather x1, waiting for transfers between devices, local(): gathered = lax.all_gather(jnp.concatenate(blocks, axis=0), 'stream')  5.53 us
    gather x1, local copies, waits for them, and re-layouts, local(): x = jnp.take(features, sorted_frames, axis=0)  3.31 us
  transfers between devices with their start and end apart: 1, of which 1 were waited for; matrix products, arithmetic and copies ran while one was open for 26% of the time, Pallas kernels for 0%

profile of v15, /device:TPU:1, one launch (start us, length us, event | category | flops | bytes accessed | tf_op | source)
XLA Modules:
  0.0 142.3 jit_solution(2594213120063831471)
XLA Ops:
  7.2 0.0 copy-start
  7.2 0.0 all-gather.3.cloned.1.call-start
  7.2 1.1 reshape.150
  8.3 0.7 reshape_squeeze.10
  9.0 0.8 copy.26
  9.9 0.2 reshape_squeeze.4
  10.1 1.7 %pad_maximum_fusion = bf16[1184,128]{1,0:T(8,128)(2,1)} fusion(bf16[512,128]{1,0:T(8,128)(2,1)} %bitcast.65, bf16[512,128]{1,0:T(8,128)(2,1)S(1)} %reshape.150, bf16[80,128]{1,0:T(8,128)(2,1)S(1)} %get-tuple-element.20, bf16[80,128]{1,0:T(8,128)(2,1)S(1)} %get-tuple-element.21), kind=kLoop, calls=%fused_computation.15 | loop fusion | flops 1212416 | bytes 606208 | tf_op jit(solution)/shard_map/concatenate | solution.py:191
  11.7 0.0 all-gather.3.cloned.1.call-update
  11.8 0.0 copy-start.4
  11.8 13.0 %copy.24 = bf16[1,768,16,384]{1,3,2,0:T(8,128)(2,1)} copy(bf16[1,768,16,384]{3,2,1,0:T(8,128)(2,1)} %param.12) | data formatting | bytes 18874368 | tf_op args[0]
  24.8 0.7 multiply_bitcast_fusion
  25.5 0.0 copy-done.4
  25.5 7.8 %convert_reduce_fusion = (f32[768,128]{1,0:T(8,128)S(1)}, bf16[768,24,128]{2,0,1:T(8,128)(2,1)}) fusion(bf16[768,16,24,16]{0,3,2,1:T(8,128)(2,1)} %bitcast.57, bf16[16,16,128,1]{2,1,3,0:T(8,128)(2,1)S(1)} %bitcast.76), kind=kOutput, calls=%fused_computation.11 | convolution fusion | flops 1233813504 | bytes 14614528 | tf_op jit(solution)/shard_map/fapbq,pqc->fabc/dot_general | solution.py:22
  33.3 0.2 multiply_reduce_fusion
  33.5 0.1 reshape.156
  33.6 0.0 copy-done.1
  33.6 0.1 convert_reduce_fusion.2
  33.7 0.2 reduce-window.9
  33.9 7.6 %copy.25 = bf16[768,24,128]{2,1,0:T(8,128)(2,1)} copy(bf16[768,24,128]{2,0,1:T(8,128)(2,1)} %get-tuple-element.19) | data formatting | bytes 9437184 | tf_op jit(solution)/shard_map/convert_element_type | solution.py:25
  41.4 0.2 convert_reduce_fusion.1
  41.6 0.1 reduce_sum.70
  41.8 0.7 select_reduce_fusion
  42.5 3.3 %gather_fusion = bf16[192,24,128]{2,1,0:T(8,128)(2,1)S(1)} fusion(bf16[768,24,128]{2,1,0:T(8,128)(2,1)} %copy.25, s32[1024]{0:T(1024)S(1)} %pad_clamp_fusion.1), kind=kCustom, calls=%fused_computation | custom fusion | bytes 2360064 | tf_op jit(solution)/shard_map/jit(_take)/gather | solution.py:216
  45.8 0.0 copy-start.3
  45.8 0.0 copy-start.5
  45.9 0.6 constant_dynamic-slice_fusion.ro_ref
  46.5 0.5 multiply_bitcast_fusion.1.gend_ref
  47.0 0.5 multiply_subtract_fusion.gstart_ref
  47.5 1.3 broadcast_select_fusion.x_ref
  48.8 5.5 %all-gather.3.cloned.1.call-done = bf16[9472,128]{1,0:T(8,128)(2,1)} async-done(((bf16[1184,128]{1,0:T(8,128)(2,1)}), bf16[9472,128]{1,0:T(8,128)(2,1)}) %all-gather.3.cloned.1.call-update) | async-done | bytes 2424848 | tf_op jit(solution)/shard_map/all_gather | solution.py:191
  54.4 1.0 slice_bitcast_fusion
  55.4 2.8 %fusion.14 = (bf16[8,512,128]{2,1,0:T(8,128)(2,1)}, bf16[8,512,128]{2,1,0:T(8,128)(2,1)S(1)}) fusion(bf16[8,1184,128]{2,1,0:T(8,128)(2,1)} %bitcast.59), kind=kLoop, calls=%fused_computation.55 | loop fusion | bytes 4194304 | tf_op jit(solution)/shard_map/slice | solution.py:194
  58.2 2.1 %reshape.153.tin_ref = bf16[8,384,24]{2,1,0:T(8,128)(2,1)} reshape(bf16[8,9216]{1,0:T(8,128)(2,1)S(1)} %slice.38) | data formatting | bytes 294912 | tf_op jit(solution)/shard_map/reshape | solution.py:195
  60.4 0.7 copy.41
  61.1 1.4 %reshape_reshape.3.cin_ref = bf16[8,128,512]{2,1,0:T(8,128)(2,1)} reshape(bf16[8,512,128]{2,1,0:T(8,128)(2,1)S(1)} %get-tuple-element.15) | data formatting | bytes 2097152 | tf_op jit(solution)/shard_map/reshape;reshape | solution.py:195
  62.5 50.6 %shard_map.139 = f32[192,128]{1,0:T(8,128)} custom-call(s32[192]{0:T(256)} %get-tuple-element.13.tgt_ref, s32[8]{0:T(128)} %multiply_subtract_fusion.gstart_ref, s32[8]{0:T(128)} %multiply_bitcast_fusion.1.gend_ref, bf16[192,24,128]{2,1,0:T(8,128)(2,1)} %broadcast_select_fusion.x_ref, bf16[8,384,24]{2,1,0:T(8,128)(2,1)} %reshape.153.tin_ref, ...), custom_call_target="tpu_custom_call" | custom-call | tf_op jit(solution)/shard_map/pallas_call | solution.py:109
  113.1 1.6 %gather_fusion.1 = f32[192,128]{1,0:T(8,128)S(1)} fusion(f32[192,128]{1,0:T(8,128)} %shard_map.139, s32[1024]{0:T(1024)S(1)} %pad_clamp_fusion), kind=kCustom, calls=%fused_computation.1 | custom fusion | bytes 197376 | tf_op jit(solution)/shard_map/jit(_take)/gather | solution.py:228
  114.7 0.1 broadcast_in_dim.56
  114.9 0.7 copy.34
  115.6 15.1 %shard_map.140 = f32[8,128]{1,0:T(8,128)} custom-call(f32[32,8,128]{2,1,0:T(8,128)} %bitcast.64), custom_call_target="tpu_custom_call" | custom-call | tf_op jit(solution)/shard_map/pallas_call | solution.py:150
  130.7 0.8 multiply_reduce_fusion.1
  131.4 1.2 slice_bitcast_fusion.2
  132.6 0.0 copy-done.3
  132.6 0.7 fusion.11
  133.4 0.6 copy.27
  134.0 0.0 copy-done.5
  134.0 0.9 convolution_bitcast_fusion
  134.8 0.6 copy.28
  (19 shorter events, 0.2 us)
Async XLA Ops:
  7.2 38.7 %copy-start = (bf16[4096,128]{1,0:T(8,128)(2,1)S(1)}, bf16[4096,128]{1,0:T(8,128)(2,1)}, u32[]{:S(2)}) copy-start(bf16[4096,128]{1,0:T(8,128)(2,1)} %param.21) | copy-start | bytes 3145732
  7.2 47.2 %all-gather.3.cloned.1.call-start = ((), (), s32[]{:S(2)}) async-start(), calls=%async_computation | async-start | bytes 2727936 | tf_op jit(solution)/shard_map/all_gather | solution.py:191
  11.8 13.7 %copy-start.4 = (bf16[256,128]{1,0:T(8,128)(2,1)S(1)}, bf16[256,128]{1,0:T(8,128)(2,1)}, u32[]{:S(2)}) copy-start(bf16[256,128]{1,0:T(8,128)(2,1)} %param.13) | copy-start | bytes 196612
  25.5 8.1 %copy-start.1 = (s32[1,192,1]{1,2,0:T(1,128)S(1)}, s32[1,192,1]{1,2,0:T(1,128)}, u32[]{:S(2)}) copy-start(s32[1,192,1]{1,2,0:T(1,128)} %param.16) | copy-start | bytes 2308
  33.3 8.4 %copy-start.2 = (s32[1,192]{1,0:T(1,128)S(1)}, s32[1,192]{1,0:T(1,128)}, u32[]{:S(2)}) copy-start(s32[1,192]{1,0:T(1,128)} %param.15) | copy-start | bytes 2308
  45.8 86.8 %copy-start.3 = (f32[128]{0:T(128)S(1)}, f32[128]{0:T(128)}, u32[]{:S(2)}) copy-start(f32[128]{0:T(128)} %param.22) | copy-start | bytes 1540
  45.8 88.1 %copy-start.5 = (f32[128,8]{0,1:T(8,128)S(1)}, f32[128,8]{0,1:T(8,128)}, u32[]{:S(2)}) copy-start(f32[128,8]{0,1:T(8,128)} %param.23) | copy-start | bytes 12292
Sparse Core Ops, SparseCore 0:
  11.9 42.4 all-gather.2
